TPU v7x, 32 devices: a whole 2x2x4 slice. The times are simulated.
32 devices in a mesh: groups: 2 (over x), ctx: 16 (over z, y, core).
Axes of the slice: x: 2, y: 2, z: 4, core: 2. Of those that a mesh axis runs over, the one named last changes fastest.
Arguments:
- query: bfloat16 [8192, 16, 128], P(('groups', 'ctx')), parts along dimension 0, may hold values from -48 to 48
- query_tangent: bfloat16 [8192, 16, 128], P(('groups', 'ctx')), parts along dimension 0, may hold values from -6 to 6
- keys: bfloat16 [8192, 8, 128], P(('groups', 'ctx')), parts along dimension 0, may hold values from -6 to 6
- values: bfloat16 [8192, 8, 128], P(('groups', 'ctx')), parts along dimension 0, may hold values from -6 to 6
- key_direction: bfloat16 [8192, 8, 128], P(('groups', 'ctx')), parts along dimension 0, may hold values from -6 to 6
- value_direction: bfloat16 [8192, 8, 128], P(('groups', 'ctx')), parts along dimension 0, may hold values from -6 to 6
- out_cotangent: bfloat16 [8192, 16, 128], P(('groups', 'ctx')), parts along dimension 0, may hold values from -6 to 6
- segment_ids: int32 [8192], P(('groups', 'ctx')), parts along dimension 0, may hold values from 0 to 15, never falling along the last dimension, each value on 1 to 1024 neighbouring positions
Outputs:
- key_adjoint: float32 [8192, 8, 128], P(('groups', 'ctx')), parts along dimension 0
- value_adjoint: float32 [8192, 8, 128], P(('groups', 'ctx')), parts along dimension 0
- key_hvp: float32 [8192, 8, 128], P(('groups', 'ctx')), parts along dimension 0
- value_hvp: float32 [8192, 8, 128], P(('groups', 'ctx')), parts along dimension 0
There are 2 independent parts, one for each index of `groups`. A program takes and returns all parts, laid end to end along the dimension named above; each array names one. Nothing has to cross between parts.
Inputs may be any that keep to these rules, and one draw needn't show every extreme that they name: `segment_ids`: segment numbers never fall along the sequence.
All inputs are finite; a program needn't handle non-finite values.
Results may differ from a plain program's by a relative error of at most 0.006.
Values may be sent and summed in bfloat16 or wider, within the bound.
No kernel may reach another device: no remote copies, remote signals or barrier semaphores. Data moves between devices by JAX's collectives and lax.ppermute only.
A program may use at most 128 MiB of HBM per device.

v0:
```python
import jax
import jax.numpy as jnp
from jax import lax
from jax.sharding import PartitionSpec as P

WINDOW_LENGTH = 1024


def shifted_2(block, axis, distance):
    devices = range(lax.axis_size(axis))
    route = [(i - distance, i) for i in devices if i - distance in devices]
    return lax.ppermute(block, axis, route)


def contract(matrix, operand):
    return jnp.dot(matrix, operand.T, preferred_element_type=jnp.float32)


def transposed(matrix, operand):
    return jnp.dot(matrix.T, operand, preferred_element_type=jnp.float32)


def by_head(array, kv_heads):
    row_count, head_count, head_size = array.shape
    query_group = head_count // kv_heads
    return (
        array.reshape(row_count, kv_heads, query_group, head_size)
        .transpose(1, 0, 2, 3)
        .reshape(kv_heads, row_count * query_group, head_size)
    )


def by_kv(array):
    return array.transpose(1, 0, 2)


def row_partials(
    query_rows, query_dots, cotangent, key_rows, value_rows, key_dots, value_dots, visible
):
    factor = query_rows.shape[-1] ** (-0.5)
    scores = factor * contract(query_rows, key_rows)
    scores_dot = factor * (contract(query_dots, key_rows) + contract(query_rows, key_dots))
    scores = jnp.where(visible, scores, -1e30)
    highest = jnp.max(scores, axis=1)
    weights = jnp.where(visible, jnp.exp(scores - highest[:, None]), 0.0)
    upstream = contract(cotangent, value_rows)
    upstream_dot = contract(cotangent, value_dots)
    weighted_dot = weights * scores_dot
    return (
        highest,
        jnp.sum(weights, axis=1),
        jnp.sum(weighted_dot, axis=1),
        jnp.sum(weights * upstream, axis=1),
        jnp.sum(weighted_dot * upstream, axis=1),
        jnp.sum(weights * upstream_dot, axis=1),
    )


def merge_rows(first, second):
    highest = jnp.maximum(first[0], second[0])
    scale_first = jnp.exp(first[0] - highest)
    scale_second = jnp.exp(second[0] - highest)
    return (highest,) + tuple(
        (left * scale_first + right * scale_second for left, right in zip(first[1:], second[1:]))
    )


def key_side_terms(
    query_rows,
    query_dots,
    cotangent,
    key_rows,
    value_rows,
    key_dots,
    value_dots,
    highest,
    total,
    summed_dot,
    summed_up,
    summed_both,
    summed_updot,
    visible,
):
    factor = query_rows.shape[-1] ** (-0.5)
    safe_total = jnp.where(total > 0.0, total, 1.0)
    mean_dot = summed_dot / safe_total
    center = summed_up / safe_total
    center_dot = summed_both / safe_total - mean_dot * center + summed_updot / safe_total
    scores = factor * contract(query_rows, key_rows)
    scores_dot = factor * (contract(query_dots, key_rows) + contract(query_rows, key_dots))
    shifted = jnp.where(visible, scores - highest[:, None], 0.0)
    mixing = jnp.where(visible, jnp.exp(shifted), 0.0) / safe_total[:, None]
    mixing_dot = mixing * (scores_dot - mean_dot[:, None])
    upstream = contract(cotangent, value_rows)
    upstream_dot = contract(cotangent, value_dots)
    grad_scores = mixing * (upstream - center[:, None])
    grad_scores_dot = mixing_dot * (upstream - center[:, None]) + mixing * (
        upstream_dot - center_dot[:, None]
    )
    mixing_b = mixing.astype(jnp.bfloat16)
    mixing_dot_b = mixing_dot.astype(jnp.bfloat16)
    grad_b = grad_scores.astype(jnp.bfloat16)
    grad_dot_b = grad_scores_dot.astype(jnp.bfloat16)
    value_adj = transposed(mixing_b, cotangent)
    value_tan = transposed(mixing_dot_b, cotangent)
    key_adj = factor * transposed(grad_b, query_rows)
    key_tan = factor * (transposed(grad_dot_b, query_rows) + transposed(grad_b, query_dots))
    return (key_adj, value_adj, key_tan, value_tan)


def fetch_queries(own_queries, offset):
    return shifted_2(
        (own_queries[0], own_queries[1], own_queries[2], own_queries[3]), "ctx", -offset
    )


def send_partials(partials, offset):
    return shifted_2(partials, "ctx", offset)


def send_merged(merged, offset):
    return shifted_2(merged, "ctx", -offset)


def queries_moved(
    query, query_tangent, keys, values, key_direction, value_direction, out_cotangent, segment_ids
):
    local_rows = query.shape[0]
    kv_heads = keys.shape[1]
    query_group = query.shape[1] // kv_heads
    blocks_back = WINDOW_LENGTH // local_rows
    device = lax.axis_index("ctx")
    count = lax.axis_size("ctx")
    start = device * local_rows
    own_queries = (query, query_tangent, out_cotangent, segment_ids.astype(jnp.bfloat16))
    pieces = [own_queries] + [
        fetch_queries(own_queries, offset) for offset in range(1, blocks_back + 1)
    ]
    band = tuple((jnp.concatenate([piece[member] for piece in pieces], 0) for member in range(4)))
    band_count = band[0].shape[0]
    query_pos = start + jnp.arange(band_count * query_group, dtype=jnp.int32) // query_group
    key_pos = start + jnp.arange(local_rows, dtype=jnp.int32)
    distance = query_pos[:, None] - key_pos[None, :]
    query_docs = jnp.repeat(band[3].astype(jnp.int32), query_group)
    visible = (
        (query_pos[:, None] < count * local_rows)
        & (distance >= 0)
        & (distance < WINDOW_LENGTH)
        & (query_docs[:, None] == segment_ids[None, :])
    )
    stacked = (
        by_head(band[0], kv_heads),
        by_head(band[1], kv_heads),
        by_head(band[2], kv_heads),
        by_kv(keys),
        by_kv(values),
        by_kv(key_direction),
        by_kv(value_direction),
    )
    partials = lax.map(lambda items: row_partials(*items, visible), stacked)
    span = local_rows * query_group

    def stats_block(offset):
        return tuple((member[:, offset * span : (offset + 1) * span] for member in partials))

    merged = stats_block(0)
    for offset in range(1, blocks_back + 1):
        arrived = send_partials(stats_block(offset), offset)
        valid = device - offset >= 0
        arrived = (jnp.where(valid, arrived[0], -1e30),) + tuple(arrived[1:])
        merged = merge_rows(merged, arrived)
    returned = [merged] + [send_merged(merged, offset) for offset in range(1, blocks_back + 1)]
    stats = tuple(
        (jnp.concatenate([piece[member] for piece in returned], 1) for member in range(6))
    )
    results = lax.map(lambda items: key_side_terms(*items, visible), stacked + stats)
    return tuple((result.transpose(1, 0, 2) for result in results))


def local(
    query, query_tangent, keys, values, key_direction, value_direction, out_cotangent, segment_ids
):
    return queries_moved(
        query,
        query_tangent,
        keys,
        values,
        key_direction,
        value_direction,
        out_cotangent,
        segment_ids,
    )


def solution(mesh):
    placed = (
        P(("groups", "ctx"), None, None),
        P(("groups", "ctx"), None, None),
        P(("groups", "ctx"), None, None),
        P(("groups", "ctx"), None, None),
        P(("groups", "ctx"), None, None),
        P(("groups", "ctx"), None, None),
        P(("groups", "ctx"), None, None),
        P(("groups", "ctx")),
    )
    return jax.shard_map(
        local,
        mesh=mesh,
        in_specs=placed,
        out_specs=(
            P(("groups", "ctx"), None, None),
            P(("groups", "ctx"), None, None),
            P(("groups", "ctx"), None, None),
            P(("groups", "ctx"), None, None),
        ),
        check_vma=False,
    )
```

profile of v0, /device:TPU:21, one launch (start us, length us, event | category | flops | bytes accessed | tf_op | source)
XLA Modules:
  0.0 881.3 jit_solution(11833786622701505699)
XLA Ops:
  18.3 67.1 %collective-permute-done.4 = bf16[256]{0:T(256)(128)(2,1)S(1)} collective-permute-done((bf16[256]{0:T(256)(128)(2,1)S(1)}, bf16[256]{0:T(256)(128)(2,1)S(1)}, u32[]{:S(2)}, u32[]{:S(2)}) %collective-permute-start.4) | collective-permute-done | bytes 544 | tf_op jit(solution)/shard_map/ppermute | solution.py:12
  119.4 5.8 collective-permute-done.8
  131.8 17.3 %collective-permute-start.14 = (bf16[256,16,128]{2,1,0:T(8,128)(2,1)S(1)}, bf16[256,16,128]{2,1,0:T(8,128)(2,1)S(1)}, u32[]{:S(2)}, u32[]{:S(2)}) collective-permute-start(bf16[256,16,128]{2,1,0:T(8,128)(2,1)S(1)} %copy-done.9), channel_id=1, source_target_pairs={{3,0},{4,1},{5,2},{6,3},{7,4},{8,5},{9,6},{10,7},{11,8},{12,9},{13... | collective-permute-start | bytes 3145736 | tf_op jit(solution)/shard_map/ppermute | solution.py:12
  156.6 6.0 copy.23
  168.7 4.6 copy.25
  173.4 41.9 %collective-permute-done.12 = bf16[256,16,128]{2,1,0:T(8,128)(2,1)S(1)} collective-permute-done((bf16[256,16,128]{2,1,0:T(8,128)(2,1)}, bf16[256,16,128]{2,1,0:T(8,128)(2,1)S(1)}, u32[]{:S(2)}, u32[]{:S(2)}) %collective-permute-start.12) | collective-permute-done | bytes 1048608 | tf_op jit(solution)/shard_map/ppermute | solution.py:12
  216.4 4.7 copy.27
  221.1 139.0 %while.38 = (s32[]{:T(128)}, f32[8,2560]{1,0:T(8,128)S(1)}, f32[8,2560]{1,0:T(8,128)S(1)}, f32[8,2560]{1,0:T(8,128)S(1)}, f32[8,2560]{1,0:T(8,128)S(1)}, /*index...) while((s32[]{:T(128)}, f32[8,2560]{1,0:T(8,128)S(1)}, ...), condition=%wide.region_7.8_spmd.clone, body=%wide.region_0.7_spmd.clone.sunk | while | flops 870302720 | bytes 35529976 | solution.py:160
  364.1 27.9 %collective-permute-start.57 = (f32[8,512]{1,0:T(8,128)S(1)}, f32[8,512]{1,0:T(8,128)S(1)}, u32[]{:S(2)}, u32[]{:S(2)}) collective-permute-start(f32[8,512]{1,0:T(8,128)S(1)} %get-tuple-element.443), channel_id=1, source_target_pairs={{0,2},{1,3},{2,4},{3,5},{4,6},{5,7},{6,8},{7,9},{8,10},{9,11},{10,... | collective-permute-start | bytes 49160 | tf_op jit(solution)/shard_map/ppermute | solution.py:12
  391.9 22.2 %collective-permute-start.56 = (f32[8,512]{1,0:T(8,128)S(1)}, f32[8,512]{1,0:T(8,128)S(1)}, u32[]{:S(2)}, u32[]{:S(2)}) collective-permute-start(f32[8,512]{1,0:T(8,128)S(1)} %get-tuple-element.441), channel_id=1, source_target_pairs={{0,1},{1,2},{2,3},{3,4},{4,5},{5,6},{6,7},{7,8},{8,9},{9,10},{10,1... | collective-permute-start | bytes 49160 | tf_op jit(solution)/shard_map/ppermute | solution.py:12
  460.6 5.2 collective-permute-start.23
  465.8 5.0 collective-permute-start.28
  520.0 361.1 %while.39 = (s32[]{:T(128)}, f32[8,256,128]{2,0,1:T(8,128)}, f32[8,256,128]{2,0,1:T(8,128)}, f32[8,256,128]{2,0,1:T(8,128)}, f32[8,256,128]{2,0,1:T(8,128)}, /*i...) while((s32[]{:T(128)}, f32[8,256,128]{2,0,1:T(8,128)}, ...), condition=%wide.region_9.10_spmd.clone, body=%wide.region_8.9_spmd.clone.sunk | while | flops 1694882304 | bytes 74691752 | solution.py:176
  523.9 4.6 multiply_convert_fusion.2
  531.2 4.7 dynamic_update_slice.58
  537.4 4.7 dynamic_update_slice.59
  553.2 4.8 dynamic_update_slice.60
  560.5 4.7 dynamic_update_slice.61
  569.0 4.6 multiply_convert_fusion.2
  576.3 4.7 dynamic_update_slice.58
  582.6 4.7 dynamic_update_slice.59
  598.4 4.8 dynamic_update_slice.60
  605.6 4.7 dynamic_update_slice.61
  614.2 4.6 multiply_convert_fusion.2
  621.5 4.7 dynamic_update_slice.58
  627.7 4.7 dynamic_update_slice.59
  643.5 4.8 dynamic_update_slice.60
  650.7 4.7 dynamic_update_slice.61
  666.6 4.7 dynamic_update_slice.58
  672.9 4.7 dynamic_update_slice.59
  688.7 4.8 dynamic_update_slice.60
  695.9 4.7 dynamic_update_slice.61
  711.8 4.7 dynamic_update_slice.58
  718.0 4.7 dynamic_update_slice.59
  733.8 4.8 dynamic_update_slice.60
  741.0 4.7 dynamic_update_slice.61
  756.9 4.7 dynamic_update_slice.58
  763.2 4.7 dynamic_update_slice.59
  779.0 4.8 dynamic_update_slice.60
  786.2 4.7 dynamic_update_slice.61
  802.0 4.7 dynamic_update_slice.58
  808.3 4.7 dynamic_update_slice.59
  824.1 4.8 dynamic_update_slice.60
  831.3 4.7 dynamic_update_slice.61
  847.2 4.7 dynamic_update_slice.58
  853.5 4.7 dynamic_update_slice.59
  869.2 4.8 dynamic_update_slice.60
  876.5 4.7 dynamic_update_slice.61
  (708 shorter events, 504.7 us)
Async XLA Ops:
  0.6 102.9 %collective-permute-start = (bf16[256,16,128]{2,1,0:T(8,128)(2,1)}, bf16[256,16,128]{2,1,0:T(8,128)(2,1)S(1)}, u32[]{:S(2)}, u32[]{:S(2)}) collective-permute-start(bf16[256,16,128]{2,1,0:T(8,128)(2,1)} %param.12), channel_id=1, source_target_pairs={{1,0},{2,1},{3,2},{4,3},{5,4},{6,5},{7,6},{8,7},{9,8},{10,9},{11,1... | collective-permute-start | bytes 3145736 | tf_op jit(solution)/shard_map/ppermute | solution.py:12
  3.4 102.7 %collective-permute-start.1 = (bf16[256,16,128]{2,1,0:T(8,128)(2,1)}, bf16[256,16,128]{2,1,0:T(8,128)(2,1)S(1)}, u32[]{:S(2)}, u32[]{:S(2)}) collective-permute-start(bf16[256,16,128]{2,1,0:T(8,128)(2,1)} %param.12), channel_id=1, source_target_pairs={{2,0},{3,1},{4,2},{5,3},{6,4},{7,5},{8,6},{9,7},{10,8},{11,9},{12,... | collective-permute-start | bytes 3145736 | tf_op jit(solution)/shard_map/ppermute | solution.py:12
  5.5 106.6 %collective-permute-start.2 = (bf16[256,16,128]{2,1,0:T(8,128)(2,1)}, bf16[256,16,128]{2,1,0:T(8,128)(2,1)}, u32[]{:S(2)}, u32[]{:S(2)}) collective-permute-start(bf16[256,16,128]{2,1,0:T(8,128)(2,1)} %param.12), channel_id=1, source_target_pairs={{3,0},{4,1},{5,2},{6,3},{7,4},{8,5},{9,6},{10,7},{11,8},{12,9},{13... | collective-permute-start | bytes 3145736 | tf_op jit(solution)/shard_map/ppermute | solution.py:12
  8.7 106.1 %collective-permute-start.3 = (bf16[256,16,128]{2,1,0:T(8,128)(2,1)}, bf16[256,16,128]{2,1,0:T(8,128)(2,1)}, u32[]{:S(2)}, u32[]{:S(2)}) collective-permute-start(bf16[256,16,128]{2,1,0:T(8,128)(2,1)} %param.12), channel_id=1, source_target_pairs={{4,0},{5,1},{6,2},{7,3},{8,4},{9,5},{10,6},{11,7},{12,8},{13,9},{1... | collective-permute-start | bytes 3145736 | tf_op jit(solution)/shard_map/ppermute | solution.py:12
  11.5 73.9 %collective-permute-start.4 = (bf16[256]{0:T(256)(128)(2,1)S(1)}, bf16[256]{0:T(256)(128)(2,1)S(1)}, u32[]{:S(2)}, u32[]{:S(2)}) collective-permute-start(bf16[256]{0:T(256)(128)(2,1)S(1)} %convert_element_type.18), channel_id=1, source_target_pairs={{1,0},{2,1},{3,2},{4,3},{5,4},{6,5},{7,6},{8,7},{9,8},{10,9},{11,1... | collective-permute-start | bytes 1544 | tf_op jit(solution)/shard_map/ppermute | solution.py:12
  99.8 25.4 %collective-permute-start.8 = (bf16[256,16,128]{2,1,0:T(8,128)(2,1)}, bf16[256,16,128]{2,1,0:T(8,128)(2,1)}, u32[]{:S(2)}, u32[]{:S(2)}) collective-permute-start(bf16[256,16,128]{2,1,0:T(8,128)(2,1)} %param.13), channel_id=1, source_target_pairs={{1,0},{2,1},{3,2},{4,3},{5,4},{6,5},{7,6},{8,7},{9,8},{10,9},{11,1... | collective-permute-start | bytes 3145736 | tf_op jit(solution)/shard_map/ppermute | solution.py:12
  103.5 28.3 %collective-permute-start.9 = (bf16[256,16,128]{2,1,0:T(8,128)(2,1)}, bf16[256,16,128]{2,1,0:T(8,128)(2,1)}, u32[]{:S(2)}, u32[]{:S(2)}) collective-permute-start(bf16[256,16,128]{2,1,0:T(8,128)(2,1)} %param.13), channel_id=1, source_target_pairs={{2,0},{3,1},{4,2},{5,3},{6,4},{7,5},{8,6},{9,7},{10,8},{11,9},{12,... | collective-permute-start | bytes 3145736 | tf_op jit(solution)/shard_map/ppermute | solution.py:12
  107.1 44.7 %collective-permute-start.10 = (bf16[256,16,128]{2,1,0:T(8,128)(2,1)}, bf16[256,16,128]{2,1,0:T(8,128)(2,1)}, u32[]{:S(2)}, u32[]{:S(2)}) collective-permute-start(bf16[256,16,128]{2,1,0:T(8,128)(2,1)} %param.13), channel_id=1, source_target_pairs={{3,0},{4,1},{5,2},{6,3},{7,4},{8,5},{9,6},{10,7},{11,8},{12,9},{13... | collective-permute-start | bytes 3145736 | tf_op jit(solution)/shard_map/ppermute | solution.py:12
  112.2 54.9 %collective-permute-start.11 = (bf16[256,16,128]{2,1,0:T(8,128)(2,1)}, bf16[256,16,128]{2,1,0:T(8,128)(2,1)}, u32[]{:S(2)}, u32[]{:S(2)}) collective-permute-start(bf16[256,16,128]{2,1,0:T(8,128)(2,1)} %param.13), channel_id=1, source_target_pairs={{4,0},{5,1},{6,2},{7,3},{8,4},{9,5},{10,6},{11,7},{12,8},{13,9},{1... | collective-permute-start | bytes 3145736 | tf_op jit(solution)/shard_map/ppermute | solution.py:12
  114.8 100.4 %collective-permute-start.12 = (bf16[256,16,128]{2,1,0:T(8,128)(2,1)}, bf16[256,16,128]{2,1,0:T(8,128)(2,1)S(1)}, u32[]{:S(2)}, u32[]{:S(2)}) collective-permute-start(bf16[256,16,128]{2,1,0:T(8,128)(2,1)} %param.18), channel_id=1, source_target_pairs={{1,0},{2,1},{3,2},{4,3},{5,4},{6,5},{7,6},{8,7},{9,8},{10,9},{11,1... | collective-permute-start | bytes 3145736 | tf_op jit(solution)/shard_map/ppermute | solution.py:12
  125.2 90.3 %collective-permute-start.13 = (bf16[256,16,128]{2,1,0:T(8,128)(2,1)}, bf16[256,16,128]{2,1,0:T(8,128)(2,1)S(1)}, u32[]{:S(2)}, u32[]{:S(2)}) collective-permute-start(bf16[256,16,128]{2,1,0:T(8,128)(2,1)} %param.18), channel_id=1, source_target_pairs={{2,0},{3,1},{4,2},{5,3},{6,4},{7,5},{8,6},{9,7},{10,8},{11,9},{12,... | collective-permute-start | bytes 3145736 | tf_op jit(solution)/shard_map/ppermute | solution.py:12
  131.8 84.0 %collective-permute-start.14 = (bf16[256,16,128]{2,1,0:T(8,128)(2,1)S(1)}, bf16[256,16,128]{2,1,0:T(8,128)(2,1)S(1)}, u32[]{:S(2)}, u32[]{:S(2)}) collective-permute-start(bf16[256,16,128]{2,1,0:T(8,128)(2,1)S(1)} %copy-done.9), channel_id=1, source_target_pairs={{3,0},{4,1},{5,2},{6,3},{7,4},{8,5},{9,6},{10,7},{11,8},{12,9},{13... | collective-permute-start | bytes 3145736 | tf_op jit(solution)/shard_map/ppermute | solution.py:12
  151.8 64.3 %collective-permute-start.15 = (bf16[256,16,128]{2,1,0:T(8,128)(2,1)S(1)}, bf16[256,16,128]{2,1,0:T(8,128)(2,1)S(1)}, u32[]{:S(2)}, u32[]{:S(2)}) collective-permute-start(bf16[256,16,128]{2,1,0:T(8,128)(2,1)S(1)} %copy-done.9), channel_id=1, source_target_pairs={{4,0},{5,1},{6,2},{7,3},{8,4},{9,5},{10,6},{11,7},{12,8},{13,9},{1... | collective-permute-start | bytes 3145736 | tf_op jit(solution)/shard_map/ppermute | solution.py:12
  360.2 55.9 %collective-permute-start.59 = (f32[8,512]{1,0:T(8,128)S(1)}, f32[8,512]{1,0:T(8,128)S(1)}, u32[]{:S(2)}, u32[]{:S(2)}) collective-permute-start(f32[8,512]{1,0:T(8,128)S(1)} %get-tuple-element.444), channel_id=1, source_target_pairs={{0,4},{1,5},{2,6},{3,7},{4,8},{5,9},{6,10},{7,11},{8,12},{9,13},{1... | collective-permute-start | bytes 49160 | tf_op jit(solution)/shard_map/ppermute | solution.py:12
  362.1 55.9 %collective-permute-start.58 = (f32[8,512]{1,0:T(8,128)S(1)}, f32[8,512]{1,0:T(8,128)S(1)}, u32[]{:S(2)}, u32[]{:S(2)}) collective-permute-start(f32[8,512]{1,0:T(8,128)S(1)} %get-tuple-element.442), channel_id=1, source_target_pairs={{0,3},{1,4},{2,5},{3,6},{4,7},{5,8},{6,9},{7,10},{8,11},{9,12},{10... | collective-permute-start | bytes 49160 | tf_op jit(solution)/shard_map/ppermute | solution.py:12
  364.1 55.9 %collective-permute-start.57 = (f32[8,512]{1,0:T(8,128)S(1)}, f32[8,512]{1,0:T(8,128)S(1)}, u32[]{:S(2)}, u32[]{:S(2)}) collective-permute-start(f32[8,512]{1,0:T(8,128)S(1)} %get-tuple-element.443), channel_id=1, source_target_pairs={{0,2},{1,3},{2,4},{3,5},{4,6},{5,7},{6,8},{7,9},{8,10},{9,11},{10,... | collective-permute-start | bytes 49160 | tf_op jit(solution)/shard_map/ppermute | solution.py:12
  391.9 30.0 %collective-permute-start.56 = (f32[8,512]{1,0:T(8,128)S(1)}, f32[8,512]{1,0:T(8,128)S(1)}, u32[]{:S(2)}, u32[]{:S(2)}) collective-permute-start(f32[8,512]{1,0:T(8,128)S(1)} %get-tuple-element.441), channel_id=1, source_target_pairs={{0,1},{1,2},{2,3},{3,4},{4,5},{5,6},{6,7},{7,8},{8,9},{9,10},{10,1... | collective-permute-start | bytes 49160 | tf_op jit(solution)/shard_map/ppermute | solution.py:12
  414.1 9.7 %collective-permute-start.18 = (f32[8,512]{1,0:T(8,128)S(1)}, f32[8,512]{1,0:T(8,128)S(1)}, u32[]{:S(2)}, u32[]{:S(2)}) collective-permute-start(f32[8,512]{1,0:T(8,128)S(1)} %get-tuple-element.438), channel_id=1, source_target_pairs={{0,3},{1,4},{2,5},{3,6},{4,7},{5,8},{6,9},{7,10},{8,11},{9,12},{10... | collective-permute-start | bytes 49160 | tf_op jit(solution)/shard_map/ppermute | solution.py:12
  423.9 9.7 %collective-permute-start.34 = (f32[8,512]{1,0:T(8,128)S(1)}, f32[8,512]{1,0:T(8,128)S(1)}, u32[]{:S(2)}, u32[]{:S(2)}) collective-permute-start(f32[8,512]{1,0:T(8,128)S(1)} %get-tuple-element.430), channel_id=1, source_target_pairs={{0,3},{1,4},{2,5},{3,6},{4,7},{5,8},{6,9},{7,10},{8,11},{9,12},{10... | collective-permute-start | bytes 49160 | tf_op jit(solution)/shard_map/ppermute | solution.py:12
  433.6 10.3 %collective-permute-start.25 = (f32[8,512]{1,0:T(8,128)S(1)}, f32[8,512]{1,0:T(8,128)S(1)}, u32[]{:S(2)}, u32[]{:S(2)}) collective-permute-start(f32[8,512]{1,0:T(8,128)S(1)} %get-tuple-element.435), channel_id=1, source_target_pairs={{0,2},{1,3},{2,4},{3,5},{4,6},{5,7},{6,8},{7,9},{8,10},{9,11},{10,... | collective-permute-start | bytes 49160 | tf_op jit(solution)/shard_map/ppermute | solution.py:12
  435.5 10.3 %collective-permute-start.24 = (f32[8,512]{1,0:T(8,128)S(1)}, f32[8,512]{1,0:T(8,128)S(1)}, u32[]{:S(2)}, u32[]{:S(2)}) collective-permute-start(f32[8,512]{1,0:T(8,128)S(1)} %get-tuple-element.433), channel_id=1, source_target_pairs={{0,1},{1,2},{2,3},{3,4},{4,5},{5,6},{6,7},{7,8},{8,9},{9,10},{10,1... | collective-permute-start | bytes 49160 | tf_op jit(solution)/shard_map/ppermute | solution.py:12
  437.5 10.3 %collective-permute-start.51 = (f32[8,512]{1,0:T(8,128)S(1)}, f32[8,512]{1,0:T(8,128)S(1)}, u32[]{:S(2)}, u32[]{:S(2)}) collective-permute-start(f32[8,512]{1,0:T(8,128)S(1)} %get-tuple-element.424), channel_id=1, source_target_pairs={{0,4},{1,5},{2,6},{3,7},{4,8},{5,9},{6,10},{7,11},{8,12},{9,13},{1... | collective-permute-start | bytes 49160 | tf_op jit(solution)/shard_map/ppermute | solution.py:12
  439.4 10.3 %collective-permute-start.50 = (f32[8,512]{1,0:T(8,128)S(1)}, f32[8,512]{1,0:T(8,128)S(1)}, u32[]{:S(2)}, u32[]{:S(2)}) collective-permute-start(f32[8,512]{1,0:T(8,128)S(1)} %get-tuple-element.422), channel_id=1, source_target_pairs={{0,3},{1,4},{2,5},{3,6},{4,7},{5,8},{6,9},{7,10},{8,11},{9,12},{10... | collective-permute-start | bytes 49160 | tf_op jit(solution)/shard_map/ppermute | solution.py:12
  441.3 10.3 %collective-permute-start.49 = (f32[8,512]{1,0:T(8,128)S(1)}, f32[8,512]{1,0:T(8,128)S(1)}, u32[]{:S(2)}, u32[]{:S(2)}) collective-permute-start(f32[8,512]{1,0:T(8,128)S(1)} %get-tuple-element.423), channel_id=1, source_target_pairs={{0,2},{1,3},{2,4},{3,5},{4,6},{5,7},{6,8},{7,9},{8,10},{9,11},{10,... | collective-permute-start | bytes 49160 | tf_op jit(solution)/shard_map/ppermute | solution.py:12
  443.9 10.5 %collective-permute-start.48 = (f32[8,512]{1,0:T(8,128)S(1)}, f32[8,512]{1,0:T(8,128)S(1)}, u32[]{:S(2)}, u32[]{:S(2)}) collective-permute-start(f32[8,512]{1,0:T(8,128)S(1)} %get-tuple-element.421), channel_id=1, source_target_pairs={{0,1},{1,2},{2,3},{3,4},{4,5},{5,6},{6,7},{7,8},{8,9},{9,10},{10,1... | collective-permute-start | bytes 49160 | tf_op jit(solution)/shard_map/ppermute | solution.py:12
  445.8 11.0 %collective-permute-start.43 = (f32[8,512]{1,0:T(8,128)S(1)}, f32[8,512]{1,0:T(8,128)S(1)}, u32[]{:S(2)}, u32[]{:S(2)}) collective-permute-start(f32[8,512]{1,0:T(8,128)S(1)} %get-tuple-element.428), channel_id=1, source_target_pairs={{0,4},{1,5},{2,6},{3,7},{4,8},{5,9},{6,10},{7,11},{8,12},{9,13},{1... | collective-permute-start | bytes 49160 | tf_op jit(solution)/shard_map/ppermute | solution.py:12
  447.8 12.8 %collective-permute-start.42 = (f32[8,512]{1,0:T(8,128)S(1)}, f32[8,512]{1,0:T(8,128)S(1)}, u32[]{:S(2)}, u32[]{:S(2)}) collective-permute-start(f32[8,512]{1,0:T(8,128)S(1)} %get-tuple-element.426), channel_id=1, source_target_pairs={{0,3},{1,4},{2,5},{3,6},{4,7},{5,8},{6,9},{7,10},{8,11},{9,12},{10... | collective-permute-start | bytes 49160 | tf_op jit(solution)/shard_map/ppermute | solution.py:12
  449.7 16.1 %collective-permute-start.41 = (f32[8,512]{1,0:T(8,128)S(1)}, f32[8,512]{1,0:T(8,128)S(1)}, u32[]{:S(2)}, u32[]{:S(2)}) collective-permute-start(f32[8,512]{1,0:T(8,128)S(1)} %get-tuple-element.427), channel_id=1, source_target_pairs={{0,2},{1,3},{2,4},{3,5},{4,6},{5,7},{6,8},{7,9},{8,10},{9,11},{10,... | collective-permute-start | bytes 49160 | tf_op jit(solution)/shard_map/ppermute | solution.py:12
  451.7 19.2 %collective-permute-start.40 = (f32[8,512]{1,0:T(8,128)S(1)}, f32[8,512]{1,0:T(8,128)S(1)}, u32[]{:S(2)}, u32[]{:S(2)}) collective-permute-start(f32[8,512]{1,0:T(8,128)S(1)} %get-tuple-element.425), channel_id=1, source_target_pairs={{0,1},{1,2},{2,3},{3,4},{4,5},{5,6},{6,7},{7,8},{8,9},{9,10},{10,1... | collective-permute-start | bytes 49160 | tf_op jit(solution)/shard_map/ppermute | solution.py:12
  454.5 20.0 %collective-permute-start.20 = (f32[8,512]{1,0:T(8,128)S(1)}, f32[8,512]{1,0:T(8,128)S(1)}, u32[]{:S(2)}, u32[]{:S(2)}) collective-permute-start(f32[8,512]{1,0:T(8,128)S(1)} %get-tuple-element.391), channel_id=1, source_target_pairs={{1,0},{2,1},{3,2},{4,3},{5,4},{6,5},{7,6},{8,7},{9,8},{10,9},{11,1... | collective-permute-start | bytes 49160 | tf_op jit(solution)/shard_map/ppermute | solution.py:12
  456.9 19.6 %collective-permute-start.21 = (f32[8,512]{1,0:T(8,128)S(1)}, f32[8,512]{1,0:T(8,128)S(1)}, u32[]{:S(2)}, u32[]{:S(2)}) collective-permute-start(f32[8,512]{1,0:T(8,128)S(1)} %get-tuple-element.391), channel_id=1, source_target_pairs={{2,0},{3,1},{4,2},{5,3},{6,4},{7,5},{8,6},{9,7},{10,8},{11,9},{12,... | collective-permute-start | bytes 49160 | tf_op jit(solution)/shard_map/ppermute | solution.py:12
  460.6 19.8 %collective-permute-start.23 = (f32[8,512]{1,0:T(8,128)S(1)}, f32[8,512]{1,0:T(8,128)S(1)}, u32[]{:S(2)}, u32[]{:S(2)}) collective-permute-start(f32[8,512]{1,0:T(8,128)S(1)} %get-tuple-element.391), channel_id=1, source_target_pairs={{4,0},{5,1},{6,2},{7,3},{8,4},{9,5},{10,6},{11,7},{12,8},{13,9},{1... | collective-permute-start | bytes 49160 | tf_op jit(solution)/shard_map/ppermute | solution.py:12
  465.8 16.9 %collective-permute-start.28 = (f32[8,512]{1,0:T(8,128)S(1)}, f32[8,512]{1,0:T(8,128)S(1)}, u32[]{:S(2)}, u32[]{:S(2)}) collective-permute-start(f32[8,512]{1,0:T(8,128)S(1)} %get-tuple-element.420), channel_id=1, source_target_pairs={{1,0},{2,1},{3,2},{4,3},{5,4},{6,5},{7,6},{8,7},{9,8},{10,9},{11,1... | collective-permute-start | bytes 49160 | tf_op jit(solution)/shard_map/ppermute | solution.py:12
  474.5 11.5 %collective-permute-start.29 = (f32[8,512]{1,0:T(8,128)S(1)}, f32[8,512]{1,0:T(8,128)S(1)}, u32[]{:S(2)}, u32[]{:S(2)}) collective-permute-start(f32[8,512]{1,0:T(8,128)S(1)} %get-tuple-element.420), channel_id=1, source_target_pairs={{2,0},{3,1},{4,2},{5,3},{6,4},{7,5},{8,6},{9,7},{10,8},{11,9},{12,... | collective-permute-start | bytes 49160 | tf_op jit(solution)/shard_map/ppermute | solution.py:12
  476.5 12.4 %collective-permute-start.30 = (f32[8,512]{1,0:T(8,128)S(1)}, f32[8,512]{1,0:T(8,128)S(1)}, u32[]{:S(2)}, u32[]{:S(2)}) collective-permute-start(f32[8,512]{1,0:T(8,128)S(1)} %get-tuple-element.420), channel_id=1, source_target_pairs={{3,0},{4,1},{5,2},{6,3},{7,4},{8,5},{9,6},{10,7},{11,8},{12,9},{13... | collective-permute-start | bytes 49160 | tf_op jit(solution)/shard_map/ppermute | solution.py:12
  478.5 12.9 %collective-permute-start.31 = (f32[8,512]{1,0:T(8,128)S(1)}, f32[8,512]{1,0:T(8,128)S(1)}, u32[]{:S(2)}, u32[]{:S(2)}) collective-permute-start(f32[8,512]{1,0:T(8,128)S(1)} %get-tuple-element.420), channel_id=1, source_target_pairs={{4,0},{5,1},{6,2},{7,3},{8,4},{9,5},{10,6},{11,7},{12,8},{13,9},{1... | collective-permute-start | bytes 49160 | tf_op jit(solution)/shard_map/ppermute | solution.py:12
  480.4 13.6 %collective-permute-start.36 = (f32[8,512]{1,0:T(8,128)S(1)}, f32[8,512]{1,0:T(8,128)S(1)}, u32[]{:S(2)}, u32[]{:S(2)}) collective-permute-start(f32[8,512]{1,0:T(8,128)S(1)} %get-tuple-element.397), channel_id=1, source_target_pairs={{1,0},{2,1},{3,2},{4,3},{5,4},{6,5},{7,6},{8,7},{9,8},{10,9},{11,1... | collective-permute-start | bytes 49160 | tf_op jit(solution)/shard_map/ppermute | solution.py:12
  482.8 13.2 %collective-permute-start.37 = (f32[8,512]{1,0:T(8,128)S(1)}, f32[8,512]{1,0:T(8,128)S(1)}, u32[]{:S(2)}, u32[]{:S(2)}) collective-permute-start(f32[8,512]{1,0:T(8,128)S(1)} %get-tuple-element.397), channel_id=1, source_target_pairs={{2,0},{3,1},{4,2},{5,3},{6,4},{7,5},{8,6},{9,7},{10,8},{11,9},{12,... | collective-permute-start | bytes 49160 | tf_op jit(solution)/shard_map/ppermute | solution.py:12
  486.0 11.9 %collective-permute-start.38 = (f32[8,512]{1,0:T(8,128)S(1)}, f32[8,512]{1,0:T(8,128)S(1)}, u32[]{:S(2)}, u32[]{:S(2)}) collective-permute-start(f32[8,512]{1,0:T(8,128)S(1)} %get-tuple-element.397), channel_id=1, source_target_pairs={{3,0},{4,1},{5,2},{6,3},{7,4},{8,5},{9,6},{10,7},{11,8},{12,9},{13... | collective-permute-start | bytes 49160 | tf_op jit(solution)/shard_map/ppermute | solution.py:12
  488.9 11.0 %collective-permute-start.39 = (f32[8,512]{1,0:T(8,128)S(1)}, f32[8,512]{1,0:T(8,128)S(1)}, u32[]{:S(2)}, u32[]{:S(2)}) collective-permute-start(f32[8,512]{1,0:T(8,128)S(1)} %get-tuple-element.397), channel_id=1, source_target_pairs={{4,0},{5,1},{6,2},{7,3},{8,4},{9,5},{10,6},{11,7},{12,8},{13,9},{1... | collective-permute-start | bytes 49160 | tf_op jit(solution)/shard_map/ppermute | solution.py:12
  491.4 10.7 %collective-permute-start.44 = (f32[8,512]{1,0:T(8,128)S(1)}, f32[8,512]{1,0:T(8,128)S(1)}, u32[]{:S(2)}, u32[]{:S(2)}) collective-permute-start(f32[8,512]{1,0:T(8,128)S(1)} %get-tuple-element.418), channel_id=1, source_target_pairs={{1,0},{2,1},{3,2},{4,3},{5,4},{6,5},{7,6},{8,7},{9,8},{10,9},{11,1... | collective-permute-start | bytes 49160 | tf_op jit(solution)/shard_map/ppermute | solution.py:12
  494.0 10.0 %collective-permute-start.45 = (f32[8,512]{1,0:T(8,128)S(1)}, f32[8,512]{1,0:T(8,128)S(1)}, u32[]{:S(2)}, u32[]{:S(2)}) collective-permute-start(f32[8,512]{1,0:T(8,128)S(1)} %get-tuple-element.418), channel_id=1, source_target_pairs={{2,0},{3,1},{4,2},{5,3},{6,4},{7,5},{8,6},{9,7},{10,8},{11,9},{12,... | collective-permute-start | bytes 49160 | tf_op jit(solution)/shard_map/ppermute | solution.py:12
  496.0 10.0 %collective-permute-start.46 = (f32[8,512]{1,0:T(8,128)S(1)}, f32[8,512]{1,0:T(8,128)S(1)}, u32[]{:S(2)}, u32[]{:S(2)}) collective-permute-start(f32[8,512]{1,0:T(8,128)S(1)} %get-tuple-element.418), channel_id=1, source_target_pairs={{3,0},{4,1},{5,2},{6,3},{7,4},{8,5},{9,6},{10,7},{11,8},{12,9},{13... | collective-permute-start | bytes 49160 | tf_op jit(solution)/shard_map/ppermute | solution.py:12
  497.9 10.0 %collective-permute-start.47 = (f32[8,512]{1,0:T(8,128)S(1)}, f32[8,512]{1,0:T(8,128)S(1)}, u32[]{:S(2)}, u32[]{:S(2)}) collective-permute-start(f32[8,512]{1,0:T(8,128)S(1)} %get-tuple-element.418), channel_id=1, source_target_pairs={{4,0},{5,1},{6,2},{7,3},{8,4},{9,5},{10,6},{11,7},{12,8},{13,9},{1... | collective-permute-start | bytes 49160 | tf_op jit(solution)/shard_map/ppermute | solution.py:12
  499.9 10.1 %collective-permute-start.52 = (f32[8,512]{1,0:T(8,128)S(1)}, f32[8,512]{1,0:T(8,128)S(1)}, u32[]{:S(2)}, u32[]{:S(2)}) collective-permute-start(f32[8,512]{1,0:T(8,128)S(1)} %get-tuple-element.393), channel_id=1, source_target_pairs={{1,0},{2,1},{3,2},{4,3},{5,4},{6,5},{7,6},{8,7},{9,8},{10,9},{11,1... | collective-permute-start | bytes 49160 | tf_op jit(solution)/shard_map/ppermute | solution.py:12
  502.1 9.8 %collective-permute-start.53 = (f32[8,512]{1,0:T(8,128)S(1)}, f32[8,512]{1,0:T(8,128)S(1)}, u32[]{:S(2)}, u32[]{:S(2)}) collective-permute-start(f32[8,512]{1,0:T(8,128)S(1)} %get-tuple-element.393), channel_id=1, source_target_pairs={{2,0},{3,1},{4,2},{5,3},{6,4},{7,5},{8,6},{9,7},{10,8},{11,9},{12,... | collective-permute-start | bytes 49160 | tf_op jit(solution)/shard_map/ppermute | solution.py:12
  504.0 9.8 %collective-permute-start.54 = (f32[8,512]{1,0:T(8,128)S(1)}, f32[8,512]{1,0:T(8,128)S(1)}, u32[]{:S(2)}, u32[]{:S(2)}) collective-permute-start(f32[8,512]{1,0:T(8,128)S(1)} %get-tuple-element.393), channel_id=1, source_target_pairs={{3,0},{4,1},{5,2},{6,3},{7,4},{8,5},{9,6},{10,7},{11,8},{12,9},{13... | collective-permute-start | bytes 49160 | tf_op jit(solution)/shard_map/ppermute | solution.py:12
  506.0 9.8 %collective-permute-start.55 = (f32[8,512]{1,0:T(8,128)S(1)}, f32[8,512]{1,0:T(8,128)S(1)}, u32[]{:S(2)}, u32[]{:S(2)}) collective-permute-start(f32[8,512]{1,0:T(8,128)S(1)} %get-tuple-element.393), channel_id=1, source_target_pairs={{4,0},{5,1},{6,2},{7,3},{8,4},{9,5},{10,6},{11,7},{12,8},{13,9},{1... | collective-permute-start | bytes 49160 | tf_op jit(solution)/shard_map/ppermute | solution.py:12
  (153 other events, 1189.0 us)
where the time goes:
time: 890 us; the launch traced here: 881 us
  matrix products  308 us (35%)
  local copies, waits for them, and re-layouts  235 us (26%)
  starting transfers between devices  202 us (23%)
  waiting for transfers between devices  129 us (14%)
    dot_general x72, matrix products, contract(): return jnp.dot(matrix, operand.T, preferred_element_type=jnp.float32)  213 us
    ppermute x64, starting transfers between devices, shifted_2(): return lax.ppermute(block, axis, route)  202 us
    dynamic_update_slice x32, local copies, waits for them, and re-layouts, queries_moved(): lax.map(lambda items: key_side_terms(*items, visible), stacked + stats)  150 us
    ppermute x64, waiting for transfers between devices, shifted_2(): return lax.ppermute(block, axis, route)  129 us
    dot_general x40, matrix products, transposed(): return jnp.dot(matrix.T, operand, preferred_element_type=jnp.float32)  94.5 us
    unnamed x69, local copies, waits for them, and re-layouts  22.7 us
  transfers between devices with their start and end apart: 64, of which 10 were waited for; matrix products, arithmetic and copies ran while one was open for 5% of the time, Pallas kernels for 0%

commit v1 on v0

v1 whole, which is shorter than its diff:
```python
import functools

import jax
import jax.numpy as jnp
from jax import lax
from jax.experimental import pallas as pl
from jax.experimental.pallas import tpu as pltpu
from jax.sharding import PartitionSpec as P

WINDOW_LENGTH = 1024
HIDDEN = -1e30
TAIL = 16
F32 = jnp.float32
BF16 = jnp.bfloat16


def shifted(block, distance):
    devices = range(lax.axis_size("ctx"))
    route = [(i, i + distance) for i in devices if i + distance in devices]
    return lax.ppermute(block, "ctx", route)


def swapped(block, partner):
    devices = range(lax.axis_size("ctx"))
    return lax.ppermute(block, "ctx", [(i, i ^ partner) for i in devices])


def pack_kernel(plane, heads, group, meta, *refs):
    seg = refs[-1 - plane * heads - 1] if group == 1 else None
    arrays = refs[: len(refs) - 1 - plane * heads - (group == 1)]
    outs = refs[-1 - plane * heads : -1]
    wide = refs[-1]
    me = meta[0]
    for t, array in enumerate(arrays):
        rows, count, width = array.shape
        wide[...] = array[...].astype(F32).reshape(rows * count, width)
        for h in range(heads):
            for k in range(plane):
                first = ((me ^ k) * heads + h) * group
                for g in range(group):
                    at = (t * group + g) * rows
                    outs[h * plane + k][at : at + rows, :] = wide[
                        pl.ds(first + g, rows, stride=count), :
                    ].astype(BF16)
    if group == 1:
        for out in outs:
            out[len(arrays) * rows :, :] = seg[...]


def pack(meta, arrays, plane, heads, group, seg=None):
    rows, count, width = arrays[0].shape
    length = len(arrays) * group * rows + (0 if seg is None else TAIL)
    vmem = pl.BlockSpec(memory_space=pltpu.VMEM)
    inputs = list(arrays) + ([] if seg is None else [seg])
    return pl.pallas_call(
        functools.partial(pack_kernel, plane, heads, group),
        out_shape=[jax.ShapeDtypeStruct((length, width), BF16)] * (plane * heads),
        in_specs=[pl.BlockSpec(memory_space=pltpu.SMEM)] + [vmem] * len(inputs),
        out_specs=[vmem] * (plane * heads),
        scratch_shapes=[pltpu.VMEM((rows * count, width), F32)],
        name="pack",
    )(meta, *inputs)


def attend_kernel(plane, group, rows, width, meta, *refs):
    own, prev, queries = refs[:plane], refs[plane : 2 * plane], refs[2 * plane : 3 * plane]
    out_prev, out_own = refs[3 * plane : 4 * plane], refs[4 * plane : 5 * plane]
    ka, kd, vv, segs, qq, do, qt, qa, dt, s, sd, u, ud, acc, tri, lims, sem = refs[5 * plane :]
    me, valid = meta[0], meta[1]
    span = group * rows
    factor = width ** (-0.5)
    slope = factor * 1.4426950408889634

    copies = []

    def fetch(source, target):
        copy = pltpu.make_async_copy(source, target, sem.at[len(copies)])
        copy.start()
        copies.append(copy)

    low, high = pl.ds(0, width), pl.ds(width, width)
    for k in range(plane):
        for piece, base in ((own[k], plane), (prev[k], 0)):
            block = base + (me ^ k)
            part = [piece.at[pl.ds(t * rows, rows), :] for t in range(4)]
            fetch(part[0], ka.at[block, :, low])
            fetch(part[0], kd.at[block, :, high])
            fetch(part[1], vv.at[block, 0])
            fetch(part[2], kd.at[block, :, low])
            fetch(part[3], vv.at[block, 1])
            fetch(piece.at[pl.ds(4 * rows, TAIL), :], segs.at[block])
        block = me ^ k
        part = [queries[k].at[pl.ds(t * span, span), :] for t in range(3)]
        fetch(part[0], qq.at[block, :, low])
        fetch(part[1], qq.at[block, :, high])
        fetch(part[2], do.at[block])
    key_at = lax.broadcasted_iota(jnp.int32, (rows, rows), 0)
    row_at = lax.broadcasted_iota(jnp.int32, (rows, rows), 1)
    for g in range(group):
        lanes = slice(g * rows, (g + 1) * rows)
        tri[0, :, lanes] = jnp.where(key_at > row_at, 0.0, HIDDEN)
        tri[1, :, lanes] = jnp.where(key_at <= row_at, 0.0, HIDDEN)
    acc[...] = jnp.zeros_like(acc)
    for copy in copies:
        copy.wait()

    lane_rows = rows // width

    def document_row(block):
        tail = segs[block].astype(F32)
        return jnp.concatenate([tail[r : r + 1, :] for r in range(lane_rows)], axis=1)

    names = lax.broadcasted_iota(jnp.int32, (width, rows), 0).astype(F32)
    for block in range(2 * plane):
        docs = document_row(block)
        hot = jnp.where(names == docs, 1.0, 0.0)
        ka[block, :, width:] = hot.T.astype(BF16)
        last = jnp.max(docs)
        lims[0, block] = jnp.min(docs)
        lims[1, block] = jnp.where(valid > 0, last, -1.0) if block < plane else last

    def folded(values):
        return values.reshape(rows // 8, 8, span)

    def one_block(a, carry):
        first = lims[0, plane + a]
        skip = sum((lims[1, a + b] < first).astype(jnp.int32) for b in range(plane))
        both = qq[a].astype(F32).T.astype(BF16)
        qt[...] = both
        qa[:width, :] = both[:width, :]
        docs = document_row(plane + a)
        cover = jnp.where(names == docs, 0.0, HIDDEN).astype(BF16)
        for g in range(group):
            qa[width:, g * rows : (g + 1) * rows] = cover
        dt[...] = do[a].astype(F32).T.astype(BF16)

        def score(b, bias, top):
            value = jnp.dot(ka[a + b], qa[...], preferred_element_type=F32)
            if bias is not None:
                value = value + tri[bias]
            s[b] = value
            return jnp.maximum(top, jnp.max(folded(value), axis=0))

        top = jnp.full((8, span), HIDDEN, F32)
        top = score(plane, 1, top)
        top = lax.fori_loop(jnp.maximum(skip, 1), plane, lambda b, t: score(b, None, t), top)
        top = lax.cond(skip == 0, lambda t: score(0, 0, t), lambda t: t, top)
        peak = slope * jnp.max(top, axis=0, keepdims=True)

        def sums(b, carry):
            total, dots, ups, both = carry
            weight = jnp.exp2(slope * s[b] - peak)
            s[b] = weight
            dot = factor * jnp.dot(kd[a + b], qt[...], preferred_element_type=F32)
            sd[b] = dot
            up = jnp.dot(vv[a + b, 0], dt[...], preferred_element_type=F32)
            u[b] = up
            updot = jnp.dot(vv[a + b, 1], dt[...], preferred_element_type=F32)
            ud[b] = updot
            total = total + jnp.sum(folded(weight), axis=0)
            dots = dots + jnp.sum(folded(weight * dot), axis=0)
            ups = ups + jnp.sum(folded(weight * up), axis=0)
            both = both + jnp.sum(folded(weight * (dot * up + updot)), axis=0)
            return total, dots, ups, both

        zero = jnp.zeros((8, span), F32)
        carried = lax.fori_loop(skip, plane + 1, sums, (zero, zero, zero, zero))
        total, dots, ups, both = (jnp.sum(x, axis=0, keepdims=True) for x in carried)
        share = 1.0 / total
        mean_dot = dots * share
        center = ups * share
        center_dot = both * share - mean_dot * center

        def adjoints(b, carry):
            mix = s[b] * share
            dot = sd[b] - mean_dot
            up = u[b] - center
            mix_dot = mix * dot
            grad = mix * up
            grad_dot = mix * (dot * up + (ud[b] - center_dot))
            mix_b, mix_dot_b = mix.astype(BF16), mix_dot.astype(BF16)
            grad_b, grad_dot_b = grad.astype(BF16), grad_dot.astype(BF16)
            cot = do[a]
            pair = jnp.dot(grad_b, qq[a], preferred_element_type=F32)
            acc[a + b, 0] += pair[:, :width]
            acc[a + b, 1] += jnp.dot(mix_b, cot, preferred_element_type=F32)
            acc[a + b, 2] += pair[:, width:] + jnp.dot(
                grad_dot_b, qq[a, :, :width], preferred_element_type=F32
            )
            acc[a + b, 3] += jnp.dot(mix_dot_b, cot, preferred_element_type=F32)
            return carry

        lax.fori_loop(skip, plane + 1, adjoints, 0)
        return carry

    lax.fori_loop(0, plane, one_block, 0)
    for k in range(plane):
        for t in range(4):
            scale = factor if t % 2 == 0 else 1.0
            at = slice(t * rows, (t + 1) * rows)
            out_prev[k][at, :] = (scale * acc[me ^ k, t]).astype(BF16)
            out_own[k][at, :] = scale * acc[plane + (me ^ k), t]


def attend(meta, own, prev, queries, plane, group):
    length, width = own[0].shape
    rows = (length - TAIL) // 4
    span = group * rows
    vmem = pl.BlockSpec(memory_space=pltpu.VMEM)
    blocks = 2 * plane
    results = pl.pallas_call(
        functools.partial(attend_kernel, plane, group, rows, width),
        out_shape=[jax.ShapeDtypeStruct((4 * rows, width), BF16)] * plane
        + [jax.ShapeDtypeStruct((4 * rows, width), F32)] * plane,
        in_specs=[pl.BlockSpec(memory_space=pltpu.SMEM)]
        + [pl.BlockSpec(memory_space=pl.ANY)] * (3 * plane),
        out_specs=[vmem] * (2 * plane),
        scratch_shapes=[
            pltpu.VMEM((blocks, rows, 2 * width), BF16),
            pltpu.VMEM((blocks, rows, 2 * width), BF16),
            pltpu.VMEM((blocks, 2, rows, width), BF16),
            pltpu.VMEM((blocks, TAIL, width), BF16),
            pltpu.VMEM((plane, span, 2 * width), BF16),
            pltpu.VMEM((plane, span, width), BF16),
            pltpu.VMEM((2 * width, span), BF16),
            pltpu.VMEM((2 * width, span), BF16),
            pltpu.VMEM((width, span), BF16),
        ]
        + [pltpu.VMEM((plane + 1, rows, span), F32)] * 4
        + [
            pltpu.VMEM((blocks, 4, rows, width), F32),
            pltpu.VMEM((2, rows, span), F32),
            pltpu.SMEM((2, blocks), F32),
            pltpu.SemaphoreType.DMA((15 * plane,)),
        ],
        name="attend",
    )(meta, *own, *prev, *queries)
    return results[:plane], results[plane:]


def finish_kernel(plane, heads, meta, *refs):
    pieces, returned = refs[: plane * heads], refs[plane * heads : plane * heads + heads]
    outs = refs[-4:]
    me = meta[0]
    for h in range(heads):
        for k in range(plane):
            piece = pieces[h * plane + k]
            rows = piece.shape[0] // 4
            head = (me ^ k) * heads + h
            for t in range(4):
                at = slice(t * rows, (t + 1) * rows)
                value = piece[at, :].astype(F32)
                if k == 0:
                    value = value + returned[h][at, :].astype(F32)
                outs[t][pl.ds(head, rows, stride=plane * heads), :] = value


def finish(meta, pieces, returned, plane, heads):
    length, width = pieces[0].shape
    vmem = pl.BlockSpec(memory_space=pltpu.VMEM)
    return pl.pallas_call(
        functools.partial(finish_kernel, plane, heads),
        out_shape=[jax.ShapeDtypeStruct((length // 4 * plane * heads, width), F32)] * 4,
        in_specs=[pl.BlockSpec(memory_space=pltpu.SMEM)] + [vmem] * (plane * heads + heads),
        out_specs=[vmem] * 4,
        name="finish",
    )(meta, *pieces, *returned)


def local(
    query, query_tangent, keys, values, key_direction, value_direction, out_cotangent, segment_ids
):
    rows, kv_heads, width = keys.shape
    group = query.shape[1] // kv_heads
    plane = WINDOW_LENGTH // rows
    heads = kv_heads // plane
    device = lax.axis_index("ctx")
    meta = jnp.stack([device % plane, device // plane]).astype(jnp.int32)
    seg = jnp.zeros((TAIL, width), BF16)
    seg = seg.at[: rows // width].set(segment_ids.reshape(rows // width, width).astype(BF16))
    kv = pack(meta, (keys, values, key_direction, value_direction), plane, heads, 1, seg)
    qs = pack(meta, (query, query_tangent, out_cotangent), plane, heads, group)

    pieces, returned = [], []
    for h in range(heads):
        own = [kv[h * plane]] + [swapped(kv[h * plane + k], k) for k in range(1, plane)]
        prev = [shifted(own[k], plane) for k in range(plane)]
        queries = [qs[h * plane]] + [swapped(qs[h * plane + k], k) for k in range(1, plane)]
        sums_prev, sums_own = attend(meta, own, prev, queries, plane, group)
        back = [shifted(sums_prev[k], -plane) for k in range(plane)]
        returned.append(back[0])
        pieces.append(sums_own[0])
        for k in range(1, plane):
            pieces.append(swapped((sums_own[k] + back[k].astype(F32)).astype(BF16), k))
    outs = finish(meta, pieces, returned, plane, heads)
    return tuple(out.reshape(rows, kv_heads, width) for out in outs)


def solution(mesh):
    whole = P(("groups", "ctx"), None, None)
    return jax.shard_map(
        local,
        mesh=mesh,
        in_specs=(whole,) * 7 + (P(("groups", "ctx")),),
        out_specs=(whole,) * 4,
        check_vma=False,
    )
```

time: 890 us -> 159 us (0.18)
  matrix products: 308 us -> 0 us
  local copies, waits for them, and re-layouts: 235 us -> 5.22 us
  starting transfers between devices: 202 us -> 53.3 us
  waiting for transfers between devices: 129 us -> 37.9 us
  Pallas kernels: 0 us -> 59.1 us
    dot_general x112 -> x0, matrix products: 308 us -> none  [the longest x72 213 us: contract(): return jnp.dot(matrix, operand.T, preferred_element_type=jnp.float32)]
    dynamic_update_slice x80 -> x0, local copies, waits for them, and re-layouts: 162 us -> none  [the longest x32 150 us: queries_moved(): lax.map(lambda items: key_side_terms(*items, visible), stacked + stats)]
    ppermute x64 -> x34, starting transfers between devices: 202 us -> 53.3 us  [the longest x16 38.5 us: shifted(): return lax.ppermute(block, 'ctx', route)]
    ppermute x64 -> x34, waiting for transfers between devices: 129 us -> 37.9 us  [the longest x18 21.3 us: swapped(): return lax.ppermute(block, 'ctx', [(i, i ^ partner) for i in devices])]
    pallas_call x0 -> x5, Pallas kernels: none -> 59.1 us  [the longest x2 42.9 us: attend(): pl.pallas_call(functools.partial(attend_kernel, plane, group, rows, width...]
    unnamed x69 -> x64, local copies, waits for them, and re-layouts: 22.7 us -> 4.63 us
    dynamic_slice x24 -> x0, local copies, waits for them, and re-layouts: 16.6 us -> none  [queries_moved(): lax.map(lambda items: key_side_terms(*items, visible), stacked + stats)]
    reshape x3 -> x0, local copies, waits for them, and re-layouts: 15.3 us -> none  [by_head(): array.reshape(row_count, kv_heads, query_group, head_size)]
  transfers between devices with their start and end apart: 64 -> 34, of which waited for: 10 -> 12; matrix products, arithmetic and copies ran while one was open for 5% -> 0% of each run, Pallas kernels for 0% -> 32%
where the time goes in v1:
time: 159 us; the launch traced here: 158 us
  Pallas kernels  59.1 us (37%)
  starting transfers between devices  53.3 us (34%)
  waiting for transfers between devices  37.9 us (24%)
  local copies, waits for them, and re-layouts  5.22 us (3%)
    pallas_call x2, Pallas kernels, attend(): pl.pallas_call(functools.partial(attend_kernel, plane, group, rows, width...  42.9 us
    ppermute x16, starting transfers between devices, shifted(): return lax.ppermute(block, 'ctx', route)  38.5 us
    ppermute x18, waiting for transfers between devices, swapped(): return lax.ppermute(block, 'ctx', [(i, i ^ partner) for i in devices])  21.3 us
    ppermute x16, waiting for transfers between devices, shifted(): return lax.ppermute(block, 'ctx', route)  16.6 us
    ppermute x18, starting transfers between devices, swapped(): return lax.ppermute(block, 'ctx', [(i, i ^ partner) for i in devices])  14.8 us
    pallas_call x2, Pallas kernels, pack(): pl.pallas_call(functools.partial(pack_kernel, plane, heads, group), out_s...  11.3 us
    pallas_call x1, Pallas kernels, finish(): pl.pallas_call(functools.partial(finish_kernel, plane, heads), out_shape=...  4.9 us
    unnamed x64, local copies, waits for them, and re-layouts  4.63 us
  transfers between devices with their start and end apart: 34, of which 12 were waited for; matrix products, arithmetic and copies ran while one was open for 0% of the time, Pallas kernels for 32%

profile of v1, /device:TPU:21, one launch (start us, length us, event | category | flops | bytes accessed | tf_op | source)
XLA Modules:
  0.0 157.8 jit_solution(11481941519252865955)
XLA Ops:
  0.7 0.7 copy-done.31
  1.3 0.6 pad_add_fusion.meta
  1.9 0.6 scatter.4.refs_4_
  2.5 4.1 %pack.2 = (bf16[1040,128]{1,0:T(8,128)(2,1)}, bf16[1040,128]{1,0:T(8,128)(2,1)}, bf16[1040,128]{1,0:T(8,128)(2,1)}, bf16[1040,128]{1,0:T(8,128)(2,1)}, bf16[1040...) custom-call(s32[2]{0:T(128)} %pad_add_fusion.meta, ...), custom_call_target="tpu_custom_call" | custom-call | tf_op jit(solution)/shard_map/pack/pallas_call | solution.py:55
  6.7 0.7 collective-permute-start.16
  7.6 1.4 collective-permute-start.18
  9.0 3.2 %collective-permute-start.19 = (bf16[1040,128]{1,0:T(8,128)(2,1)}, bf16[1040,128]{1,0:T(8,128)(2,1)S(1)}, u32[]{:S(2)}, u32[]{:S(2)}) collective-permute-start(bf16[1040,128]{1,0:T(8,128)(2,1)} %get-tuple-element.67.refs_0_), channel_id=1, source_target_pairs={{0,4},{1,5},{2,6},{3,7},{4,8},{5,9},{6,10},{7,11},{8,12},{9,13},{1... | collective-permute-start | bytes 798728 | tf_op jit(solution)/shard_map/ppermute | solution.py:20
  13.0 2.6 %collective-permute-done.17.refs_2_ = bf16[1040,128]{1,0:T(8,128)(2,1)} collective-permute-done((bf16[1040,128]{1,0:T(8,128)(2,1)}, bf16[1040,128]{1,0:T(8,128)(2,1)}, u32[]{:S(2)}, u32[]{:S(2)}) %collective-permute-start.17) | collective-permute-done | bytes 266272 | tf_op jit(solution)/shard_map/ppermute | solution.py:25
  15.6 1.5 collective-permute-start.2
  17.1 7.2 %pack.3 = (bf16[1536,128]{1,0:T(8,128)(2,1)}, bf16[1536,128]{1,0:T(8,128)(2,1)}, bf16[1536,128]{1,0:T(8,128)(2,1)}, bf16[1536,128]{1,0:T(8,128)(2,1)}, bf16[1536...) custom-call(s32[2]{0:T(128)} %pad_add_fusion.meta, ...), custom_call_target="tpu_custom_call" | custom-call | tf_op jit(solution)/shard_map/pack/pallas_call | solution.py:55
  24.3 1.3 collective-permute-start.24
  25.6 0.8 collective-permute-start.25
  26.9 3.2 %collective-permute-start.3 = (bf16[1040,128]{1,0:T(8,128)(2,1)S(1)}, bf16[1040,128]{1,0:T(8,128)(2,1)S(1)}, u32[]{:S(2)}, u32[]{:S(2)}) collective-permute-start(bf16[1040,128]{1,0:T(8,128)(2,1)S(1)} %copy-done.12), channel_id=1, source_target_pairs={{0,4},{1,5},{2,6},{3,7},{4,8},{5,9},{6,10},{7,11},{8,12},{9,13},{1... | collective-permute-start | bytes 798728 | tf_op jit(solution)/shard_map/ppermute | solution.py:20
  30.1 3.5 %collective-permute-done.2.refs_3_ = bf16[1040,128]{1,0:T(8,128)(2,1)S(1)} collective-permute-done((bf16[1040,128]{1,0:T(8,128)(2,1)}, bf16[1040,128]{1,0:T(8,128)(2,1)S(1)}, u32[]{:S(2)}, u32[]{:S(2)}) %collective-permute-start.2) | collective-permute-done | bytes 266272 | tf_op jit(solution)/shard_map/ppermute | solution.py:25
  33.6 1.7 %collective-permute-done.3.refs_4_ = bf16[1040,128]{1,0:T(8,128)(2,1)S(1)} collective-permute-done((bf16[1040,128]{1,0:T(8,128)(2,1)S(1)}, bf16[1040,128]{1,0:T(8,128)(2,1)S(1)}, u32[]{:S(2)}, u32[]{:S(2)}) %collective-permute-start.3) | collective-permute-done | bytes 266272 | tf_op jit(solution)/shard_map/ppermute | solution.py:20
  35.3 0.7 copy-done.17
  36.0 1.3 collective-permute-start.8
  37.3 3.2 %collective-permute-start.20 = (bf16[1040,128]{1,0:T(8,128)(2,1)}, bf16[1040,128]{1,0:T(8,128)(2,1)}, u32[]{:S(2)}, u32[]{:S(2)}) collective-permute-start(bf16[1040,128]{1,0:T(8,128)(2,1)} %collective-permute-done.16.refs_1_), channel_id=1, source_target_pairs={{0,4},{1,5},{2,6},{3,7},{4,8},{5,9},{6,10},{7,11},{8,12},{9,13},{1... | collective-permute-start | bytes 798728 | tf_op jit(solution)/shard_map/ppermute | solution.py:20
  41.0 3.2 %collective-permute-start.21 = (bf16[1040,128]{1,0:T(8,128)(2,1)}, bf16[1040,128]{1,0:T(8,128)(2,1)S(1)}, u32[]{:S(2)}, u32[]{:S(2)}) collective-permute-start(bf16[1040,128]{1,0:T(8,128)(2,1)} %collective-permute-done.17.refs_2_), channel_id=1, source_target_pairs={{0,4},{1,5},{2,6},{3,7},{4,8},{5,9},{6,10},{7,11},{8,12},{9,13},{1... | collective-permute-start | bytes 798728 | tf_op jit(solution)/shard_map/ppermute | solution.py:20
  44.2 6.2 %collective-permute-done.25.refs_11_ = bf16[1536,128]{1,0:T(8,128)(2,1)S(1)} collective-permute-done((bf16[1536,128]{1,0:T(8,128)(2,1)}, bf16[1536,128]{1,0:T(8,128)(2,1)S(1)}, u32[]{:S(2)}, u32[]{:S(2)}) %collective-permute-start.25) | collective-permute-done | bytes 393248 | tf_op jit(solution)/shard_map/ppermute | solution.py:25
  50.4 3.2 %collective-permute-start.22 = (bf16[1040,128]{1,0:T(8,128)(2,1)}, bf16[1040,128]{1,0:T(8,128)(2,1)S(1)}, u32[]{:S(2)}, u32[]{:S(2)}) collective-permute-start(bf16[1040,128]{1,0:T(8,128)(2,1)} %collective-permute-done.18.refs_3_), channel_id=1, source_target_pairs={{0,4},{1,5},{2,6},{3,7},{4,8},{5,9},{6,10},{7,11},{8,12},{9,13},{1... | collective-permute-start | bytes 798728 | tf_op jit(solution)/shard_map/ppermute | solution.py:20
  53.7 1.9 %collective-permute-start.4 = (bf16[1040,128]{1,0:T(8,128)(2,1)S(1)}, bf16[1040,128]{1,0:T(8,128)(2,1)S(1)}, u32[]{:S(2)}, u32[]{:S(2)}) collective-permute-start(bf16[1040,128]{1,0:T(8,128)(2,1)S(1)} %collective-permute-done.refs_1_), channel_id=1, source_target_pairs={{0,4},{1,5},{2,6},{3,7},{4,8},{5,9},{6,10},{7,11},{8,12},{9,13},{1... | collective-permute-start | bytes 798728 | tf_op jit(solution)/shard_map/ppermute | solution.py:20
  55.7 1.9 %collective-permute-start.5 = (bf16[1040,128]{1,0:T(8,128)(2,1)S(1)}, bf16[1040,128]{1,0:T(8,128)(2,1)}, u32[]{:S(2)}, u32[]{:S(2)}) collective-permute-start(bf16[1040,128]{1,0:T(8,128)(2,1)S(1)} %collective-permute-done.1.refs_2_), channel_id=1, source_target_pairs={{0,4},{1,5},{2,6},{3,7},{4,8},{5,9},{6,10},{7,11},{8,12},{9,13},{1... | collective-permute-start | bytes 798728 | tf_op jit(solution)/shard_map/ppermute | solution.py:20
  57.6 3.3 %collective-permute-done.22.refs_7_ = bf16[1040,128]{1,0:T(8,128)(2,1)S(1)} collective-permute-done((bf16[1040,128]{1,0:T(8,128)(2,1)}, bf16[1040,128]{1,0:T(8,128)(2,1)S(1)}, u32[]{:S(2)}, u32[]{:S(2)}) %collective-permute-start.22) | collective-permute-done | bytes 266272 | tf_op jit(solution)/shard_map/ppermute | solution.py:20
  60.9 0.7 copy-done.20
  61.6 3.2 %collective-permute-start.6 = (bf16[1040,128]{1,0:T(8,128)(2,1)S(1)}, bf16[1040,128]{1,0:T(8,128)(2,1)}, u32[]{:S(2)}, u32[]{:S(2)}) collective-permute-start(bf16[1040,128]{1,0:T(8,128)(2,1)S(1)} %collective-permute-done.2.refs_3_), channel_id=1, source_target_pairs={{0,4},{1,5},{2,6},{3,7},{4,8},{5,9},{6,10},{7,11},{8,12},{9,13},{1... | collective-permute-start | bytes 798728 | tf_op jit(solution)/shard_map/ppermute | solution.py:20
  64.9 21.4 %attend.3 = (bf16[1024,128]{1,0:T(8,128)(2,1)}, bf16[1024,128]{1,0:T(8,128)(2,1)}, bf16[1024,128]{1,0:T(8,128)(2,1)}, bf16[1024,128]{1,0:T(8,128)(2,1)}, f32[102...) custom-call(s32[2]{0:T(128)} %pad_add_fusion.meta, ...), custom_call_target="tpu_custom_call" | custom-call | tf_op jit(solution)/shard_map/attend/pallas_call | solution.py:211
  86.4 1.9 %collective-permute-start.30 = (bf16[1024,128]{1,0:T(8,128)(2,1)}, bf16[1024,128]{1,0:T(8,128)(2,1)S(1)}, u32[]{:S(2)}, u32[]{:S(2)}) collective-permute-start(bf16[1024,128]{1,0:T(8,128)(2,1)} %get-tuple-element.81), channel_id=1, source_target_pairs={{4,0},{5,1},{6,2},{7,3},{8,4},{9,5},{10,6},{11,7},{12,8},{13,9},{1... | collective-permute-start | bytes 786440 | tf_op jit(solution)/shard_map/ppermute | solution.py:20
  88.3 1.9 %collective-permute-start.28 = (bf16[1024,128]{1,0:T(8,128)(2,1)}, bf16[1024,128]{1,0:T(8,128)(2,1)S(1)}, u32[]{:S(2)}, u32[]{:S(2)}) collective-permute-start(bf16[1024,128]{1,0:T(8,128)(2,1)} %get-tuple-element.79), channel_id=1, source_target_pairs={{4,0},{5,1},{6,2},{7,3},{8,4},{9,5},{10,6},{11,7},{12,8},{13,9},{1... | collective-permute-start | bytes 786440 | tf_op jit(solution)/shard_map/ppermute | solution.py:20
  90.3 1.9 %collective-permute-start.26 = (bf16[1024,128]{1,0:T(8,128)(2,1)}, bf16[1024,128]{1,0:T(8,128)(2,1)S(1)}, u32[]{:S(2)}, u32[]{:S(2)}) collective-permute-start(bf16[1024,128]{1,0:T(8,128)(2,1)} %get-tuple-element.77), channel_id=1, source_target_pairs={{4,0},{5,1},{6,2},{7,3},{8,4},{9,5},{10,6},{11,7},{12,8},{13,9},{1... | collective-permute-start | bytes 786440 | tf_op jit(solution)/shard_map/ppermute | solution.py:20
  92.2 2.1 %collective-permute-start.33 = (bf16[1024,128]{1,0:T(8,128)(2,1)}, bf16[1024,128]{1,0:T(8,128)(2,1)S(1)}, u32[]{:S(2)}, u32[]{:S(2)}) collective-permute-start(bf16[1024,128]{1,0:T(8,128)(2,1)} %get-tuple-element.83), channel_id=1, source_target_pairs={{4,0},{5,1},{6,2},{7,3},{8,4},{9,5},{10,6},{11,7},{12,8},{13,9},{1... | collective-permute-start | bytes 786440 | tf_op jit(solution)/shard_map/ppermute | solution.py:20
  94.3 21.5 %attend.2 = (bf16[1024,128]{1,0:T(8,128)(2,1)}, bf16[1024,128]{1,0:T(8,128)(2,1)}, bf16[1024,128]{1,0:T(8,128)(2,1)}, bf16[1024,128]{1,0:T(8,128)(2,1)}, f32[102...) custom-call(s32[2]{0:T(128)} %pad_add_fusion.meta, ...), custom_call_target="tpu_custom_call" | custom-call | tf_op jit(solution)/shard_map/attend/pallas_call | solution.py:211
  115.9 1.9 %collective-permute-start.14 = (bf16[1024,128]{1,0:T(8,128)(2,1)}, bf16[1024,128]{1,0:T(8,128)(2,1)S(1)}, u32[]{:S(2)}, u32[]{:S(2)}) collective-permute-start(bf16[1024,128]{1,0:T(8,128)(2,1)} %get-tuple-element.66), channel_id=1, source_target_pairs={{4,0},{5,1},{6,2},{7,3},{8,4},{9,5},{10,6},{11,7},{12,8},{13,9},{1... | collective-permute-start | bytes 786440 | tf_op jit(solution)/shard_map/ppermute | solution.py:20
  117.8 1.9 %collective-permute-start.12 = (bf16[1024,128]{1,0:T(8,128)(2,1)}, bf16[1024,128]{1,0:T(8,128)(2,1)S(1)}, u32[]{:S(2)}, u32[]{:S(2)}) collective-permute-start(bf16[1024,128]{1,0:T(8,128)(2,1)} %get-tuple-element.64), channel_id=1, source_target_pairs={{4,0},{5,1},{6,2},{7,3},{8,4},{9,5},{10,6},{11,7},{12,8},{13,9},{1... | collective-permute-start | bytes 786440 | tf_op jit(solution)/shard_map/ppermute | solution.py:20
  119.8 0.8 copy-done.30
  120.7 1.9 %collective-permute-start.10 = (bf16[1024,128]{1,0:T(8,128)(2,1)S(1)}, bf16[1024,128]{1,0:T(8,128)(2,1)S(1)}, u32[]{:S(2)}, u32[]{:S(2)}) collective-permute-start(bf16[1024,128]{1,0:T(8,128)(2,1)S(1)} %copy-done.30), channel_id=1, source_target_pairs={{4,0},{5,1},{6,2},{7,3},{8,4},{9,5},{10,6},{11,7},{12,8},{13,9},{1... | collective-permute-start | bytes 786440 | tf_op jit(solution)/shard_map/ppermute | solution.py:20
  122.7 0.9 copy-done.29
  123.6 1.9 %collective-permute-start.32 = (bf16[1024,128]{1,0:T(8,128)(2,1)S(1)}, bf16[1024,128]{1,0:T(8,128)(2,1)S(1)}, u32[]{:S(2)}, u32[]{:S(2)}) collective-permute-start(bf16[1024,128]{1,0:T(8,128)(2,1)S(1)} %copy-done.29), channel_id=1, source_target_pairs={{4,0},{5,1},{6,2},{7,3},{8,4},{9,5},{10,6},{11,7},{12,8},{13,9},{1... | collective-permute-start | bytes 786440 | tf_op jit(solution)/shard_map/ppermute | solution.py:20
  125.6 2.4 %collective-permute-start.31 = (bf16[1024,128]{1,0:T(8,128)(2,1)S(1)}, bf16[1024,128]{1,0:T(8,128)(2,1)S(1)}, u32[]{:S(2)}, u32[]{:S(2)}) collective-permute-start(bf16[1024,128]{1,0:T(8,128)(2,1)S(1)} %add_convert_fusion), channel_id=1, source_target_pairs={{0,3},{1,2},{2,1},{3,0},{4,7},{5,6},{6,5},{7,4},{8,11},{9,10},{10,... | collective-permute-start | bytes 786440 | tf_op jit(solution)/shard_map/ppermute | solution.py:25
  128.0 3.0 %collective-permute-done.12 = bf16[1024,128]{1,0:T(8,128)(2,1)S(1)} collective-permute-done((bf16[1024,128]{1,0:T(8,128)(2,1)}, bf16[1024,128]{1,0:T(8,128)(2,1)S(1)}, u32[]{:S(2)}, u32[]{:S(2)}) %collective-permute-start.12) | collective-permute-done | bytes 262176 | tf_op jit(solution)/shard_map/ppermute | solution.py:20
  131.1 5.5 %collective-permute-done.10 = bf16[1024,128]{1,0:T(8,128)(2,1)S(1)} collective-permute-done((bf16[1024,128]{1,0:T(8,128)(2,1)S(1)}, bf16[1024,128]{1,0:T(8,128)(2,1)S(1)}, u32[]{:S(2)}, u32[]{:S(2)}) %collective-permute-start.10) | collective-permute-done | bytes 262176 | tf_op jit(solution)/shard_map/ppermute | solution.py:20
  136.7 2.1 %collective-permute-start.27 = (bf16[1024,128]{1,0:T(8,128)(2,1)S(1)}, bf16[1024,128]{1,0:T(8,128)(2,1)S(1)}, u32[]{:S(2)}, u32[]{:S(2)}) collective-permute-start(bf16[1024,128]{1,0:T(8,128)(2,1)S(1)} %add_convert_fusion.2), channel_id=1, source_target_pairs={{0,1},{1,0},{2,3},{3,2},{4,5},{5,4},{6,7},{7,6},{8,9},{9,8},{10,11... | collective-permute-start | bytes 786440 | tf_op jit(solution)/shard_map/ppermute | solution.py:25
  139.3 2.9 %collective-permute-done.32.refs_8_ = bf16[1024,128]{1,0:T(8,128)(2,1)S(1)} collective-permute-done((bf16[1024,128]{1,0:T(8,128)(2,1)S(1)}, bf16[1024,128]{1,0:T(8,128)(2,1)S(1)}, u32[]{:S(2)}, u32[]{:S(2)}) %collective-permute-start.32) | collective-permute-done | bytes 262176 | tf_op jit(solution)/shard_map/ppermute | solution.py:20
  142.3 1.7 %collective-permute-start.11 = (bf16[1024,128]{1,0:T(8,128)(2,1)S(1)}, bf16[1024,128]{1,0:T(8,128)(2,1)S(1)}, u32[]{:S(2)}, u32[]{:S(2)}) collective-permute-start(bf16[1024,128]{1,0:T(8,128)(2,1)S(1)} %add_convert_fusion.5), channel_id=1, source_target_pairs={{0,1},{1,0},{2,3},{3,2},{4,5},{5,4},{6,7},{7,6},{8,9},{9,8},{10,11... | collective-permute-start | bytes 786440 | tf_op jit(solution)/shard_map/ppermute | solution.py:25
  144.0 3.5 %collective-permute-done.15.refs_3_ = bf16[1024,128]{1,0:T(8,128)(2,1)S(1)} collective-permute-done((bf16[1024,128]{1,0:T(8,128)(2,1)S(1)}, bf16[1024,128]{1,0:T(8,128)(2,1)S(1)}, u32[]{:S(2)}, u32[]{:S(2)}) %collective-permute-start.15) | collective-permute-done | bytes 262176 | tf_op jit(solution)/shard_map/ppermute | solution.py:25
  147.5 4.5 %collective-permute-done.13.refs_2_ = bf16[1024,128]{1,0:T(8,128)(2,1)S(1)} collective-permute-done((bf16[1024,128]{1,0:T(8,128)(2,1)S(1)}, bf16[1024,128]{1,0:T(8,128)(2,1)S(1)}, u32[]{:S(2)}, u32[]{:S(2)}) %collective-permute-start.13) | collective-permute-done | bytes 262176 | tf_op jit(solution)/shard_map/ppermute | solution.py:25
  152.1 0.7 copy-done.27
  152.9 4.9 %finish.1 = (f32[2048,128]{1,0:T(8,128)}, f32[2048,128]{1,0:T(8,128)}, f32[2048,128]{1,0:T(8,128)}, f32[2048,128]{1,0:T(8,128)}) custom-call(s32[2]{0:T(128)} %pad_add_fusion.meta, f32[1024,128]{1,0:T(8,128)} %get-tuple-element.60.refs_0_, bf16[1024,128]{1,0:T(8,128)(2,1)} %copy-done.28, bf16[1024,128]{1,0:T(8,128)(2,1)} %copy-done.27, ...), custom_call_target="tpu_custom_call" | custom-call | tf_op jit(solution)/shard_map/finish/pallas_call | solution.py:261
  (98 shorter events, 3.1 us)
Async XLA Ops:
  6.7 6.1 %collective-permute-start.16 = (bf16[1040,128]{1,0:T(8,128)(2,1)}, bf16[1040,128]{1,0:T(8,128)(2,1)}, u32[]{:S(2)}, u32[]{:S(2)}) collective-permute-start(bf16[1040,128]{1,0:T(8,128)(2,1)} %get-tuple-element.68), channel_id=1, source_target_pairs={{0,1},{1,0},{2,3},{3,2},{4,5},{5,4},{6,7},{7,6},{8,9},{9,8},{10,11... | collective-permute-start | bytes 798728 | tf_op jit(solution)/shard_map/ppermute | solution.py:25
  7.3 8.2 %collective-permute-start.17 = (bf16[1040,128]{1,0:T(8,128)(2,1)}, bf16[1040,128]{1,0:T(8,128)(2,1)}, u32[]{:S(2)}, u32[]{:S(2)}) collective-permute-start(bf16[1040,128]{1,0:T(8,128)(2,1)} %get-tuple-element.69), channel_id=1, source_target_pairs={{0,2},{1,3},{2,0},{3,1},{4,6},{5,7},{6,4},{7,5},{8,10},{9,11},{10,... | collective-permute-start | bytes 798728 | tf_op jit(solution)/shard_map/ppermute | solution.py:25
  7.6 16.7 %collective-permute-start.18 = (bf16[1040,128]{1,0:T(8,128)(2,1)}, bf16[1040,128]{1,0:T(8,128)(2,1)}, u32[]{:S(2)}, u32[]{:S(2)}) collective-permute-start(bf16[1040,128]{1,0:T(8,128)(2,1)} %get-tuple-element.70), channel_id=1, source_target_pairs={{0,3},{1,2},{2,1},{3,0},{4,7},{5,6},{6,5},{7,4},{8,11},{9,10},{10,... | collective-permute-start | bytes 798728 | tf_op jit(solution)/shard_map/ppermute | solution.py:25
  9.0 15.3 %collective-permute-start.19 = (bf16[1040,128]{1,0:T(8,128)(2,1)}, bf16[1040,128]{1,0:T(8,128)(2,1)S(1)}, u32[]{:S(2)}, u32[]{:S(2)}) collective-permute-start(bf16[1040,128]{1,0:T(8,128)(2,1)} %get-tuple-element.67.refs_0_), channel_id=1, source_target_pairs={{0,4},{1,5},{2,6},{3,7},{4,8},{5,9},{6,10},{7,11},{8,12},{9,13},{1... | collective-permute-start | bytes 798728 | tf_op jit(solution)/shard_map/ppermute | solution.py:20
  12.2 13.4 %collective-permute-start = (bf16[1040,128]{1,0:T(8,128)(2,1)}, bf16[1040,128]{1,0:T(8,128)(2,1)S(1)}, u32[]{:S(2)}, u32[]{:S(2)}) collective-permute-start(bf16[1040,128]{1,0:T(8,128)(2,1)} %get-tuple-element.53), channel_id=1, source_target_pairs={{0,1},{1,0},{2,3},{3,2},{4,5},{5,4},{6,7},{7,6},{8,9},{9,8},{10,11... | collective-permute-start | bytes 798728 | tf_op jit(solution)/shard_map/ppermute | solution.py:25
  12.7 14.1 %collective-permute-start.1 = (bf16[1040,128]{1,0:T(8,128)(2,1)}, bf16[1040,128]{1,0:T(8,128)(2,1)S(1)}, u32[]{:S(2)}, u32[]{:S(2)}) collective-permute-start(bf16[1040,128]{1,0:T(8,128)(2,1)} %get-tuple-element.54), channel_id=1, source_target_pairs={{0,2},{1,3},{2,0},{3,1},{4,6},{5,7},{6,4},{7,5},{8,10},{9,11},{10,... | collective-permute-start | bytes 798728 | tf_op jit(solution)/shard_map/ppermute | solution.py:25
  15.6 11.3 %copy-start.12 = (bf16[1040,128]{1,0:T(8,128)(2,1)S(1)}, bf16[1040,128]{1,0:T(8,128)(2,1)}, u32[]{:S(2)}) copy-start(bf16[1040,128]{1,0:T(8,128)(2,1)} %get-tuple-element.52.refs_0_) | copy-start | bytes 798724
  15.6 18.0 %collective-permute-start.2 = (bf16[1040,128]{1,0:T(8,128)(2,1)}, bf16[1040,128]{1,0:T(8,128)(2,1)S(1)}, u32[]{:S(2)}, u32[]{:S(2)}) collective-permute-start(bf16[1040,128]{1,0:T(8,128)(2,1)} %get-tuple-element.55), channel_id=1, source_target_pairs={{0,3},{1,2},{2,1},{3,0},{4,7},{5,6},{6,5},{7,4},{8,11},{9,10},{10,... | collective-permute-start | bytes 798728 | tf_op jit(solution)/shard_map/ppermute | solution.py:25
  24.2 13.1 %collective-permute-start.23 = (bf16[1536,128]{1,0:T(8,128)(2,1)}, bf16[1536,128]{1,0:T(8,128)(2,1)S(1)}, u32[]{:S(2)}, u32[]{:S(2)}) collective-permute-start(bf16[1536,128]{1,0:T(8,128)(2,1)} %get-tuple-element.72), channel_id=1, source_target_pairs={{0,1},{1,0},{2,3},{3,2},{4,5},{5,4},{6,7},{7,6},{8,9},{9,8},{10,11... | collective-permute-start | bytes 1179656 | tf_op jit(solution)/shard_map/ppermute | solution.py:25
  24.3 9.3 %copy-start.16 = (bf16[1040,128]{1,0:T(8,128)(2,1)}, bf16[1040,128]{1,0:T(8,128)(2,1)S(1)}, u32[]{:S(2)}) copy-start(bf16[1040,128]{1,0:T(8,128)(2,1)S(1)} %collective-permute-done.19.refs_4_) | copy-start | bytes 798724
  24.3 16.7 %collective-permute-start.24 = (bf16[1536,128]{1,0:T(8,128)(2,1)}, bf16[1536,128]{1,0:T(8,128)(2,1)S(1)}, u32[]{:S(2)}, u32[]{:S(2)}) collective-permute-start(bf16[1536,128]{1,0:T(8,128)(2,1)} %get-tuple-element.73), channel_id=1, source_target_pairs={{0,2},{1,3},{2,0},{3,1},{4,6},{5,7},{6,4},{7,5},{8,10},{9,11},{10,... | collective-permute-start | bytes 1179656 | tf_op jit(solution)/shard_map/ppermute | solution.py:25
  25.6 60.7 %copy-start.13 = (bf16[1040,128]{1,0:T(8,128)(2,1)}, bf16[1040,128]{1,0:T(8,128)(2,1)S(1)}, u32[]{:S(2)}) copy-start(bf16[1040,128]{1,0:T(8,128)(2,1)S(1)} %collective-permute-done.refs_1_) | copy-start | bytes 798724
  25.6 24.8 %collective-permute-start.25 = (bf16[1536,128]{1,0:T(8,128)(2,1)}, bf16[1536,128]{1,0:T(8,128)(2,1)S(1)}, u32[]{:S(2)}, u32[]{:S(2)}) collective-permute-start(bf16[1536,128]{1,0:T(8,128)(2,1)} %get-tuple-element.74), channel_id=1, source_target_pairs={{0,3},{1,2},{2,1},{3,0},{4,7},{5,6},{6,5},{7,4},{8,11},{9,10},{10,... | collective-permute-start | bytes 1179656 | tf_op jit(solution)/shard_map/ppermute | solution.py:25
  26.9 59.4 %copy-start.14 = (bf16[1040,128]{1,0:T(8,128)(2,1)}, bf16[1040,128]{1,0:T(8,128)(2,1)S(1)}, u32[]{:S(2)}) copy-start(bf16[1040,128]{1,0:T(8,128)(2,1)S(1)} %collective-permute-done.1.refs_2_) | copy-start | bytes 798724
  26.9 8.4 %collective-permute-start.3 = (bf16[1040,128]{1,0:T(8,128)(2,1)S(1)}, bf16[1040,128]{1,0:T(8,128)(2,1)S(1)}, u32[]{:S(2)}, u32[]{:S(2)}) collective-permute-start(bf16[1040,128]{1,0:T(8,128)(2,1)S(1)} %copy-done.12), channel_id=1, source_target_pairs={{0,4},{1,5},{2,6},{3,7},{4,8},{5,9},{6,10},{7,11},{8,12},{9,13},{1... | collective-permute-start | bytes 798728 | tf_op jit(solution)/shard_map/ppermute | solution.py:20
  33.6 52.7 %copy-start.15 = (bf16[1040,128]{1,0:T(8,128)(2,1)}, bf16[1040,128]{1,0:T(8,128)(2,1)S(1)}, u32[]{:S(2)}) copy-start(bf16[1040,128]{1,0:T(8,128)(2,1)S(1)} %collective-permute-done.2.refs_3_) | copy-start | bytes 798724
  33.6 20.1 %collective-permute-start.7 = (bf16[1536,128]{1,0:T(8,128)(2,1)}, bf16[1536,128]{1,0:T(8,128)(2,1)S(1)}, u32[]{:S(2)}, u32[]{:S(2)}) collective-permute-start(bf16[1536,128]{1,0:T(8,128)(2,1)} %get-tuple-element.57), channel_id=1, source_target_pairs={{0,1},{1,0},{2,3},{3,2},{4,5},{5,4},{6,7},{7,6},{8,9},{9,8},{10,11... | collective-permute-start | bytes 1179656 | tf_op jit(solution)/shard_map/ppermute | solution.py:25
  36.0 50.3 %collective-permute-start.8 = (bf16[1536,128]{1,0:T(8,128)(2,1)}, bf16[1536,128]{1,0:T(8,128)(2,1)S(1)}, u32[]{:S(2)}, u32[]{:S(2)}) collective-permute-start(bf16[1536,128]{1,0:T(8,128)(2,1)} %get-tuple-element.58), channel_id=1, source_target_pairs={{0,2},{1,3},{2,0},{3,1},{4,6},{5,7},{6,4},{7,5},{8,10},{9,11},{10,... | collective-permute-start | bytes 1179656 | tf_op jit(solution)/shard_map/ppermute | solution.py:25
  37.3 27.5 %copy-start.8 = (bf16[1536,128]{1,0:T(8,128)(2,1)}, bf16[1536,128]{1,0:T(8,128)(2,1)S(1)}, u32[]{:S(2)}) copy-start(bf16[1536,128]{1,0:T(8,128)(2,1)S(1)} %collective-permute-done.23.refs_9_) | copy-start | bytes 1179652
  37.3 16.4 %collective-permute-start.20 = (bf16[1040,128]{1,0:T(8,128)(2,1)}, bf16[1040,128]{1,0:T(8,128)(2,1)}, u32[]{:S(2)}, u32[]{:S(2)}) collective-permute-start(bf16[1040,128]{1,0:T(8,128)(2,1)} %collective-permute-done.16.refs_1_), channel_id=1, source_target_pairs={{0,4},{1,5},{2,6},{3,7},{4,8},{5,9},{6,10},{7,11},{8,12},{9,13},{1... | collective-permute-start | bytes 798728 | tf_op jit(solution)/shard_map/ppermute | solution.py:20
  41.0 23.8 %copy-start.9 = (bf16[1536,128]{1,0:T(8,128)(2,1)}, bf16[1536,128]{1,0:T(8,128)(2,1)S(1)}, u32[]{:S(2)}) copy-start(bf16[1536,128]{1,0:T(8,128)(2,1)S(1)} %collective-permute-done.24.refs_10_) | copy-start | bytes 1179652
  41.0 14.7 %collective-permute-start.21 = (bf16[1040,128]{1,0:T(8,128)(2,1)}, bf16[1040,128]{1,0:T(8,128)(2,1)S(1)}, u32[]{:S(2)}, u32[]{:S(2)}) collective-permute-start(bf16[1040,128]{1,0:T(8,128)(2,1)} %collective-permute-done.17.refs_2_), channel_id=1, source_target_pairs={{0,4},{1,5},{2,6},{3,7},{4,8},{5,9},{6,10},{7,11},{8,12},{9,13},{1... | collective-permute-start | bytes 798728 | tf_op jit(solution)/shard_map/ppermute | solution.py:20
  50.4 14.4 %copy-start.10 = (bf16[1536,128]{1,0:T(8,128)(2,1)}, bf16[1536,128]{1,0:T(8,128)(2,1)S(1)}, u32[]{:S(2)}) copy-start(bf16[1536,128]{1,0:T(8,128)(2,1)S(1)} %collective-permute-done.25.refs_11_) | copy-start | bytes 1179652
  50.4 10.5 %collective-permute-start.22 = (bf16[1040,128]{1,0:T(8,128)(2,1)}, bf16[1040,128]{1,0:T(8,128)(2,1)S(1)}, u32[]{:S(2)}, u32[]{:S(2)}) collective-permute-start(bf16[1040,128]{1,0:T(8,128)(2,1)} %collective-permute-done.18.refs_3_), channel_id=1, source_target_pairs={{0,4},{1,5},{2,6},{3,7},{4,8},{5,9},{6,10},{7,11},{8,12},{9,13},{1... | collective-permute-start | bytes 798728 | tf_op jit(solution)/shard_map/ppermute | solution.py:20
  53.6 32.7 %copy-start.6 = (bf16[1536,128]{1,0:T(8,128)(2,1)}, bf16[1536,128]{1,0:T(8,128)(2,1)S(1)}, u32[]{:S(2)}) copy-start(bf16[1536,128]{1,0:T(8,128)(2,1)S(1)} %collective-permute-done.7.refs_9_) | copy-start | bytes 1179652
  53.6 34.6 %collective-permute-start.9 = (bf16[1536,128]{1,0:T(8,128)(2,1)}, bf16[1536,128]{1,0:T(8,128)(2,1)S(1)}, u32[]{:S(2)}, u32[]{:S(2)}) collective-permute-start(bf16[1536,128]{1,0:T(8,128)(2,1)} %get-tuple-element.59), channel_id=1, source_target_pairs={{0,3},{1,2},{2,1},{3,0},{4,7},{5,6},{6,5},{7,4},{8,11},{9,10},{10,... | collective-permute-start | bytes 1179656 | tf_op jit(solution)/shard_map/ppermute | solution.py:25
  53.7 36.5 %collective-permute-start.4 = (bf16[1040,128]{1,0:T(8,128)(2,1)S(1)}, bf16[1040,128]{1,0:T(8,128)(2,1)S(1)}, u32[]{:S(2)}, u32[]{:S(2)}) collective-permute-start(bf16[1040,128]{1,0:T(8,128)(2,1)S(1)} %collective-permute-done.refs_1_), channel_id=1, source_target_pairs={{0,4},{1,5},{2,6},{3,7},{4,8},{5,9},{6,10},{7,11},{8,12},{9,13},{1... | collective-permute-start | bytes 798728 | tf_op jit(solution)/shard_map/ppermute | solution.py:20
  55.7 36.5 %collective-permute-start.5 = (bf16[1040,128]{1,0:T(8,128)(2,1)S(1)}, bf16[1040,128]{1,0:T(8,128)(2,1)}, u32[]{:S(2)}, u32[]{:S(2)}) collective-permute-start(bf16[1040,128]{1,0:T(8,128)(2,1)S(1)} %collective-permute-done.1.refs_2_), channel_id=1, source_target_pairs={{0,4},{1,5},{2,6},{3,7},{4,8},{5,9},{6,10},{7,11},{8,12},{9,13},{1... | collective-permute-start | bytes 798728 | tf_op jit(solution)/shard_map/ppermute | solution.py:20
  61.6 32.7 %collective-permute-start.6 = (bf16[1040,128]{1,0:T(8,128)(2,1)S(1)}, bf16[1040,128]{1,0:T(8,128)(2,1)}, u32[]{:S(2)}, u32[]{:S(2)}) collective-permute-start(bf16[1040,128]{1,0:T(8,128)(2,1)S(1)} %collective-permute-done.2.refs_3_), channel_id=1, source_target_pairs={{0,4},{1,5},{2,6},{3,7},{4,8},{5,9},{6,10},{7,11},{8,12},{9,13},{1... | collective-permute-start | bytes 798728 | tf_op jit(solution)/shard_map/ppermute | solution.py:20
  86.4 31.4 %collective-permute-start.30 = (bf16[1024,128]{1,0:T(8,128)(2,1)}, bf16[1024,128]{1,0:T(8,128)(2,1)S(1)}, u32[]{:S(2)}, u32[]{:S(2)}) collective-permute-start(bf16[1024,128]{1,0:T(8,128)(2,1)} %get-tuple-element.81), channel_id=1, source_target_pairs={{4,0},{5,1},{6,2},{7,3},{8,4},{9,5},{10,6},{11,7},{12,8},{13,9},{1... | collective-permute-start | bytes 786440 | tf_op jit(solution)/shard_map/ppermute | solution.py:20
  88.3 31.5 %collective-permute-start.28 = (bf16[1024,128]{1,0:T(8,128)(2,1)}, bf16[1024,128]{1,0:T(8,128)(2,1)S(1)}, u32[]{:S(2)}, u32[]{:S(2)}) collective-permute-start(bf16[1024,128]{1,0:T(8,128)(2,1)} %get-tuple-element.79), channel_id=1, source_target_pairs={{4,0},{5,1},{6,2},{7,3},{8,4},{9,5},{10,6},{11,7},{12,8},{13,9},{1... | collective-permute-start | bytes 786440 | tf_op jit(solution)/shard_map/ppermute | solution.py:20
  90.3 32.5 %collective-permute-start.26 = (bf16[1024,128]{1,0:T(8,128)(2,1)}, bf16[1024,128]{1,0:T(8,128)(2,1)S(1)}, u32[]{:S(2)}, u32[]{:S(2)}) collective-permute-start(bf16[1024,128]{1,0:T(8,128)(2,1)} %get-tuple-element.77), channel_id=1, source_target_pairs={{4,0},{5,1},{6,2},{7,3},{8,4},{9,5},{10,6},{11,7},{12,8},{13,9},{1... | collective-permute-start | bytes 786440 | tf_op jit(solution)/shard_map/ppermute | solution.py:20
  92.2 46.7 %collective-permute-start.33 = (bf16[1024,128]{1,0:T(8,128)(2,1)}, bf16[1024,128]{1,0:T(8,128)(2,1)S(1)}, u32[]{:S(2)}, u32[]{:S(2)}) collective-permute-start(bf16[1024,128]{1,0:T(8,128)(2,1)} %get-tuple-element.83), channel_id=1, source_target_pairs={{4,0},{5,1},{6,2},{7,3},{8,4},{9,5},{10,6},{11,7},{12,8},{13,9},{1... | collective-permute-start | bytes 786440 | tf_op jit(solution)/shard_map/ppermute | solution.py:20
  94.3 25.4 %copy-start.2 = (f32[1024,128]{1,0:T(8,128)S(1)}, f32[1024,128]{1,0:T(8,128)}, u32[]{:S(2)}) copy-start(f32[1024,128]{1,0:T(8,128)} %get-tuple-element.80) | copy-start | bytes 1572868
  115.9 9.7 %collective-permute-start.14 = (bf16[1024,128]{1,0:T(8,128)(2,1)}, bf16[1024,128]{1,0:T(8,128)(2,1)S(1)}, u32[]{:S(2)}, u32[]{:S(2)}) collective-permute-start(bf16[1024,128]{1,0:T(8,128)(2,1)} %get-tuple-element.66), channel_id=1, source_target_pairs={{4,0},{5,1},{6,2},{7,3},{8,4},{9,5},{10,6},{11,7},{12,8},{13,9},{1... | collective-permute-start | bytes 786440 | tf_op jit(solution)/shard_map/ppermute | solution.py:20
  117.8 13.2 %collective-permute-start.12 = (bf16[1024,128]{1,0:T(8,128)(2,1)}, bf16[1024,128]{1,0:T(8,128)(2,1)S(1)}, u32[]{:S(2)}, u32[]{:S(2)}) collective-permute-start(bf16[1024,128]{1,0:T(8,128)(2,1)} %get-tuple-element.64), channel_id=1, source_target_pairs={{4,0},{5,1},{6,2},{7,3},{8,4},{9,5},{10,6},{11,7},{12,8},{13,9},{1... | collective-permute-start | bytes 786440 | tf_op jit(solution)/shard_map/ppermute | solution.py:20
  120.7 16.0 %collective-permute-start.10 = (bf16[1024,128]{1,0:T(8,128)(2,1)S(1)}, bf16[1024,128]{1,0:T(8,128)(2,1)S(1)}, u32[]{:S(2)}, u32[]{:S(2)}) collective-permute-start(bf16[1024,128]{1,0:T(8,128)(2,1)S(1)} %copy-done.30), channel_id=1, source_target_pairs={{4,0},{5,1},{6,2},{7,3},{8,4},{9,5},{10,6},{11,7},{12,8},{13,9},{1... | collective-permute-start | bytes 786440 | tf_op jit(solution)/shard_map/ppermute | solution.py:20
  123.6 18.7 %collective-permute-start.32 = (bf16[1024,128]{1,0:T(8,128)(2,1)S(1)}, bf16[1024,128]{1,0:T(8,128)(2,1)S(1)}, u32[]{:S(2)}, u32[]{:S(2)}) collective-permute-start(bf16[1024,128]{1,0:T(8,128)(2,1)S(1)} %copy-done.29), channel_id=1, source_target_pairs={{4,0},{5,1},{6,2},{7,3},{8,4},{9,5},{10,6},{11,7},{12,8},{13,9},{1... | collective-permute-start | bytes 786440 | tf_op jit(solution)/shard_map/ppermute | solution.py:20
  125.6 16.7 %collective-permute-start.31 = (bf16[1024,128]{1,0:T(8,128)(2,1)S(1)}, bf16[1024,128]{1,0:T(8,128)(2,1)S(1)}, u32[]{:S(2)}, u32[]{:S(2)}) collective-permute-start(bf16[1024,128]{1,0:T(8,128)(2,1)S(1)} %add_convert_fusion), channel_id=1, source_target_pairs={{0,3},{1,2},{2,1},{3,0},{4,7},{5,6},{6,5},{7,4},{8,11},{9,10},{10,... | collective-permute-start | bytes 786440 | tf_op jit(solution)/shard_map/ppermute | solution.py:25
  131.0 13.0 %collective-permute-start.29 = (bf16[1024,128]{1,0:T(8,128)(2,1)S(1)}, bf16[1024,128]{1,0:T(8,128)(2,1)S(1)}, u32[]{:S(2)}, u32[]{:S(2)}) collective-permute-start(bf16[1024,128]{1,0:T(8,128)(2,1)S(1)} %add_convert_fusion.1), channel_id=1, source_target_pairs={{0,2},{1,3},{2,0},{3,1},{4,6},{5,7},{6,4},{7,5},{8,10},{9,11},{10,... | collective-permute-start | bytes 786440 | tf_op jit(solution)/shard_map/ppermute | solution.py:25
  136.7 7.4 %collective-permute-start.27 = (bf16[1024,128]{1,0:T(8,128)(2,1)S(1)}, bf16[1024,128]{1,0:T(8,128)(2,1)S(1)}, u32[]{:S(2)}, u32[]{:S(2)}) collective-permute-start(bf16[1024,128]{1,0:T(8,128)(2,1)S(1)} %add_convert_fusion.2), channel_id=1, source_target_pairs={{0,1},{1,0},{2,3},{3,2},{4,5},{5,4},{6,7},{7,6},{8,9},{9,8},{10,11... | collective-permute-start | bytes 786440 | tf_op jit(solution)/shard_map/ppermute | solution.py:25
  138.9 13.2 %copy-start.21 = (bf16[1024,128]{1,0:T(8,128)(2,1)}, bf16[1024,128]{1,0:T(8,128)(2,1)S(1)}, u32[]{:S(2)}) copy-start(bf16[1024,128]{1,0:T(8,128)(2,1)S(1)} %collective-permute-done.33.refs_9_) | copy-start | bytes 786436
  138.9 8.7 %collective-permute-start.15 = (bf16[1024,128]{1,0:T(8,128)(2,1)S(1)}, bf16[1024,128]{1,0:T(8,128)(2,1)S(1)}, u32[]{:S(2)}, u32[]{:S(2)}) collective-permute-start(bf16[1024,128]{1,0:T(8,128)(2,1)S(1)} %add_convert_fusion.3), channel_id=1, source_target_pairs={{0,3},{1,2},{2,1},{3,0},{4,7},{5,6},{6,5},{7,4},{8,11},{9,10},{10,... | collective-permute-start | bytes 786440 | tf_op jit(solution)/shard_map/ppermute | solution.py:25
  142.3 9.8 %copy-start.22 = (bf16[1024,128]{1,0:T(8,128)(2,1)}, bf16[1024,128]{1,0:T(8,128)(2,1)S(1)}, u32[]{:S(2)}) copy-start(bf16[1024,128]{1,0:T(8,128)(2,1)S(1)} %collective-permute-done.32.refs_8_) | copy-start | bytes 786436
  142.3 9.8 %collective-permute-start.13 = (bf16[1024,128]{1,0:T(8,128)(2,1)S(1)}, bf16[1024,128]{1,0:T(8,128)(2,1)S(1)}, u32[]{:S(2)}, u32[]{:S(2)}) collective-permute-start(bf16[1024,128]{1,0:T(8,128)(2,1)S(1)} %add_convert_fusion.4), channel_id=1, source_target_pairs={{0,2},{1,3},{2,0},{3,1},{4,6},{5,7},{6,4},{7,5},{8,10},{9,11},{10,... | collective-permute-start | bytes 786440 | tf_op jit(solution)/shard_map/ppermute | solution.py:25
  142.3 9.8 %copy-start.23 = (bf16[1024,128]{1,0:T(8,128)(2,1)}, bf16[1024,128]{1,0:T(8,128)(2,1)S(1)}, u32[]{:S(2)}) copy-start(bf16[1024,128]{1,0:T(8,128)(2,1)S(1)} %collective-permute-done.31.refs_7_) | copy-start | bytes 786436
  142.3 9.8 %collective-permute-start.11 = (bf16[1024,128]{1,0:T(8,128)(2,1)S(1)}, bf16[1024,128]{1,0:T(8,128)(2,1)S(1)}, u32[]{:S(2)}, u32[]{:S(2)}) collective-permute-start(bf16[1024,128]{1,0:T(8,128)(2,1)S(1)} %add_convert_fusion.5), channel_id=1, source_target_pairs={{0,1},{1,0},{2,3},{3,2},{4,5},{5,4},{6,7},{7,6},{8,9},{9,8},{10,11... | collective-permute-start | bytes 786440 | tf_op jit(solution)/shard_map/ppermute | solution.py:25
  144.0 8.1 %copy-start.25 = (bf16[1024,128]{1,0:T(8,128)(2,1)}, bf16[1024,128]{1,0:T(8,128)(2,1)S(1)}, u32[]{:S(2)}) copy-start(bf16[1024,128]{1,0:T(8,128)(2,1)S(1)} %collective-permute-done.27.refs_5_) | copy-start | bytes 786436
  (18 other events, 57.2 us)

commit v2 on v1

--- a/solution.py
+++ b/solution.py
@@ -7,6 +7,7 @@
 from jax.experimental.pallas import tpu as pltpu
 from jax.sharding import PartitionSpec as P
 
+
 WINDOW_LENGTH = 1024
 HIDDEN = -1e30
 TAIL = 16
@@ -25,13 +26,11 @@
     return lax.ppermute(block, "ctx", [(i, i ^ partner) for i in devices])
 
 
-def pack_kernel(plane, heads, group, meta, *refs):
-    seg = refs[-1 - plane * heads - 1] if group == 1 else None
-    arrays = refs[: len(refs) - 1 - plane * heads - (group == 1)]
-    outs = refs[-1 - plane * heads : -1]
-    wide = refs[-1]
-    me = meta[0]
-    for t, array in enumerate(arrays):
+def pack_kernel(plane, heads, group, arrays, *refs):
+    seg = refs[arrays] if group == 1 else None
+    outs, wide = refs[-1 - plane * heads : -1], refs[-1]
+    me = lax.rem(lax.axis_index("ctx"), plane)
+    for t, array in enumerate(refs[:arrays]):
         rows, count, width = array.shape
         wide[...] = array[...].astype(F32).reshape(rows * count, width)
         for h in range(heads):
@@ -43,30 +42,36 @@
                         pl.ds(first + g, rows, stride=count), :
                     ].astype(BF16)
     if group == 1:
+        docs = seg[...].astype(F32)
+        filler = jnp.zeros((TAIL - docs.shape[0], docs.shape[1]), F32)
+        tail = jnp.concatenate([docs, filler], axis=0).astype(BF16)
         for out in outs:
-            out[len(arrays) * rows :, :] = seg[...]
-
-
-def pack(meta, arrays, plane, heads, group, seg=None):
+            out[arrays * rows :, :] = tail
+
+
+def pack(arrays, plane, heads, group, seg=None):
     rows, count, width = arrays[0].shape
     length = len(arrays) * group * rows + (0 if seg is None else TAIL)
     vmem = pl.BlockSpec(memory_space=pltpu.VMEM)
     inputs = list(arrays) + ([] if seg is None else [seg])
     return pl.pallas_call(
-        functools.partial(pack_kernel, plane, heads, group),
+        functools.partial(pack_kernel, plane, heads, group, len(arrays)),
         out_shape=[jax.ShapeDtypeStruct((length, width), BF16)] * (plane * heads),
-        in_specs=[pl.BlockSpec(memory_space=pltpu.SMEM)] + [vmem] * len(inputs),
+        in_specs=[vmem] * len(inputs),
         out_specs=[vmem] * (plane * heads),
         scratch_shapes=[pltpu.VMEM((rows * count, width), F32)],
         name="pack",
-    )(meta, *inputs)
-
-
-def attend_kernel(plane, group, rows, width, meta, *refs):
-    own, prev, queries = refs[:plane], refs[plane : 2 * plane], refs[2 * plane : 3 * plane]
-    out_prev, out_own = refs[3 * plane : 4 * plane], refs[4 * plane : 5 * plane]
-    ka, kd, vv, segs, qq, do, qt, qa, dt, s, sd, u, ud, acc, tri, lims, sem = refs[5 * plane :]
-    me, valid = meta[0], meta[1]
+    )(*inputs)
+
+
+def attend_kernel(plane, group, rows, width, *refs):
+    half = plane // 2
+    length = 4 * rows + TAIL
+    own, pairs, queries = refs[:plane], refs[plane : plane + 2], refs[plane + 2 : 2 * plane + 2]
+    out_prev, out_own = refs[2 * plane + 2 : 2 * plane + 4], refs[2 * plane + 4 : 3 * plane + 4]
+    ka, kd, vv, segs, qq, do, qt, qa, dt, s, sd, u, ud, acc, tri, lims, sem = refs[3 * plane + 4 :]
+    device = lax.axis_index("ctx")
+    me = lax.rem(device, plane)
     span = group * rows
     factor = width ** (-0.5)
     slope = factor * 1.4426950408889634
@@ -80,15 +85,15 @@
 
     low, high = pl.ds(0, width), pl.ds(width, width)
     for k in range(plane):
-        for piece, base in ((own[k], plane), (prev[k], 0)):
+        for piece, start, base in ((own[k], 0, plane), (pairs[k // half], k % half * length, 0)):
             block = base + (me ^ k)
-            part = [piece.at[pl.ds(t * rows, rows), :] for t in range(4)]
+            part = [piece.at[pl.ds(start + t * rows, rows), :] for t in range(4)]
             fetch(part[0], ka.at[block, :, low])
             fetch(part[0], kd.at[block, :, high])
             fetch(part[1], vv.at[block, 0])
             fetch(part[2], kd.at[block, :, low])
             fetch(part[3], vv.at[block, 1])
-            fetch(piece.at[pl.ds(4 * rows, TAIL), :], segs.at[block])
+            fetch(piece.at[pl.ds(start + 4 * rows, TAIL), :], segs.at[block])
         block = me ^ k
         part = [queries[k].at[pl.ds(t * span, span), :] for t in range(3)]
         fetch(part[0], qq.at[block, :, low])
@@ -117,7 +122,7 @@
         ka[block, :, width:] = hot.T.astype(BF16)
         last = jnp.max(docs)
         lims[0, block] = jnp.min(docs)
-        lims[1, block] = jnp.where(valid > 0, last, -1.0) if block < plane else last
+        lims[1, block] = jnp.where(device >= plane, last, -1.0) if block < plane else last
 
     def folded(values):
         return values.reshape(rows // 8, 8, span)
@@ -198,11 +203,12 @@
         for t in range(4):
             scale = factor if t % 2 == 0 else 1.0
             at = slice(t * rows, (t + 1) * rows)
-            out_prev[k][at, :] = (scale * acc[me ^ k, t]).astype(BF16)
+            there = slice((k % half * 4 + t) * rows, (k % half * 4 + t + 1) * rows)
+            out_prev[k // half][there, :] = (scale * acc[me ^ k, t]).astype(BF16)
             out_own[k][at, :] = scale * acc[plane + (me ^ k), t]
 
 
-def attend(meta, own, prev, queries, plane, group):
+def attend(own, pairs, queries, plane, group):
     length, width = own[0].shape
     rows = (length - TAIL) // 4
     span = group * rows
@@ -210,11 +216,10 @@
     blocks = 2 * plane
     results = pl.pallas_call(
         functools.partial(attend_kernel, plane, group, rows, width),
-        out_shape=[jax.ShapeDtypeStruct((4 * rows, width), BF16)] * plane
+        out_shape=[jax.ShapeDtypeStruct((2 * plane * rows, width), BF16)] * 2
         + [jax.ShapeDtypeStruct((4 * rows, width), F32)] * plane,
-        in_specs=[pl.BlockSpec(memory_space=pltpu.SMEM)]
-        + [pl.BlockSpec(memory_space=pl.ANY)] * (3 * plane),
-        out_specs=[vmem] * (2 * plane),
+        in_specs=[pl.BlockSpec(memory_space=pl.ANY)] * (2 * plane + 2),
+        out_specs=[vmem] * (plane + 2),
         scratch_shapes=[
             pltpu.VMEM((blocks, rows, 2 * width), BF16),
             pltpu.VMEM((blocks, rows, 2 * width), BF16),
@@ -234,14 +239,14 @@
             pltpu.SemaphoreType.DMA((15 * plane,)),
         ],
         name="attend",
-    )(meta, *own, *prev, *queries)
-    return results[:plane], results[plane:]
-
-
-def finish_kernel(plane, heads, meta, *refs):
+    )(*own, *pairs, *queries)
+    return results[:2], results[2:]
+
+
+def finish_kernel(plane, heads, *refs):
     pieces, returned = refs[: plane * heads], refs[plane * heads : plane * heads + heads]
     outs = refs[-4:]
-    me = meta[0]
+    me = lax.rem(lax.axis_index("ctx"), plane)
     for h in range(heads):
         for k in range(plane):
             piece = pieces[h * plane + k]
@@ -255,16 +260,16 @@
                 outs[t][pl.ds(head, rows, stride=plane * heads), :] = value
 
 
-def finish(meta, pieces, returned, plane, heads):
+def finish(pieces, returned, plane, heads):
     length, width = pieces[0].shape
     vmem = pl.BlockSpec(memory_space=pltpu.VMEM)
     return pl.pallas_call(
         functools.partial(finish_kernel, plane, heads),
         out_shape=[jax.ShapeDtypeStruct((length // 4 * plane * heads, width), F32)] * 4,
-        in_specs=[pl.BlockSpec(memory_space=pltpu.SMEM)] + [vmem] * (plane * heads + heads),
+        in_specs=[vmem] * (plane * heads + heads),
         out_specs=[vmem] * 4,
         name="finish",
-    )(meta, *pieces, *returned)
+    )(*pieces, *returned)
 
 
 def local(
@@ -273,26 +278,40 @@
     rows, kv_heads, width = keys.shape
     group = query.shape[1] // kv_heads
     plane = WINDOW_LENGTH // rows
+    half = plane // 2
     heads = kv_heads // plane
-    device = lax.axis_index("ctx")
-    meta = jnp.stack([device % plane, device // plane]).astype(jnp.int32)
-    seg = jnp.zeros((TAIL, width), BF16)
-    seg = seg.at[: rows // width].set(segment_ids.reshape(rows // width, width).astype(BF16))
-    kv = pack(meta, (keys, values, key_direction, value_direction), plane, heads, 1, seg)
-    qs = pack(meta, (query, query_tangent, out_cotangent), plane, heads, group)
-
+    far_first = list(range(half, plane)) + list(range(1, half))
+
+    def spread(blocks, h):
+        results = [blocks[h * plane]] + [None] * (plane - 1)
+        for k in far_first:
+            results[k] = swapped(blocks[h * plane + k], k)
+        return results
+
+    seg = segment_ids.reshape(rows // width, width)
+    kv = pack((keys, values, key_direction, value_direction), plane, heads, 1, seg)
+    qs = pack((query, query_tangent, out_cotangent), plane, heads, group)
     pieces, returned = [], []
     for h in range(heads):
-        own = [kv[h * plane]] + [swapped(kv[h * plane + k], k) for k in range(1, plane)]
-        prev = [shifted(own[k], plane) for k in range(plane)]
-        queries = [qs[h * plane]] + [swapped(qs[h * plane + k], k) for k in range(1, plane)]
-        sums_prev, sums_own = attend(meta, own, prev, queries, plane, group)
-        back = [shifted(sums_prev[k], -plane) for k in range(plane)]
+        own = spread(kv, h)
+        pairs = []
+        for part in (own[:half], own[half:]):
+            pairs.append(shifted(jnp.concatenate(part, axis=0), plane))
+        queries = spread(qs, h)
+        sums_prev, sums_own = attend(own, pairs, queries, plane, group)
+        back = [None, None]
+        for i in (1, 0):
+            back[i] = shifted(sums_prev[i], -plane)
         returned.append(back[0])
-        pieces.append(sums_own[0])
+        totals = [sums_own[0]]
         for k in range(1, plane):
-            pieces.append(swapped((sums_own[k] + back[k].astype(F32)).astype(BF16), k))
-    outs = finish(meta, pieces, returned, plane, heads)
+            at = slice(k % half * 4 * rows, (k % half + 1) * 4 * rows)
+            totals.append((sums_own[k] + back[k // half][at].astype(F32)).astype(BF16))
+        results = [totals[0]] + [None] * (plane - 1)
+        for k in far_first:
+            results[k] = swapped(totals[k], k)
+        pieces.extend(results)
+    outs = finish(pieces, returned, plane, heads)
     return tuple(out.reshape(rows, kv_heads, width) for out in outs)
 
 

time: 159 us -> 168 us (1.057)
  the two profiles are of different devices: /device:TPU:21 before, /device:TPU:0 now
where the time goes in v2:
time: 168 us
  waiting for transfers between devices  81.9 us (49%)
  Pallas kernels  45.3 us (27%)
  starting transfers between devices  33.7 us (20%)
  local copies, waits for them, and re-layouts  3.17 us (2%)
  other arithmetic  2.35 us (1%)
    ppermute x8, waiting for transfers between devices, shifted(): return lax.ppermute(block, 'ctx', route)  45.2 us
    ppermute x18, waiting for transfers between devices, swapped(): return lax.ppermute(block, 'ctx', [(i, i ^ partner) for i in devices])  36.7 us
    pallas_call x2, Pallas kernels, attend(): pl.pallas_call(functools.partial(attend_kernel, plane, group, rows, width...  28.6 us
    ppermute x8, starting transfers between devices, shifted(): return lax.ppermute(block, 'ctx', route)  20.2 us
    ppermute x18, starting transfers between devices, swapped(): return lax.ppermute(block, 'ctx', [(i, i ^ partner) for i in devices])  13.5 us
    pallas_call x2, Pallas kernels, pack(): pl.pallas_call(functools.partial(pack_kernel, plane, heads, group, len(ar...  11.6 us
    pallas_call x1, Pallas kernels, finish(): pl.pallas_call(functools.partial(finish_kernel, plane, heads), out_shape=...  5.07 us
  transfers between devices with their start and end apart: 26, of which 10 were waited for; matrix products, arithmetic and copies ran while one was open for 1% of the time, Pallas kernels for 22%

profile of v2, /device:TPU:0, one launch (start us, length us, event | category | flops | bytes accessed | tf_op | source)
XLA Modules:
  0.0 167.5 jit_solution(8183865686512658716)
XLA Ops:
  0.6 4.2 %pack.2 = (bf16[1040,128]{1,0:T(8,128)(2,1)}, bf16[1040,128]{1,0:T(8,128)(2,1)}, bf16[1040,128]{1,0:T(8,128)(2,1)}, bf16[1040,128]{1,0:T(8,128)(2,1)}, bf16[1040...) custom-call(bf16[256,8,128]{2,1,0:T(8,128)(2,1)} %refs_0_.2, ...), custom_call_target="tpu_custom_call" | custom-call | tf_op jit(solution)/shard_map/pack/pallas_call | solution.py:57
  4.8 3.0 %collective-permute-start.14 = (bf16[1040,128]{1,0:T(8,128)(2,1)}, bf16[1040,128]{1,0:T(8,128)(2,1)S(1)}, u32[]{:S(2)}, u32[]{:S(2)}) collective-permute-start(bf16[1040,128]{1,0:T(8,128)(2,1)} %get-tuple-element.52), channel_id=1, source_target_pairs={{0,2},{1,3},{2,0},{3,1},{4,6},{5,7},{6,4},{7,5},{8,10},{9,11},{10,... | collective-permute-start | bytes 798728 | tf_op jit(solution)/shard_map/ppermute | solution.py:26
  7.8 0.1 collective-permute-start.13
  7.9 7.4 %pack.3 = (bf16[1536,128]{1,0:T(8,128)(2,1)}, bf16[1536,128]{1,0:T(8,128)(2,1)}, bf16[1536,128]{1,0:T(8,128)(2,1)}, bf16[1536,128]{1,0:T(8,128)(2,1)}, bf16[1536...) custom-call(bf16[256,16,128]{2,1,0:T(8,128)(2,1)} %refs_0_.3, ...), custom_call_target="tpu_custom_call" | custom-call | tf_op jit(solution)/shard_map/pack/pallas_call | solution.py:57
  15.4 0.4 collective-permute-start.18
  15.7 1.7 %collective-permute-start.19 = (bf16[1536,128]{1,0:T(8,128)(2,1)}, bf16[1536,128]{1,0:T(8,128)(2,1)S(1)}, u32[]{:S(2)}, u32[]{:S(2)}) collective-permute-start(bf16[1536,128]{1,0:T(8,128)(2,1)} %get-tuple-element.56), channel_id=1, source_target_pairs={{0,2},{1,3},{2,0},{3,1},{4,6},{5,7},{6,4},{7,5},{8,10},{9,11},{10,... | collective-permute-start | bytes 1179656 | tf_op jit(solution)/shard_map/ppermute | solution.py:26
  17.5 0.4 collective-permute-start.1
  17.8 2.8 %collective-permute-done.15.refs_3_ = bf16[1040,128]{1,0:T(8,128)(2,1)S(1)} collective-permute-done((bf16[1040,128]{1,0:T(8,128)(2,1)}, bf16[1040,128]{1,0:T(8,128)(2,1)S(1)}, u32[]{:S(2)}, u32[]{:S(2)}) %collective-permute-start.15) | collective-permute-done | bytes 266272 | tf_op jit(solution)/shard_map/ppermute | solution.py:26
  20.6 1.8 %collective-permute-start.2 = (bf16[1040,128]{1,0:T(8,128)(2,1)S(1)}, bf16[1040,128]{1,0:T(8,128)(2,1)S(1)}, u32[]{:S(2)}, u32[]{:S(2)}) collective-permute-start(bf16[1040,128]{1,0:T(8,128)(2,1)S(1)} %copy-done.33), channel_id=1, source_target_pairs={{0,3},{1,2},{2,1},{3,0},{4,7},{5,6},{6,5},{7,4},{8,11},{9,10},{10,... | collective-permute-start | bytes 798728 | tf_op jit(solution)/shard_map/ppermute | solution.py:26
  22.5 0.1 collective-permute-start
  22.6 12.4 %collective-permute-done.1.refs_2_ = bf16[1040,128]{1,0:T(8,128)(2,1)S(1)} collective-permute-done((bf16[1040,128]{1,0:T(8,128)(2,1)S(1)}, bf16[1040,128]{1,0:T(8,128)(2,1)S(1)}, u32[]{:S(2)}, u32[]{:S(2)}) %collective-permute-start.1) | collective-permute-done | bytes 266272 | tf_op jit(solution)/shard_map/ppermute | solution.py:26
  35.1 5.2 %collective-permute-done.2.refs_3_ = bf16[1040,128]{1,0:T(8,128)(2,1)S(1)} collective-permute-done((bf16[1040,128]{1,0:T(8,128)(2,1)S(1)}, bf16[1040,128]{1,0:T(8,128)(2,1)S(1)}, u32[]{:S(2)}, u32[]{:S(2)}) %collective-permute-start.2) | collective-permute-done | bytes 266272 | tf_op jit(solution)/shard_map/ppermute | solution.py:26
  40.3 3.5 %collective-permute-start.17 = (bf16[2080,128]{1,0:T(8,128)(2,1)S(1)}, bf16[2080,128]{1,0:T(8,128)(2,1)S(1)}, u32[]{:S(2)}, u32[]{:S(2)}) collective-permute-start(bf16[2080,128]{1,0:T(8,128)(2,1)S(1)} %pad_maximum_fusion.3), channel_id=1, source_target_pairs={{0,4},{1,5},{2,6},{3,7},{4,8},{5,9},{6,10},{7,11},{8,12},{9,13},{1... | collective-permute-start | bytes 1597448 | tf_op jit(solution)/shard_map/ppermute | solution.py:21
  43.9 3.5 %collective-permute-start.16 = (bf16[2080,128]{1,0:T(8,128)(2,1)S(1)}, bf16[2080,128]{1,0:T(8,128)(2,1)S(1)}, u32[]{:S(2)}, u32[]{:S(2)}) collective-permute-start(bf16[2080,128]{1,0:T(8,128)(2,1)S(1)} %pad_maximum_fusion.2), channel_id=1, source_target_pairs={{0,4},{1,5},{2,6},{3,7},{4,8},{5,9},{6,10},{7,11},{8,12},{9,13},{1... | collective-permute-start | bytes 1597448 | tf_op jit(solution)/shard_map/ppermute | solution.py:21
  47.4 0.6 collective-permute-start.5
  48.0 1.5 collective-permute-start.6
  49.5 0.8 pad_maximum_fusion
  50.4 3.5 %collective-permute-start.4 = (bf16[2080,128]{1,0:T(8,128)(2,1)S(1)}, bf16[2080,128]{1,0:T(8,128)(2,1)S(1)}, u32[]{:S(2)}, u32[]{:S(2)}) collective-permute-start(bf16[2080,128]{1,0:T(8,128)(2,1)S(1)} %pad_maximum_fusion.1), channel_id=1, source_target_pairs={{0,4},{1,5},{2,6},{3,7},{4,8},{5,9},{6,10},{7,11},{8,12},{9,13},{1... | collective-permute-start | bytes 1597448 | tf_op jit(solution)/shard_map/ppermute | solution.py:21
  53.9 2.3 %collective-permute-done.17.refs_5_ = bf16[2080,128]{1,0:T(8,128)(2,1)S(1)} collective-permute-done((bf16[2080,128]{1,0:T(8,128)(2,1)S(1)}, bf16[2080,128]{1,0:T(8,128)(2,1)S(1)}, u32[]{:S(2)}, u32[]{:S(2)}) %collective-permute-start.17) | collective-permute-done | bytes 532512 | tf_op jit(solution)/shard_map/ppermute | solution.py:21
  56.2 4.4 %collective-permute-start.3 = (bf16[2080,128]{1,0:T(8,128)(2,1)}, bf16[2080,128]{1,0:T(8,128)(2,1)S(1)}, u32[]{:S(2)}, u32[]{:S(2)}) collective-permute-start(bf16[2080,128]{1,0:T(8,128)(2,1)} %pad_maximum_fusion), channel_id=1, source_target_pairs={{0,4},{1,5},{2,6},{3,7},{4,8},{5,9},{6,10},{7,11},{8,12},{9,13},{1... | collective-permute-start | bytes 1597448 | tf_op jit(solution)/shard_map/ppermute | solution.py:21
  60.6 7.0 %collective-permute-done.16.refs_4_ = bf16[2080,128]{1,0:T(8,128)(2,1)S(1)} collective-permute-done((bf16[2080,128]{1,0:T(8,128)(2,1)S(1)}, bf16[2080,128]{1,0:T(8,128)(2,1)S(1)}, u32[]{:S(2)}, u32[]{:S(2)}) %collective-permute-start.16) | collective-permute-done | bytes 532512 | tf_op jit(solution)/shard_map/ppermute | solution.py:21
  67.6 0.8 copy-done.13
  68.4 14.2 %attend.3 = (bf16[2048,128]{1,0:T(8,128)(2,1)}, bf16[2048,128]{1,0:T(8,128)(2,1)}, f32[1024,128]{1,0:T(8,128)}, f32[1024,128]{1,0:T(8,128)}, f32[1024,128]{1,0:T(8,128)}, /*index=5*/f32[1024,128]{1,0:T(8,128)}) custom-call(bf16[1040,128]{1,0:T(8,128)(2,1)} %get-tuple-element.50.refs_0_, bf16[1040,128]{1,0:T(8,128)(2,1)} %copy-done.9, ...), custom_call_target="tpu_custom_call" | custom-call | tf_op jit(solution)/shard_map/attend/pallas_call | solution.py:217
  82.6 1.3 collective-permute-start.23
  84.0 1.5 collective-permute-start.7
  85.5 1.5 collective-permute-start.21
  87.0 8.2 %collective-permute-done.7.refs_9_ = bf16[1536,128]{1,0:T(8,128)(2,1)S(1)} collective-permute-done((bf16[1536,128]{1,0:T(8,128)(2,1)}, bf16[1536,128]{1,0:T(8,128)(2,1)S(1)}, u32[]{:S(2)}, u32[]{:S(2)}) %collective-permute-start.7) | collective-permute-done | bytes 393248 | tf_op jit(solution)/shard_map/ppermute | solution.py:26
  95.2 0.7 copy-done.24
  95.9 0.2 copy-done.10
  96.1 0.6 copy-done.11
  96.7 14.4 %attend.2 = (bf16[2048,128]{1,0:T(8,128)(2,1)}, bf16[2048,128]{1,0:T(8,128)(2,1)}, f32[1024,128]{1,0:T(8,128)}, f32[1024,128]{1,0:T(8,128)}, f32[1024,128]{1,0:T(8,128)}, /*index=5*/f32[1024,128]{1,0:T(8,128)}) custom-call(bf16[1040,128]{1,0:T(8,128)(2,1)} %get-tuple-element.36.refs_0_, bf16[1040,128]{1,0:T(8,128)(2,1)} %copy-done.6, ...), custom_call_target="tpu_custom_call" | custom-call | tf_op jit(solution)/shard_map/attend/pallas_call | solution.py:217
  111.1 1.3 collective-permute-start.10
  112.4 1.3 collective-permute-start.8
  113.7 1.2 add_convert_fusion
  114.9 0.2 collective-permute-start.24
  115.1 1.9 %collective-permute-start.25 = (bf16[1024,128]{1,0:T(8,128)(2,1)S(1)}, bf16[1024,128]{1,0:T(8,128)(2,1)S(1)}, u32[]{:S(2)}, u32[]{:S(2)}) collective-permute-start(bf16[1024,128]{1,0:T(8,128)(2,1)S(1)} %get-tuple-element.68), channel_id=1, source_target_pairs={{0,3},{1,2},{2,1},{3,0},{4,7},{5,6},{6,5},{7,4},{8,11},{9,10},{10,... | collective-permute-start | bytes 786440 | tf_op jit(solution)/shard_map/ppermute | solution.py:26
  117.1 0.3 collective-permute-done.21.refs_9_
  117.4 0.1 collective-permute-start.22
  117.5 24.6 %collective-permute-done.10 = bf16[2048,128]{1,0:T(8,128)(2,1)S(1)} collective-permute-done((bf16[2048,128]{1,0:T(8,128)(2,1)}, bf16[2048,128]{1,0:T(8,128)(2,1)S(1)}, u32[]{:S(2)}, u32[]{:S(2)}) %collective-permute-start.10) | collective-permute-done | bytes 524320 | tf_op jit(solution)/shard_map/ppermute | solution.py:21
  142.1 0.1 add_convert_fusion.3
  142.2 0.1 collective-permute-start.11
  142.3 11.0 %collective-permute-done.8.refs_8_ = bf16[2048,128]{1,0:T(8,128)(2,1)S(1)} collective-permute-done((bf16[2048,128]{1,0:T(8,128)(2,1)}, bf16[2048,128]{1,0:T(8,128)(2,1)S(1)}, u32[]{:S(2)}, u32[]{:S(2)}) %collective-permute-start.8) | collective-permute-done | bytes 524320 | tf_op jit(solution)/shard_map/ppermute | solution.py:21
  153.3 0.1 add_convert_fusion.5
  153.4 0.2 collective-permute-start.9
  153.6 8.0 %collective-permute-done.12.refs_3_ = bf16[1024,128]{1,0:T(8,128)(2,1)S(1)} collective-permute-done((bf16[1024,128]{1,0:T(8,128)(2,1)S(1)}, bf16[1024,128]{1,0:T(8,128)(2,1)S(1)}, u32[]{:S(2)}, u32[]{:S(2)}) %collective-permute-start.12) | collective-permute-done | bytes 262176 | tf_op jit(solution)/shard_map/ppermute | solution.py:26
  161.7 0.7 copy-done.29
  162.4 0.1 copy-done.30
  162.5 5.1 %finish.1 = (f32[2048,128]{1,0:T(8,128)}, f32[2048,128]{1,0:T(8,128)}, f32[2048,128]{1,0:T(8,128)}, f32[2048,128]{1,0:T(8,128)}) custom-call(f32[1024,128]{1,0:T(8,128)} %get-tuple-element.44.refs_0_, bf16[1024,128]{1,0:T(8,128)(2,1)} %copy-done.30, bf16[1024,128]{1,0:T(8,128)(2,1)} %copy-done.28, bf16[1024,128]{1,0:T(8,128)(2,1)} %copy-done.29, ...), custom_call_target="tpu_custom_call" | custom-call | tf_op jit(solution)/shard_map/finish/pallas_call | solution.py:266
  (87 shorter events, 0.3 us)
Async XLA Ops:
  4.8 12.7 %collective-permute-start.14 = (bf16[1040,128]{1,0:T(8,128)(2,1)}, bf16[1040,128]{1,0:T(8,128)(2,1)S(1)}, u32[]{:S(2)}, u32[]{:S(2)}) collective-permute-start(bf16[1040,128]{1,0:T(8,128)(2,1)} %get-tuple-element.52), channel_id=1, source_target_pairs={{0,2},{1,3},{2,0},{3,1},{4,6},{5,7},{6,4},{7,5},{8,10},{9,11},{10,... | collective-permute-start | bytes 798728 | tf_op jit(solution)/shard_map/ppermute | solution.py:26
  7.8 12.8 %collective-permute-start.15 = (bf16[1040,128]{1,0:T(8,128)(2,1)}, bf16[1040,128]{1,0:T(8,128)(2,1)S(1)}, u32[]{:S(2)}, u32[]{:S(2)}) collective-permute-start(bf16[1040,128]{1,0:T(8,128)(2,1)} %get-tuple-element.53), channel_id=1, source_target_pairs={{0,3},{1,2},{2,1},{3,0},{4,7},{5,6},{6,5},{7,4},{8,11},{9,10},{10,... | collective-permute-start | bytes 798728 | tf_op jit(solution)/shard_map/ppermute | solution.py:26
  7.8 9.7 %copy-start.34 = (bf16[1040,128]{1,0:T(8,128)(2,1)S(1)}, bf16[1040,128]{1,0:T(8,128)(2,1)}, u32[]{:S(2)}) copy-start(bf16[1040,128]{1,0:T(8,128)(2,1)} %get-tuple-element.38) | copy-start | bytes 798724
  7.8 12.8 %copy-start.33 = (bf16[1040,128]{1,0:T(8,128)(2,1)S(1)}, bf16[1040,128]{1,0:T(8,128)(2,1)}, u32[]{:S(2)}) copy-start(bf16[1040,128]{1,0:T(8,128)(2,1)} %get-tuple-element.39) | copy-start | bytes 798724
  7.8 14.6 %collective-permute-start.13 = (bf16[1040,128]{1,0:T(8,128)(2,1)}, bf16[1040,128]{1,0:T(8,128)(2,1)S(1)}, u32[]{:S(2)}, u32[]{:S(2)}) collective-permute-start(bf16[1040,128]{1,0:T(8,128)(2,1)} %get-tuple-element.51), channel_id=1, source_target_pairs={{0,1},{1,0},{2,3},{3,2},{4,5},{5,4},{6,7},{7,6},{8,9},{9,8},{10,11... | collective-permute-start | bytes 798728 | tf_op jit(solution)/shard_map/ppermute | solution.py:26
  15.4 32.0 %collective-permute-start.18 = (bf16[1536,128]{1,0:T(8,128)(2,1)}, bf16[1536,128]{1,0:T(8,128)(2,1)S(1)}, u32[]{:S(2)}, u32[]{:S(2)}) collective-permute-start(bf16[1536,128]{1,0:T(8,128)(2,1)} %get-tuple-element.55), channel_id=1, source_target_pairs={{0,1},{1,0},{2,3},{3,2},{4,5},{5,4},{6,7},{7,6},{8,9},{9,8},{10,11... | collective-permute-start | bytes 1179656 | tf_op jit(solution)/shard_map/ppermute | solution.py:26
  15.7 32.3 %collective-permute-start.19 = (bf16[1536,128]{1,0:T(8,128)(2,1)}, bf16[1536,128]{1,0:T(8,128)(2,1)S(1)}, u32[]{:S(2)}, u32[]{:S(2)}) collective-permute-start(bf16[1536,128]{1,0:T(8,128)(2,1)} %get-tuple-element.56), channel_id=1, source_target_pairs={{0,2},{1,3},{2,0},{3,1},{4,6},{5,7},{6,4},{7,5},{8,10},{9,11},{10,... | collective-permute-start | bytes 1179656 | tf_op jit(solution)/shard_map/ppermute | solution.py:26
  17.5 17.6 %collective-permute-start.1 = (bf16[1040,128]{1,0:T(8,128)(2,1)S(1)}, bf16[1040,128]{1,0:T(8,128)(2,1)S(1)}, u32[]{:S(2)}, u32[]{:S(2)}) collective-permute-start(bf16[1040,128]{1,0:T(8,128)(2,1)S(1)} %copy-done.34), channel_id=1, source_target_pairs={{0,2},{1,3},{2,0},{3,1},{4,6},{5,7},{6,4},{7,5},{8,10},{9,11},{10,... | collective-permute-start | bytes 798728 | tf_op jit(solution)/shard_map/ppermute | solution.py:26
  20.6 14.5 %copy-start.31 = (bf16[1536,128]{1,0:T(8,128)(2,1)S(1)}, bf16[1536,128]{1,0:T(8,128)(2,1)}, u32[]{:S(2)}) copy-start(bf16[1536,128]{1,0:T(8,128)(2,1)} %get-tuple-element.57) | copy-start | bytes 1179652
  20.6 19.7 %collective-permute-start.2 = (bf16[1040,128]{1,0:T(8,128)(2,1)S(1)}, bf16[1040,128]{1,0:T(8,128)(2,1)S(1)}, u32[]{:S(2)}, u32[]{:S(2)}) collective-permute-start(bf16[1040,128]{1,0:T(8,128)(2,1)S(1)} %copy-done.33), channel_id=1, source_target_pairs={{0,3},{1,2},{2,1},{3,0},{4,7},{5,6},{6,5},{7,4},{8,11},{9,10},{10,... | collective-permute-start | bytes 798728 | tf_op jit(solution)/shard_map/ppermute | solution.py:26
  22.4 24.9 %copy-start.9 = (bf16[1040,128]{1,0:T(8,128)(2,1)}, bf16[1040,128]{1,0:T(8,128)(2,1)S(1)}, u32[]{:S(2)}) copy-start(bf16[1040,128]{1,0:T(8,128)(2,1)S(1)} %collective-permute-done.13.refs_1_) | copy-start | bytes 798724
  22.5 21.4 %collective-permute-start = (bf16[1040,128]{1,0:T(8,128)(2,1)S(1)}, bf16[1040,128]{1,0:T(8,128)(2,1)S(1)}, u32[]{:S(2)}, u32[]{:S(2)}) collective-permute-start(bf16[1040,128]{1,0:T(8,128)(2,1)S(1)} %copy-done.32), channel_id=1, source_target_pairs={{0,1},{1,0},{2,3},{3,2},{4,5},{5,4},{6,7},{7,6},{8,9},{9,8},{10,11... | collective-permute-start | bytes 798728 | tf_op jit(solution)/shard_map/ppermute | solution.py:26
  22.6 27.0 %copy-start.2 = (bf16[1040,128]{1,0:T(8,128)(2,1)S(1)}, bf16[1040,128]{1,0:T(8,128)(2,1)}, u32[]{:S(2)}) copy-start(bf16[1040,128]{1,0:T(8,128)(2,1)} %get-tuple-element.36.refs_0_) | copy-start | bytes 798724
  35.1 15.3 %copy-start.3 = (bf16[1040,128]{1,0:T(8,128)(2,1)}, bf16[1040,128]{1,0:T(8,128)(2,1)S(1)}, u32[]{:S(2)}) copy-start(bf16[1040,128]{1,0:T(8,128)(2,1)S(1)} %collective-permute-done.1.refs_2_) | copy-start | bytes 798724
  35.1 15.3 %collective-permute-start.20 = (bf16[1536,128]{1,0:T(8,128)(2,1)S(1)}, bf16[1536,128]{1,0:T(8,128)(2,1)S(1)}, u32[]{:S(2)}, u32[]{:S(2)}) collective-permute-start(bf16[1536,128]{1,0:T(8,128)(2,1)S(1)} %copy-done.31), channel_id=1, source_target_pairs={{0,3},{1,2},{2,1},{3,0},{4,7},{5,6},{6,5},{7,4},{8,11},{9,10},{10,... | collective-permute-start | bytes 1179656 | tf_op jit(solution)/shard_map/ppermute | solution.py:26
  40.3 10.0 %copy-start.4 = (bf16[1040,128]{1,0:T(8,128)(2,1)}, bf16[1040,128]{1,0:T(8,128)(2,1)S(1)}, u32[]{:S(2)}) copy-start(bf16[1040,128]{1,0:T(8,128)(2,1)S(1)} %collective-permute-done.2.refs_3_) | copy-start | bytes 798724
  40.3 15.8 %collective-permute-start.17 = (bf16[2080,128]{1,0:T(8,128)(2,1)S(1)}, bf16[2080,128]{1,0:T(8,128)(2,1)S(1)}, u32[]{:S(2)}, u32[]{:S(2)}) collective-permute-start(bf16[2080,128]{1,0:T(8,128)(2,1)S(1)} %pad_maximum_fusion.3), channel_id=1, source_target_pairs={{0,4},{1,5},{2,6},{3,7},{4,8},{5,9},{6,10},{7,11},{8,12},{9,13},{1... | collective-permute-start | bytes 1597448 | tf_op jit(solution)/shard_map/ppermute | solution.py:21
  43.9 23.7 %collective-permute-start.16 = (bf16[2080,128]{1,0:T(8,128)(2,1)S(1)}, bf16[2080,128]{1,0:T(8,128)(2,1)S(1)}, u32[]{:S(2)}, u32[]{:S(2)}) collective-permute-start(bf16[2080,128]{1,0:T(8,128)(2,1)S(1)} %pad_maximum_fusion.2), channel_id=1, source_target_pairs={{0,4},{1,5},{2,6},{3,7},{4,8},{5,9},{6,10},{7,11},{8,12},{9,13},{1... | collective-permute-start | bytes 1597448 | tf_op jit(solution)/shard_map/ppermute | solution.py:21
  47.4 20.2 %copy-start.20 = (bf16[1536,128]{1,0:T(8,128)(2,1)}, bf16[1536,128]{1,0:T(8,128)(2,1)S(1)}, u32[]{:S(2)}) copy-start(bf16[1536,128]{1,0:T(8,128)(2,1)S(1)} %collective-permute-done.18.refs_7_) | copy-start | bytes 1179652
  47.4 36.5 %collective-permute-start.5 = (bf16[1536,128]{1,0:T(8,128)(2,1)}, bf16[1536,128]{1,0:T(8,128)(2,1)S(1)}, u32[]{:S(2)}, u32[]{:S(2)}) collective-permute-start(bf16[1536,128]{1,0:T(8,128)(2,1)} %get-tuple-element.41), channel_id=1, source_target_pairs={{0,1},{1,0},{2,3},{3,2},{4,5},{5,4},{6,7},{7,6},{8,9},{9,8},{10,11... | collective-permute-start | bytes 1179656 | tf_op jit(solution)/shard_map/ppermute | solution.py:26
  48.0 19.6 %copy-start.21 = (bf16[1536,128]{1,0:T(8,128)(2,1)}, bf16[1536,128]{1,0:T(8,128)(2,1)S(1)}, u32[]{:S(2)}) copy-start(bf16[1536,128]{1,0:T(8,128)(2,1)S(1)} %collective-permute-done.19.refs_8_) | copy-start | bytes 1179652
  48.0 37.5 %collective-permute-start.6 = (bf16[1536,128]{1,0:T(8,128)(2,1)}, bf16[1536,128]{1,0:T(8,128)(2,1)}, u32[]{:S(2)}, u32[]{:S(2)}) collective-permute-start(bf16[1536,128]{1,0:T(8,128)(2,1)} %get-tuple-element.42), channel_id=1, source_target_pairs={{0,2},{1,3},{2,0},{3,1},{4,6},{5,7},{6,4},{7,5},{8,10},{9,11},{10,... | collective-permute-start | bytes 1179656 | tf_op jit(solution)/shard_map/ppermute | solution.py:26
  50.4 17.2 %copy-start.23 = (bf16[1536,128]{1,0:T(8,128)(2,1)}, bf16[1536,128]{1,0:T(8,128)(2,1)S(1)}, u32[]{:S(2)}) copy-start(bf16[1536,128]{1,0:T(8,128)(2,1)S(1)} %collective-permute-done.20.refs_9_) | copy-start | bytes 1179652
  50.4 44.8 %collective-permute-start.4 = (bf16[2080,128]{1,0:T(8,128)(2,1)S(1)}, bf16[2080,128]{1,0:T(8,128)(2,1)S(1)}, u32[]{:S(2)}, u32[]{:S(2)}) collective-permute-start(bf16[2080,128]{1,0:T(8,128)(2,1)S(1)} %pad_maximum_fusion.1), channel_id=1, source_target_pairs={{0,4},{1,5},{2,6},{3,7},{4,8},{5,9},{6,10},{7,11},{8,12},{9,13},{1... | collective-permute-start | bytes 1597448 | tf_op jit(solution)/shard_map/ppermute | solution.py:21
  56.2 11.4 %copy-start.12 = (bf16[2080,128]{1,0:T(8,128)(2,1)}, bf16[2080,128]{1,0:T(8,128)(2,1)S(1)}, u32[]{:S(2)}) copy-start(bf16[2080,128]{1,0:T(8,128)(2,1)S(1)} %collective-permute-done.17.refs_5_) | copy-start | bytes 1597444
  56.2 39.0 %collective-permute-start.3 = (bf16[2080,128]{1,0:T(8,128)(2,1)}, bf16[2080,128]{1,0:T(8,128)(2,1)S(1)}, u32[]{:S(2)}, u32[]{:S(2)}) collective-permute-start(bf16[2080,128]{1,0:T(8,128)(2,1)} %pad_maximum_fusion), channel_id=1, source_target_pairs={{0,4},{1,5},{2,6},{3,7},{4,8},{5,9},{6,10},{7,11},{8,12},{9,13},{1... | collective-permute-start | bytes 1597448 | tf_op jit(solution)/shard_map/ppermute | solution.py:21
  82.6 31.0 %collective-permute-start.23 = (bf16[2048,128]{1,0:T(8,128)(2,1)}, bf16[2048,128]{1,0:T(8,128)(2,1)}, u32[]{:S(2)}, u32[]{:S(2)}) collective-permute-start(bf16[2048,128]{1,0:T(8,128)(2,1)} %get-tuple-element.62), channel_id=1, source_target_pairs={{4,0},{5,1},{6,2},{7,3},{8,4},{9,5},{10,6},{11,7},{12,8},{13,9},{1... | collective-permute-start | bytes 1572872 | tf_op jit(solution)/shard_map/ppermute | solution.py:21
  84.0 11.2 %collective-permute-start.7 = (bf16[1536,128]{1,0:T(8,128)(2,1)}, bf16[1536,128]{1,0:T(8,128)(2,1)S(1)}, u32[]{:S(2)}, u32[]{:S(2)}) collective-permute-start(bf16[1536,128]{1,0:T(8,128)(2,1)} %get-tuple-element.43), channel_id=1, source_target_pairs={{0,3},{1,2},{2,1},{3,0},{4,7},{5,6},{6,5},{7,4},{8,11},{9,10},{10,... | collective-permute-start | bytes 1179656 | tf_op jit(solution)/shard_map/ppermute | solution.py:26
  85.5 31.8 %collective-permute-start.21 = (bf16[2048,128]{1,0:T(8,128)(2,1)}, bf16[2048,128]{1,0:T(8,128)(2,1)S(1)}, u32[]{:S(2)}, u32[]{:S(2)}) collective-permute-start(bf16[2048,128]{1,0:T(8,128)(2,1)} %get-tuple-element.60), channel_id=1, source_target_pairs={{4,0},{5,1},{6,2},{7,3},{8,4},{9,5},{10,6},{11,7},{12,8},{13,9},{1... | collective-permute-start | bytes 1572872 | tf_op jit(solution)/shard_map/ppermute | solution.py:21
  96.7 17.0 %copy-start.16 = (f32[1024,128]{1,0:T(8,128)S(1)}, f32[1024,128]{1,0:T(8,128)}, u32[]{:S(2)}) copy-start(f32[1024,128]{1,0:T(8,128)} %get-tuple-element.61) | copy-start | bytes 1572868
  96.7 17.0 %copy-start.17 = (f32[1024,128]{1,0:T(8,128)S(1)}, f32[1024,128]{1,0:T(8,128)}, u32[]{:S(2)}) copy-start(f32[1024,128]{1,0:T(8,128)} %get-tuple-element.63) | copy-start | bytes 1572868
  111.1 31.0 %collective-permute-start.10 = (bf16[2048,128]{1,0:T(8,128)(2,1)}, bf16[2048,128]{1,0:T(8,128)(2,1)S(1)}, u32[]{:S(2)}, u32[]{:S(2)}) collective-permute-start(bf16[2048,128]{1,0:T(8,128)(2,1)} %get-tuple-element.48), channel_id=1, source_target_pairs={{4,0},{5,1},{6,2},{7,3},{8,4},{9,5},{10,6},{11,7},{12,8},{13,9},{1... | collective-permute-start | bytes 1572872 | tf_op jit(solution)/shard_map/ppermute | solution.py:21
  112.4 41.0 %collective-permute-start.8 = (bf16[2048,128]{1,0:T(8,128)(2,1)}, bf16[2048,128]{1,0:T(8,128)(2,1)S(1)}, u32[]{:S(2)}, u32[]{:S(2)}) collective-permute-start(bf16[2048,128]{1,0:T(8,128)(2,1)} %get-tuple-element.46), channel_id=1, source_target_pairs={{4,0},{5,1},{6,2},{7,3},{8,4},{9,5},{10,6},{11,7},{12,8},{13,9},{1... | collective-permute-start | bytes 1572872 | tf_op jit(solution)/shard_map/ppermute | solution.py:21
  114.9 27.2 %copy-start.18 = (f32[1024,128]{1,0:T(8,128)S(1)}, f32[1024,128]{1,0:T(8,128)}, u32[]{:S(2)}) copy-start(f32[1024,128]{1,0:T(8,128)} %get-tuple-element.47) | copy-start | bytes 1572868
  114.9 27.2 %copy-start.19 = (f32[1024,128]{1,0:T(8,128)S(1)}, f32[1024,128]{1,0:T(8,128)}, u32[]{:S(2)}) copy-start(f32[1024,128]{1,0:T(8,128)} %get-tuple-element.49) | copy-start | bytes 1572868
  114.9 38.5 %collective-permute-start.24 = (bf16[1024,128]{1,0:T(8,128)(2,1)S(1)}, bf16[1024,128]{1,0:T(8,128)(2,1)S(1)}, u32[]{:S(2)}, u32[]{:S(2)}) collective-permute-start(bf16[1024,128]{1,0:T(8,128)(2,1)S(1)} %get-tuple-element.69), channel_id=1, source_target_pairs={{0,2},{1,3},{2,0},{3,1},{4,6},{5,7},{6,4},{7,5},{8,10},{9,11},{10,... | collective-permute-start | bytes 786440 | tf_op jit(solution)/shard_map/ppermute | solution.py:26
  115.1 38.5 %collective-permute-start.25 = (bf16[1024,128]{1,0:T(8,128)(2,1)S(1)}, bf16[1024,128]{1,0:T(8,128)(2,1)S(1)}, u32[]{:S(2)}, u32[]{:S(2)}) collective-permute-start(bf16[1024,128]{1,0:T(8,128)(2,1)S(1)} %get-tuple-element.68), channel_id=1, source_target_pairs={{0,3},{1,2},{2,1},{3,0},{4,7},{5,6},{6,5},{7,4},{8,11},{9,10},{10,... | collective-permute-start | bytes 786440 | tf_op jit(solution)/shard_map/ppermute | solution.py:26
  117.3 24.9 %copy-start = (bf16[2048,128]{1,0:T(8,128)(2,1)}, bf16[2048,128]{1,0:T(8,128)(2,1)S(1)}, u32[]{:S(2)}) copy-start(bf16[2048,128]{1,0:T(8,128)(2,1)S(1)} %collective-permute-done.21.refs_9_) | copy-start | bytes 1572868
  117.4 36.2 %collective-permute-start.22 = (bf16[1024,128]{1,0:T(8,128)(2,1)S(1)}, bf16[1024,128]{1,0:T(8,128)(2,1)S(1)}, u32[]{:S(2)}, u32[]{:S(2)}) collective-permute-start(bf16[1024,128]{1,0:T(8,128)(2,1)S(1)} %add_convert_fusion.2), channel_id=1, source_target_pairs={{0,1},{1,0},{2,3},{3,2},{4,5},{5,4},{6,7},{7,6},{8,9},{9,8},{10,11... | collective-permute-start | bytes 786440 | tf_op jit(solution)/shard_map/ppermute | solution.py:26
  142.1 11.2 %copy-start.15 = (f32[1024,128]{1,0:T(8,128)S(1)}, f32[1024,128]{1,0:T(8,128)}, u32[]{:S(2)}) copy-start(f32[1024,128]{1,0:T(8,128)} %get-tuple-element.45) | copy-start | bytes 1572868
  142.2 11.4 %collective-permute-start.11 = (bf16[1024,128]{1,0:T(8,128)(2,1)S(1)}, bf16[1024,128]{1,0:T(8,128)(2,1)S(1)}, u32[]{:S(2)}, u32[]{:S(2)}) collective-permute-start(bf16[1024,128]{1,0:T(8,128)(2,1)S(1)} %get-tuple-element.71), channel_id=1, source_target_pairs={{0,2},{1,3},{2,0},{3,1},{4,6},{5,7},{6,4},{7,5},{8,10},{9,11},{10,... | collective-permute-start | bytes 786440 | tf_op jit(solution)/shard_map/ppermute | solution.py:26
  153.3 8.3 %copy-start.1 = (bf16[2048,128]{1,0:T(8,128)(2,1)}, bf16[2048,128]{1,0:T(8,128)(2,1)S(1)}, u32[]{:S(2)}) copy-start(bf16[2048,128]{1,0:T(8,128)(2,1)S(1)} %collective-permute-done.8.refs_8_) | copy-start | bytes 1572868
  153.3 8.3 %collective-permute-start.12 = (bf16[1024,128]{1,0:T(8,128)(2,1)S(1)}, bf16[1024,128]{1,0:T(8,128)(2,1)S(1)}, u32[]{:S(2)}, u32[]{:S(2)}) collective-permute-start(bf16[1024,128]{1,0:T(8,128)(2,1)S(1)} %get-tuple-element.70), channel_id=1, source_target_pairs={{0,3},{1,2},{2,1},{3,0},{4,7},{5,6},{6,5},{7,4},{8,11},{9,10},{10,... | collective-permute-start | bytes 786440 | tf_op jit(solution)/shard_map/ppermute | solution.py:26
  153.4 8.3 %copy-start.25 = (bf16[1024,128]{1,0:T(8,128)(2,1)}, bf16[1024,128]{1,0:T(8,128)(2,1)S(1)}, u32[]{:S(2)}) copy-start(bf16[1024,128]{1,0:T(8,128)(2,1)S(1)} %collective-permute-done.24.refs_6_) | copy-start | bytes 786436
  153.4 8.2 %collective-permute-start.9 = (bf16[1024,128]{1,0:T(8,128)(2,1)S(1)}, bf16[1024,128]{1,0:T(8,128)(2,1)S(1)}, u32[]{:S(2)}, u32[]{:S(2)}) collective-permute-start(bf16[1024,128]{1,0:T(8,128)(2,1)S(1)} %add_convert_fusion.5), channel_id=1, source_target_pairs={{0,1},{1,0},{2,3},{3,2},{4,5},{5,4},{6,7},{7,6},{8,9},{9,8},{10,11... | collective-permute-start | bytes 786440 | tf_op jit(solution)/shard_map/ppermute | solution.py:26
  153.6 8.1 %copy-start.26 = (bf16[1024,128]{1,0:T(8,128)(2,1)}, bf16[1024,128]{1,0:T(8,128)(2,1)S(1)}, u32[]{:S(2)}) copy-start(bf16[1024,128]{1,0:T(8,128)(2,1)S(1)} %collective-permute-done.25.refs_7_) | copy-start | bytes 786436
  153.6 8.1 %copy-start.27 = (bf16[1024,128]{1,0:T(8,128)(2,1)}, bf16[1024,128]{1,0:T(8,128)(2,1)S(1)}, u32[]{:S(2)}) copy-start(bf16[1024,128]{1,0:T(8,128)(2,1)S(1)} %collective-permute-done.22.refs_5_) | copy-start | bytes 786436
  153.6 8.1 %copy-start.28 = (bf16[1024,128]{1,0:T(8,128)(2,1)}, bf16[1024,128]{1,0:T(8,128)(2,1)S(1)}, u32[]{:S(2)}) copy-start(bf16[1024,128]{1,0:T(8,128)(2,1)S(1)} %collective-permute-done.11.refs_2_) | copy-start | bytes 786436
  (13 other events, 38.0 us)

commit v3 on v2

--- a/solution.py
+++ b/solution.py
@@ -28,7 +28,8 @@
 
 def pack_kernel(plane, heads, group, arrays, *refs):
     seg = refs[arrays] if group == 1 else None
-    outs, wide = refs[-1 - plane * heads : -1], refs[-1]
+    outs, wide = refs[-2 - (plane - 1) * heads : -1], refs[-1]
+    length = outs[1].shape[0]
     me = lax.rem(lax.axis_index("ctx"), plane)
     for t, array in enumerate(refs[:arrays]):
         rows, count, width = array.shape
@@ -36,17 +37,20 @@
         for h in range(heads):
             for k in range(plane):
                 first = ((me ^ k) * heads + h) * group
+                out = outs[0] if k == 0 else outs[h * (plane - 1) + k]
                 for g in range(group):
-                    at = (t * group + g) * rows
-                    outs[h * plane + k][at : at + rows, :] = wide[
+                    at = (t * group + g) * rows + (h * length if k == 0 else 0)
+                    out[at : at + rows, :] = wide[
                         pl.ds(first + g, rows, stride=count), :
                     ].astype(BF16)
     if group == 1:
         docs = seg[...].astype(F32)
         filler = jnp.zeros((TAIL - docs.shape[0], docs.shape[1]), F32)
         tail = jnp.concatenate([docs, filler], axis=0).astype(BF16)
-        for out in outs:
-            out[arrays * rows :, :] = tail
+        for h in range(heads):
+            outs[0][(h + 1) * length - TAIL : (h + 1) * length, :] = tail
+        for out in outs[1:]:
+            out[length - TAIL :, :] = tail
 
 
 def pack(arrays, plane, heads, group, seg=None):
@@ -54,17 +58,19 @@
     length = len(arrays) * group * rows + (0 if seg is None else TAIL)
     vmem = pl.BlockSpec(memory_space=pltpu.VMEM)
     inputs = list(arrays) + ([] if seg is None else [seg])
+    pieces = (plane - 1) * heads
     return pl.pallas_call(
         functools.partial(pack_kernel, plane, heads, group, len(arrays)),
-        out_shape=[jax.ShapeDtypeStruct((length, width), BF16)] * (plane * heads),
+        out_shape=[jax.ShapeDtypeStruct((heads * length, width), BF16)]
+        + [jax.ShapeDtypeStruct((length, width), BF16)] * pieces,
         in_specs=[vmem] * len(inputs),
-        out_specs=[vmem] * (plane * heads),
+        out_specs=[vmem] * (1 + pieces),
         scratch_shapes=[pltpu.VMEM((rows * count, width), F32)],
         name="pack",
     )(*inputs)
 
 
-def attend_kernel(plane, group, rows, width, *refs):
+def attend_kernel(plane, group, rows, width, head, *refs):
     half = plane // 2
     length = 4 * rows + TAIL
     own, pairs, queries = refs[:plane], refs[plane : plane + 2], refs[plane + 2 : 2 * plane + 2]
@@ -85,7 +91,9 @@
 
     low, high = pl.ds(0, width), pl.ds(width, width)
     for k in range(plane):
-        for piece, start, base in ((own[k], 0, plane), (pairs[k // half], k % half * length, 0)):
+        mine = (own[k], head * length if k == 0 else 0, plane)
+        past = (pairs[min(k, 1)], (head if k == 0 else k - 1) * length, 0)
+        for piece, start, base in (mine, past):
             block = base + (me ^ k)
             part = [piece.at[pl.ds(start + t * rows, rows), :] for t in range(4)]
             fetch(part[0], ka.at[block, :, low])
@@ -95,7 +103,8 @@
             fetch(part[3], vv.at[block, 1])
             fetch(piece.at[pl.ds(start + 4 * rows, TAIL), :], segs.at[block])
         block = me ^ k
-        part = [queries[k].at[pl.ds(t * span, span), :] for t in range(3)]
+        start = head * 3 * span if k == 0 else 0
+        part = [queries[k].at[pl.ds(start + t * span, span), :] for t in range(3)]
         fetch(part[0], qq.at[block, :, low])
         fetch(part[1], qq.at[block, :, high])
         fetch(part[2], do.at[block])
@@ -208,14 +217,14 @@
             out_own[k][at, :] = scale * acc[plane + (me ^ k), t]
 
 
-def attend(own, pairs, queries, plane, group):
-    length, width = own[0].shape
+def attend(own, pairs, queries, plane, group, head):
+    length, width = own[1].shape
     rows = (length - TAIL) // 4
     span = group * rows
     vmem = pl.BlockSpec(memory_space=pltpu.VMEM)
     blocks = 2 * plane
     results = pl.pallas_call(
-        functools.partial(attend_kernel, plane, group, rows, width),
+        functools.partial(attend_kernel, plane, group, rows, width, head),
         out_shape=[jax.ShapeDtypeStruct((2 * plane * rows, width), BF16)] * 2
         + [jax.ShapeDtypeStruct((4 * rows, width), F32)] * plane,
         in_specs=[pl.BlockSpec(memory_space=pl.ANY)] * (2 * plane + 2),
@@ -247,29 +256,32 @@
     pieces, returned = refs[: plane * heads], refs[plane * heads : plane * heads + heads]
     outs = refs[-4:]
     me = lax.rem(lax.axis_index("ctx"), plane)
+    rows = pieces[0].shape[1]
     for h in range(heads):
         for k in range(plane):
             piece = pieces[h * plane + k]
-            rows = piece.shape[0] // 4
             head = (me ^ k) * heads + h
             for t in range(4):
-                at = slice(t * rows, (t + 1) * rows)
-                value = piece[at, :].astype(F32)
+                value = piece[t].astype(F32)
                 if k == 0:
-                    value = value + returned[h][at, :].astype(F32)
+                    value = value + returned[h][t].astype(F32)
                 outs[t][pl.ds(head, rows, stride=plane * heads), :] = value
 
 
 def finish(pieces, returned, plane, heads):
-    length, width = pieces[0].shape
-    vmem = pl.BlockSpec(memory_space=pltpu.VMEM)
+    width = pieces[0].shape[1]
+    rows = pieces[0].shape[0] // 4
+    steps = 4
+    tile = rows // steps
+    stacked = [x.reshape(-1, rows, width) for x in list(pieces) + list(returned)]
     return pl.pallas_call(
         functools.partial(finish_kernel, plane, heads),
-        out_shape=[jax.ShapeDtypeStruct((length // 4 * plane * heads, width), F32)] * 4,
-        in_specs=[vmem] * (plane * heads + heads),
-        out_specs=[vmem] * 4,
+        grid=(steps,),
+        out_shape=[jax.ShapeDtypeStruct((rows * plane * heads, width), F32)] * 4,
+        in_specs=[pl.BlockSpec((4, tile, width), lambda i: (0, i, 0))] * len(stacked),
+        out_specs=[pl.BlockSpec((tile * plane * heads, width), lambda i: (i, 0))] * 4,
         name="finish",
-    )(*pieces, *returned)
+    )(*stacked)
 
 
 def local(
@@ -283,22 +295,21 @@
     far_first = list(range(half, plane)) + list(range(1, half))
 
     def spread(blocks, h):
-        results = [blocks[h * plane]] + [None] * (plane - 1)
+        results = [blocks[0]] + [None] * (plane - 1)
         for k in far_first:
-            results[k] = swapped(blocks[h * plane + k], k)
+            results[k] = swapped(blocks[h * (plane - 1) + k], k)
         return results
 
     seg = segment_ids.reshape(rows // width, width)
     kv = pack((keys, values, key_direction, value_direction), plane, heads, 1, seg)
     qs = pack((query, query_tangent, out_cotangent), plane, heads, group)
+    first = shifted(kv[0], plane)
     pieces, returned = [], []
     for h in range(heads):
         own = spread(kv, h)
-        pairs = []
-        for part in (own[:half], own[half:]):
-            pairs.append(shifted(jnp.concatenate(part, axis=0), plane))
+        pairs = [first, shifted(jnp.concatenate(own[1:], axis=0), plane)]
         queries = spread(qs, h)
-        sums_prev, sums_own = attend(own, pairs, queries, plane, group)
+        sums_prev, sums_own = attend(own, pairs, queries, plane, group, h)
         back = [None, None]
         for i in (1, 0):
             back[i] = shifted(sums_prev[i], -plane)

time: 168 us -> 164 us (0.976)
  starting transfers between devices: 33.7 us -> 30.4 us
    ppermute x8 -> x7, waiting for transfers between devices: 45.2 us -> 33.4 us  [shifted(): return lax.ppermute(block, 'ctx', route)]
    ppermute x18, waiting for transfers between devices: 36.7 us -> 47 us  [swapped(): return lax.ppermute(block, 'ctx', [(i, i ^ partner) for i in devices])]
    ppermute x8 -> x7, starting transfers between devices: 20.2 us -> 15.9 us  [shifted(): return lax.ppermute(block, 'ctx', route)]
  transfers between devices with their start and end apart: 26 -> 25, of which waited for: 10 -> 9; matrix products, arithmetic and copies ran while one was open for 1% -> 2% of each run, Pallas kernels for 22% -> 22%
where the time goes in v3:
time: 164 us
  waiting for transfers between devices  80.5 us (49%)
  Pallas kernels  45.1 us (28%)
  starting transfers between devices  30.4 us (19%)
  other arithmetic  3.34 us (2%)
  local copies, waits for them, and re-layouts  3.33 us (2%)
    ppermute x18, waiting for transfers between devices, swapped(): return lax.ppermute(block, 'ctx', [(i, i ^ partner) for i in devices])  47 us
    ppermute x7, waiting for transfers between devices, shifted(): return lax.ppermute(block, 'ctx', route)  33.4 us
    pallas_call x2, Pallas kernels, attend(): pl.pallas_call(functools.partial(attend_kernel, plane, group, rows, width...  28.5 us
    ppermute x7, starting transfers between devices, shifted(): return lax.ppermute(block, 'ctx', route)  15.9 us
    ppermute x18, starting transfers between devices, swapped(): return lax.ppermute(block, 'ctx', [(i, i ^ partner) for i in devices])  14.4 us
    pallas_call x2, Pallas kernels, pack(): pl.pallas_call(functools.partial(pack_kernel, plane, heads, group, len(ar...  11.7 us
    pallas_call x1, Pallas kernels, finish(): pl.pallas_call(functools.partial(finish_kernel, plane, heads), grid=(step...  4.94 us
    unnamed x54, local copies, waits for them, and re-layouts  3.33 us
  transfers between devices with their start and end apart: 25, of which 9 were waited for; matrix products, arithmetic and copies ran while one was open for 2% of the time, Pallas kernels for 22%

profile of v3, /device:TPU:0, one launch (start us, length us, event | category | flops | bytes accessed | tf_op | source)
XLA Modules:
  0.0 163.7 jit_solution(14663610014735935960)
XLA Ops:
  0.6 4.1 %pack.2 = (bf16[2080,128]{1,0:T(8,128)(2,1)}, bf16[1040,128]{1,0:T(8,128)(2,1)}, bf16[1040,128]{1,0:T(8,128)(2,1)}, bf16[1040,128]{1,0:T(8,128)(2,1)}, bf16[1040...) custom-call(bf16[256,8,128]{2,1,0:T(8,128)(2,1)} %refs_0_.2, bf16[256,8,128]{2,1,0:T(8,128)(2,1)} %refs_1_.2, ...), custom_call_target="tpu_custom_call" | custom-call | tf_op jit(solution)/shard_map/pack/pallas_call | solution.py:62
  4.7 0.5 collective-permute-start.13
  5.2 2.6 %collective-permute-start.14 = (bf16[1040,128]{1,0:T(8,128)(2,1)}, bf16[1040,128]{1,0:T(8,128)(2,1)S(1)}, u32[]{:S(2)}, u32[]{:S(2)}) collective-permute-start(bf16[1040,128]{1,0:T(8,128)(2,1)} %get-tuple-element.49), channel_id=1, source_target_pairs={{0,2},{1,3},{2,0},{3,1},{4,6},{5,7},{6,4},{7,5},{8,10},{9,11},{10,... | collective-permute-start | bytes 798728 | tf_op jit(solution)/shard_map/ppermute | solution.py:26
  7.9 0.1 collective-permute-start
  8.0 1.9 %collective-permute-start.1 = (bf16[1040,128]{1,0:T(8,128)(2,1)}, bf16[1040,128]{1,0:T(8,128)(2,1)S(1)}, u32[]{:S(2)}, u32[]{:S(2)}) collective-permute-start(bf16[1040,128]{1,0:T(8,128)(2,1)} %get-tuple-element.36), channel_id=1, source_target_pairs={{0,2},{1,3},{2,0},{3,1},{4,6},{5,7},{6,4},{7,5},{8,10},{9,11},{10,... | collective-permute-start | bytes 798728 | tf_op jit(solution)/shard_map/ppermute | solution.py:26
  10.0 5.3 %collective-permute-done.14.refs_2_ = bf16[1040,128]{1,0:T(8,128)(2,1)S(1)} collective-permute-done((bf16[1040,128]{1,0:T(8,128)(2,1)}, bf16[1040,128]{1,0:T(8,128)(2,1)S(1)}, u32[]{:S(2)}, u32[]{:S(2)}) %collective-permute-start.14) | collective-permute-done | bytes 266272 | tf_op jit(solution)/shard_map/ppermute | solution.py:26
  15.3 5.3 %collective-permute-done.15.refs_3_ = bf16[1040,128]{1,0:T(8,128)(2,1)S(1)} collective-permute-done((bf16[1040,128]{1,0:T(8,128)(2,1)}, bf16[1040,128]{1,0:T(8,128)(2,1)S(1)}, u32[]{:S(2)}, u32[]{:S(2)}) %collective-permute-start.15) | collective-permute-done | bytes 266272 | tf_op jit(solution)/shard_map/ppermute | solution.py:26
  20.6 1.0 pad_maximum_fusion.1
  21.6 3.5 %collective-permute-start.16 = (bf16[3120,128]{1,0:T(8,128)(2,1)}, bf16[3120,128]{1,0:T(8,128)(2,1)S(1)}, u32[]{:S(2)}, u32[]{:S(2)}) collective-permute-start(bf16[3120,128]{1,0:T(8,128)(2,1)} %pad_maximum_fusion.1), channel_id=1, source_target_pairs={{0,4},{1,5},{2,6},{3,7},{4,8},{5,9},{6,10},{7,11},{8,12},{9,13},{1... | collective-permute-start | bytes 2396168 | tf_op jit(solution)/shard_map/ppermute | solution.py:21
  25.1 3.5 %collective-permute-start.3 = (bf16[2080,128]{1,0:T(8,128)(2,1)S(1)}, bf16[2080,128]{1,0:T(8,128)(2,1)S(1)}, u32[]{:S(2)}, u32[]{:S(2)}) collective-permute-start(bf16[2080,128]{1,0:T(8,128)(2,1)S(1)} %copy-done), channel_id=1, source_target_pairs={{0,4},{1,5},{2,6},{3,7},{4,8},{5,9},{6,10},{7,11},{8,12},{9,13},{1... | collective-permute-start | bytes 1597448 | tf_op jit(solution)/shard_map/ppermute | solution.py:21
  28.6 7.5 %pack.3 = (bf16[3072,128]{1,0:T(8,128)(2,1)}, bf16[1536,128]{1,0:T(8,128)(2,1)}, bf16[1536,128]{1,0:T(8,128)(2,1)}, bf16[1536,128]{1,0:T(8,128)(2,1)}, bf16[1536...) custom-call(bf16[256,16,128]{2,1,0:T(8,128)(2,1)} %refs_0_.3, ...), custom_call_target="tpu_custom_call" | custom-call | tf_op jit(solution)/shard_map/pack/pallas_call | solution.py:62
  36.2 0.2 collective-permute-start.17
  36.4 1.5 collective-permute-start.18
  37.9 0.2 collective-permute-start.19
  38.1 0.9 pad_maximum_fusion
  39.1 3.5 %collective-permute-start.4 = (bf16[3120,128]{1,0:T(8,128)(2,1)}, bf16[3120,128]{1,0:T(8,128)(2,1)S(1)}, u32[]{:S(2)}, u32[]{:S(2)}) collective-permute-start(bf16[3120,128]{1,0:T(8,128)(2,1)} %pad_maximum_fusion), channel_id=1, source_target_pairs={{0,4},{1,5},{2,6},{3,7},{4,8},{5,9},{6,10},{7,11},{8,12},{9,13},{1... | collective-permute-start | bytes 2396168 | tf_op jit(solution)/shard_map/ppermute | solution.py:21
  42.6 6.0 %collective-permute-done.18.refs_8_ = bf16[1536,128]{1,0:T(8,128)(2,1)S(1)} collective-permute-done((bf16[1536,128]{1,0:T(8,128)(2,1)}, bf16[1536,128]{1,0:T(8,128)(2,1)S(1)}, u32[]{:S(2)}, u32[]{:S(2)}) %collective-permute-start.18) | collective-permute-done | bytes 393248 | tf_op jit(solution)/shard_map/ppermute | solution.py:26
  48.6 7.3 %collective-permute-done.19.refs_9_ = bf16[1536,128]{1,0:T(8,128)(2,1)S(1)} collective-permute-done((bf16[1536,128]{1,0:T(8,128)(2,1)}, bf16[1536,128]{1,0:T(8,128)(2,1)S(1)}, u32[]{:S(2)}, u32[]{:S(2)}) %collective-permute-start.19) | collective-permute-done | bytes 393248 | tf_op jit(solution)/shard_map/ppermute | solution.py:26
  55.9 0.7 copy-done.19
  56.6 0.2 copy-done.1
  56.8 0.7 copy-done.11
  57.5 14.2 %attend.3 = (bf16[2048,128]{1,0:T(8,128)(2,1)}, bf16[2048,128]{1,0:T(8,128)(2,1)}, f32[1024,128]{1,0:T(8,128)}, f32[1024,128]{1,0:T(8,128)}, f32[1024,128]{1,0:T(8,128)}, /*index=5*/f32[1024,128]{1,0:T(8,128)}) custom-call(bf16[2080,128]{1,0:T(8,128)(2,1)} %get-tuple-element.34.refs_0_, bf16[1040,128]{1,0:T(8,128)(2,1)} %copy-done.7, ...), custom_call_target="tpu_custom_call" | custom-call | tf_op jit(solution)/shard_map/attend/pallas_call | solution.py:226
  71.8 1.3 collective-permute-start.22
  73.1 1.2 collective-permute-start.6
  74.3 0.6 collective-permute-start.7
  74.9 1.6 collective-permute-start.20
  76.5 8.8 %collective-permute-done.6.refs_8_ = bf16[1536,128]{1,0:T(8,128)(2,1)S(1)} collective-permute-done((bf16[1536,128]{1,0:T(8,128)(2,1)}, bf16[1536,128]{1,0:T(8,128)(2,1)S(1)}, u32[]{:S(2)}, u32[]{:S(2)}) %collective-permute-start.6) | collective-permute-done | bytes 393248 | tf_op jit(solution)/shard_map/ppermute | solution.py:26
  85.3 7.4 %collective-permute-done.7.refs_9_ = bf16[1536,128]{1,0:T(8,128)(2,1)} collective-permute-done((bf16[1536,128]{1,0:T(8,128)(2,1)}, bf16[1536,128]{1,0:T(8,128)(2,1)}, u32[]{:S(2)}, u32[]{:S(2)}) %collective-permute-start.7) | collective-permute-done | bytes 393248 | tf_op jit(solution)/shard_map/ppermute | solution.py:26
  92.8 0.9 copy-done.10
  93.6 14.2 %attend.2 = (bf16[2048,128]{1,0:T(8,128)(2,1)}, bf16[2048,128]{1,0:T(8,128)(2,1)}, f32[1024,128]{1,0:T(8,128)}, f32[1024,128]{1,0:T(8,128)}, f32[1024,128]{1,0:T(8,128)}, /*index=5*/f32[1024,128]{1,0:T(8,128)}) custom-call(bf16[2080,128]{1,0:T(8,128)(2,1)} %get-tuple-element.34.refs_0_, bf16[1040,128]{1,0:T(8,128)(2,1)} %copy-done.4, ...), custom_call_target="tpu_custom_call" | custom-call | tf_op jit(solution)/shard_map/attend/pallas_call | solution.py:226
  107.9 1.3 collective-permute-start.10
  109.2 1.3 collective-permute-start.8
  110.5 1.2 add_convert_fusion
  111.8 1.6 collective-permute-start.23
  113.3 0.5 collective-permute-start.24
  113.9 0.1 add_convert_fusion.2
  113.9 0.2 collective-permute-start.21
  114.1 24.3 %collective-permute-done.10 = bf16[2048,128]{1,0:T(8,128)(2,1)S(1)} collective-permute-done((bf16[2048,128]{1,0:T(8,128)(2,1)}, bf16[2048,128]{1,0:T(8,128)(2,1)S(1)}, u32[]{:S(2)}, u32[]{:S(2)}) %collective-permute-start.10) | collective-permute-done | bytes 524320 | tf_op jit(solution)/shard_map/ppermute | solution.py:21
  138.4 0.1 add_convert_fusion.3
  138.6 1.6 collective-permute-start.11
  140.2 9.1 %collective-permute-done.8 = bf16[2048,128]{1,0:T(8,128)(2,1)S(1)} collective-permute-done((bf16[2048,128]{1,0:T(8,128)(2,1)}, bf16[2048,128]{1,0:T(8,128)(2,1)S(1)}, u32[]{:S(2)}, u32[]{:S(2)}) %collective-permute-start.8) | collective-permute-done | bytes 524320 | tf_op jit(solution)/shard_map/ppermute | solution.py:21
  149.3 0.5 collective-permute-start.12
  149.8 0.1 add_convert_fusion.5
  149.8 1.1 collective-permute-start.9
  150.9 6.9 %collective-permute-done.12 = bf16[1024,128]{1,0:T(8,128)(2,1)S(1)} collective-permute-done((bf16[1024,128]{1,0:T(8,128)(2,1)S(1)}, bf16[1024,128]{1,0:T(8,128)(2,1)S(1)}, u32[]{:S(2)}, u32[]{:S(2)}) %collective-permute-start.12) | collective-permute-done | bytes 262176 | tf_op jit(solution)/shard_map/ppermute | solution.py:26
  157.8 0.6 copy-done.25
  158.5 0.1 copy-done.26
  158.6 4.9 %finish.1 = (f32[2048,128]{1,0:T(8,128)}, f32[2048,128]{1,0:T(8,128)}, f32[2048,128]{1,0:T(8,128)}, f32[2048,128]{1,0:T(8,128)}) custom-call(f32[4,256,128]{2,1,0:T(8,128)} %bitcast.18, bf16[4,256,128]{2,1,0:T(8,128)(2,1)} %bitcast.24, bf16[4,256,128]{2,1,0:T(8,128)(2,1)} %bitcast.22, bf16[4,256,128]{2,1,0:T(8,128)(2,1)} %bitcast.23, ...), custom_call_target="tpu_custom_call" | custom-call | tf_op jit(solution)/shard_map/finish/pallas_call | solution.py:277
  (67 shorter events, 0.2 us)
Async XLA Ops:
  4.7 20.4 %copy-start = (bf16[2080,128]{1,0:T(8,128)(2,1)S(1)}, bf16[2080,128]{1,0:T(8,128)(2,1)}, u32[]{:S(2)}) copy-start(bf16[2080,128]{1,0:T(8,128)(2,1)} %get-tuple-element.34.refs_0_) | copy-start | bytes 1597444
  4.7 5.2 %collective-permute-start.13 = (bf16[1040,128]{1,0:T(8,128)(2,1)}, bf16[1040,128]{1,0:T(8,128)(2,1)S(1)}, u32[]{:S(2)}, u32[]{:S(2)}) collective-permute-start(bf16[1040,128]{1,0:T(8,128)(2,1)} %get-tuple-element.48), channel_id=1, source_target_pairs={{0,1},{1,0},{2,3},{3,2},{4,5},{5,4},{6,7},{7,6},{8,9},{9,8},{10,11... | collective-permute-start | bytes 798728 | tf_op jit(solution)/shard_map/ppermute | solution.py:26
  5.2 10.0 %collective-permute-start.14 = (bf16[1040,128]{1,0:T(8,128)(2,1)}, bf16[1040,128]{1,0:T(8,128)(2,1)S(1)}, u32[]{:S(2)}, u32[]{:S(2)}) collective-permute-start(bf16[1040,128]{1,0:T(8,128)(2,1)} %get-tuple-element.49), channel_id=1, source_target_pairs={{0,2},{1,3},{2,0},{3,1},{4,6},{5,7},{6,4},{7,5},{8,10},{9,11},{10,... | collective-permute-start | bytes 798728 | tf_op jit(solution)/shard_map/ppermute | solution.py:26
  7.8 12.8 %collective-permute-start.15 = (bf16[1040,128]{1,0:T(8,128)(2,1)}, bf16[1040,128]{1,0:T(8,128)(2,1)S(1)}, u32[]{:S(2)}, u32[]{:S(2)}) collective-permute-start(bf16[1040,128]{1,0:T(8,128)(2,1)} %get-tuple-element.50), channel_id=1, source_target_pairs={{0,3},{1,2},{2,1},{3,0},{4,7},{5,6},{6,5},{7,4},{8,11},{9,10},{10,... | collective-permute-start | bytes 798728 | tf_op jit(solution)/shard_map/ppermute | solution.py:26
  7.9 28.3 %collective-permute-start = (bf16[1040,128]{1,0:T(8,128)(2,1)}, bf16[1040,128]{1,0:T(8,128)(2,1)S(1)}, u32[]{:S(2)}, u32[]{:S(2)}) collective-permute-start(bf16[1040,128]{1,0:T(8,128)(2,1)} %get-tuple-element.35), channel_id=1, source_target_pairs={{0,1},{1,0},{2,3},{3,2},{4,5},{5,4},{6,7},{7,6},{8,9},{9,8},{10,11... | collective-permute-start | bytes 798728 | tf_op jit(solution)/shard_map/ppermute | solution.py:26
  8.0 28.4 %collective-permute-start.1 = (bf16[1040,128]{1,0:T(8,128)(2,1)}, bf16[1040,128]{1,0:T(8,128)(2,1)S(1)}, u32[]{:S(2)}, u32[]{:S(2)}) collective-permute-start(bf16[1040,128]{1,0:T(8,128)(2,1)} %get-tuple-element.36), channel_id=1, source_target_pairs={{0,2},{1,3},{2,0},{3,1},{4,6},{5,7},{6,4},{7,5},{8,10},{9,11},{10,... | collective-permute-start | bytes 798728 | tf_op jit(solution)/shard_map/ppermute | solution.py:26
  10.0 26.2 %copy-start.7 = (bf16[1040,128]{1,0:T(8,128)(2,1)}, bf16[1040,128]{1,0:T(8,128)(2,1)S(1)}, u32[]{:S(2)}) copy-start(bf16[1040,128]{1,0:T(8,128)(2,1)S(1)} %collective-permute-done.13.refs_1_) | copy-start | bytes 798724
  10.0 27.9 %collective-permute-start.2 = (bf16[1040,128]{1,0:T(8,128)(2,1)}, bf16[1040,128]{1,0:T(8,128)(2,1)S(1)}, u32[]{:S(2)}, u32[]{:S(2)}) collective-permute-start(bf16[1040,128]{1,0:T(8,128)(2,1)} %get-tuple-element.37), channel_id=1, source_target_pairs={{0,3},{1,2},{2,1},{3,0},{4,7},{5,6},{6,5},{7,4},{8,11},{9,10},{10,... | collective-permute-start | bytes 798728 | tf_op jit(solution)/shard_map/ppermute | solution.py:26
  15.3 20.9 %copy-start.8 = (bf16[1040,128]{1,0:T(8,128)(2,1)}, bf16[1040,128]{1,0:T(8,128)(2,1)S(1)}, u32[]{:S(2)}) copy-start(bf16[1040,128]{1,0:T(8,128)(2,1)S(1)} %collective-permute-done.14.refs_2_) | copy-start | bytes 798724
  20.6 15.5 %copy-start.9 = (bf16[1040,128]{1,0:T(8,128)(2,1)}, bf16[1040,128]{1,0:T(8,128)(2,1)S(1)}, u32[]{:S(2)}) copy-start(bf16[1040,128]{1,0:T(8,128)(2,1)S(1)} %collective-permute-done.15.refs_3_) | copy-start | bytes 798724
  21.6 34.3 %collective-permute-start.16 = (bf16[3120,128]{1,0:T(8,128)(2,1)}, bf16[3120,128]{1,0:T(8,128)(2,1)S(1)}, u32[]{:S(2)}, u32[]{:S(2)}) collective-permute-start(bf16[3120,128]{1,0:T(8,128)(2,1)} %pad_maximum_fusion.1), channel_id=1, source_target_pairs={{0,4},{1,5},{2,6},{3,7},{4,8},{5,9},{6,10},{7,11},{8,12},{9,13},{1... | collective-permute-start | bytes 2396168 | tf_op jit(solution)/shard_map/ppermute | solution.py:21
  25.1 30.7 %collective-permute-start.3 = (bf16[2080,128]{1,0:T(8,128)(2,1)S(1)}, bf16[2080,128]{1,0:T(8,128)(2,1)S(1)}, u32[]{:S(2)}, u32[]{:S(2)}) collective-permute-start(bf16[2080,128]{1,0:T(8,128)(2,1)S(1)} %copy-done), channel_id=1, source_target_pairs={{0,4},{1,5},{2,6},{3,7},{4,8},{5,9},{6,10},{7,11},{8,12},{9,13},{1... | collective-permute-start | bytes 1597448 | tf_op jit(solution)/shard_map/ppermute | solution.py:21
  36.2 35.6 %copy-start.4 = (bf16[1040,128]{1,0:T(8,128)(2,1)}, bf16[1040,128]{1,0:T(8,128)(2,1)S(1)}, u32[]{:S(2)}) copy-start(bf16[1040,128]{1,0:T(8,128)(2,1)S(1)} %collective-permute-done.refs_1_) | copy-start | bytes 798724
  36.2 2.9 %collective-permute-start.17 = (bf16[1536,128]{1,0:T(8,128)(2,1)}, bf16[1536,128]{1,0:T(8,128)(2,1)}, u32[]{:S(2)}, u32[]{:S(2)}) collective-permute-start(bf16[1536,128]{1,0:T(8,128)(2,1)} %get-tuple-element.51), channel_id=1, source_target_pairs={{0,1},{1,0},{2,3},{3,2},{4,5},{5,4},{6,7},{7,6},{8,9},{9,8},{10,11... | collective-permute-start | bytes 1179656 | tf_op jit(solution)/shard_map/ppermute | solution.py:26
  36.4 35.4 %copy-start.5 = (bf16[1040,128]{1,0:T(8,128)(2,1)}, bf16[1040,128]{1,0:T(8,128)(2,1)S(1)}, u32[]{:S(2)}) copy-start(bf16[1040,128]{1,0:T(8,128)(2,1)S(1)} %collective-permute-done.1.refs_2_) | copy-start | bytes 798724
  36.4 12.2 %collective-permute-start.18 = (bf16[1536,128]{1,0:T(8,128)(2,1)}, bf16[1536,128]{1,0:T(8,128)(2,1)S(1)}, u32[]{:S(2)}, u32[]{:S(2)}) collective-permute-start(bf16[1536,128]{1,0:T(8,128)(2,1)} %get-tuple-element.52), channel_id=1, source_target_pairs={{0,2},{1,3},{2,0},{3,1},{4,6},{5,7},{6,4},{7,5},{8,10},{9,11},{10,... | collective-permute-start | bytes 1179656 | tf_op jit(solution)/shard_map/ppermute | solution.py:26
  37.9 33.9 %copy-start.6 = (bf16[1040,128]{1,0:T(8,128)(2,1)}, bf16[1040,128]{1,0:T(8,128)(2,1)S(1)}, u32[]{:S(2)}) copy-start(bf16[1040,128]{1,0:T(8,128)(2,1)S(1)} %collective-permute-done.2.refs_3_) | copy-start | bytes 798724
  37.9 17.9 %collective-permute-start.19 = (bf16[1536,128]{1,0:T(8,128)(2,1)}, bf16[1536,128]{1,0:T(8,128)(2,1)S(1)}, u32[]{:S(2)}, u32[]{:S(2)}) collective-permute-start(bf16[1536,128]{1,0:T(8,128)(2,1)} %get-tuple-element.53), channel_id=1, source_target_pairs={{0,3},{1,2},{2,1},{3,0},{4,7},{5,6},{6,5},{7,4},{8,11},{9,10},{10,... | collective-permute-start | bytes 1179656 | tf_op jit(solution)/shard_map/ppermute | solution.py:26
  39.1 53.7 %collective-permute-start.4 = (bf16[3120,128]{1,0:T(8,128)(2,1)}, bf16[3120,128]{1,0:T(8,128)(2,1)S(1)}, u32[]{:S(2)}, u32[]{:S(2)}) collective-permute-start(bf16[3120,128]{1,0:T(8,128)(2,1)} %pad_maximum_fusion), channel_id=1, source_target_pairs={{0,4},{1,5},{2,6},{3,7},{4,8},{5,9},{6,10},{7,11},{8,12},{9,13},{1... | collective-permute-start | bytes 2396168 | tf_op jit(solution)/shard_map/ppermute | solution.py:21
  48.6 7.3 %copy-start.18 = (bf16[1536,128]{1,0:T(8,128)(2,1)}, bf16[1536,128]{1,0:T(8,128)(2,1)S(1)}, u32[]{:S(2)}) copy-start(bf16[1536,128]{1,0:T(8,128)(2,1)S(1)} %collective-permute-done.18.refs_8_) | copy-start | bytes 1179652
  48.6 26.3 %collective-permute-start.5 = (bf16[1536,128]{1,0:T(8,128)(2,1)}, bf16[1536,128]{1,0:T(8,128)(2,1)}, u32[]{:S(2)}, u32[]{:S(2)}) collective-permute-start(bf16[1536,128]{1,0:T(8,128)(2,1)} %get-tuple-element.39), channel_id=1, source_target_pairs={{0,1},{1,0},{2,3},{3,2},{4,5},{5,4},{6,7},{7,6},{8,9},{9,8},{10,11... | collective-permute-start | bytes 1179656 | tf_op jit(solution)/shard_map/ppermute | solution.py:26
  55.8 1.0 copy-start.1
  71.8 38.7 %collective-permute-start.22 = (bf16[2048,128]{1,0:T(8,128)(2,1)}, bf16[2048,128]{1,0:T(8,128)(2,1)}, u32[]{:S(2)}, u32[]{:S(2)}) collective-permute-start(bf16[2048,128]{1,0:T(8,128)(2,1)} %get-tuple-element.58), channel_id=1, source_target_pairs={{4,0},{5,1},{6,2},{7,3},{8,4},{9,5},{10,6},{11,7},{12,8},{13,9},{1... | collective-permute-start | bytes 1572872 | tf_op jit(solution)/shard_map/ppermute | solution.py:21
  73.1 12.3 %collective-permute-start.6 = (bf16[1536,128]{1,0:T(8,128)(2,1)}, bf16[1536,128]{1,0:T(8,128)(2,1)S(1)}, u32[]{:S(2)}, u32[]{:S(2)}) collective-permute-start(bf16[1536,128]{1,0:T(8,128)(2,1)} %get-tuple-element.40), channel_id=1, source_target_pairs={{0,2},{1,3},{2,0},{3,1},{4,6},{5,7},{6,4},{7,5},{8,10},{9,11},{10,... | collective-permute-start | bytes 1179656 | tf_op jit(solution)/shard_map/ppermute | solution.py:26
  74.3 18.5 %collective-permute-start.7 = (bf16[1536,128]{1,0:T(8,128)(2,1)}, bf16[1536,128]{1,0:T(8,128)(2,1)}, u32[]{:S(2)}, u32[]{:S(2)}) collective-permute-start(bf16[1536,128]{1,0:T(8,128)(2,1)} %get-tuple-element.41), channel_id=1, source_target_pairs={{0,3},{1,2},{2,1},{3,0},{4,7},{5,6},{6,5},{7,4},{8,11},{9,10},{10,... | collective-permute-start | bytes 1179656 | tf_op jit(solution)/shard_map/ppermute | solution.py:26
  74.9 35.6 %copy-start.14 = (f32[1024,128]{1,0:T(8,128)S(1)}, f32[1024,128]{1,0:T(8,128)}, u32[]{:S(2)}) copy-start(f32[1024,128]{1,0:T(8,128)} %get-tuple-element.57) | copy-start | bytes 1572868
  74.9 35.6 %copy-start.15 = (f32[1024,128]{1,0:T(8,128)S(1)}, f32[1024,128]{1,0:T(8,128)}, u32[]{:S(2)}) copy-start(f32[1024,128]{1,0:T(8,128)} %get-tuple-element.59) | copy-start | bytes 1572868
  74.9 39.0 %collective-permute-start.20 = (bf16[2048,128]{1,0:T(8,128)(2,1)}, bf16[2048,128]{1,0:T(8,128)(2,1)S(1)}, u32[]{:S(2)}, u32[]{:S(2)}) collective-permute-start(bf16[2048,128]{1,0:T(8,128)(2,1)} %get-tuple-element.56), channel_id=1, source_target_pairs={{4,0},{5,1},{6,2},{7,3},{8,4},{9,5},{10,6},{11,7},{12,8},{13,9},{1... | collective-permute-start | bytes 1572872 | tf_op jit(solution)/shard_map/ppermute | solution.py:21
  85.3 7.4 %copy-start.20 = (bf16[1536,128]{1,0:T(8,128)(2,1)}, bf16[1536,128]{1,0:T(8,128)(2,1)S(1)}, u32[]{:S(2)}) copy-start(bf16[1536,128]{1,0:T(8,128)(2,1)S(1)} %collective-permute-done.6.refs_8_) | copy-start | bytes 1179652
  92.7 0.9 copy-start.10
  107.9 30.5 %collective-permute-start.10 = (bf16[2048,128]{1,0:T(8,128)(2,1)}, bf16[2048,128]{1,0:T(8,128)(2,1)S(1)}, u32[]{:S(2)}, u32[]{:S(2)}) collective-permute-start(bf16[2048,128]{1,0:T(8,128)(2,1)} %get-tuple-element.46), channel_id=1, source_target_pairs={{4,0},{5,1},{6,2},{7,3},{8,4},{9,5},{10,6},{11,7},{12,8},{13,9},{1... | collective-permute-start | bytes 1572872 | tf_op jit(solution)/shard_map/ppermute | solution.py:21
  109.2 40.1 %collective-permute-start.8 = (bf16[2048,128]{1,0:T(8,128)(2,1)}, bf16[2048,128]{1,0:T(8,128)(2,1)S(1)}, u32[]{:S(2)}, u32[]{:S(2)}) collective-permute-start(bf16[2048,128]{1,0:T(8,128)(2,1)} %get-tuple-element.44), channel_id=1, source_target_pairs={{4,0},{5,1},{6,2},{7,3},{8,4},{9,5},{10,6},{11,7},{12,8},{13,9},{1... | collective-permute-start | bytes 1572872 | tf_op jit(solution)/shard_map/ppermute | solution.py:21
  110.5 3.4 %copy-start.12 = (f32[1024,128]{1,0:T(8,128)S(1)}, f32[1024,128]{1,0:T(8,128)}, u32[]{:S(2)}) copy-start(f32[1024,128]{1,0:T(8,128)} %get-tuple-element.55) | copy-start | bytes 1572868
  111.8 26.7 %copy-start.16 = (f32[1024,128]{1,0:T(8,128)S(1)}, f32[1024,128]{1,0:T(8,128)}, u32[]{:S(2)}) copy-start(f32[1024,128]{1,0:T(8,128)} %get-tuple-element.45) | copy-start | bytes 1572868
  111.8 26.7 %copy-start.17 = (f32[1024,128]{1,0:T(8,128)S(1)}, f32[1024,128]{1,0:T(8,128)}, u32[]{:S(2)}) copy-start(f32[1024,128]{1,0:T(8,128)} %get-tuple-element.47) | copy-start | bytes 1572868
  111.8 38.0 %collective-permute-start.23 = (bf16[1024,128]{1,0:T(8,128)(2,1)S(1)}, bf16[1024,128]{1,0:T(8,128)(2,1)S(1)}, u32[]{:S(2)}, u32[]{:S(2)}) collective-permute-start(bf16[1024,128]{1,0:T(8,128)(2,1)S(1)} %get-tuple-element.65), channel_id=1, source_target_pairs={{0,2},{1,3},{2,0},{3,1},{4,6},{5,7},{6,4},{7,5},{8,10},{9,11},{10,... | collective-permute-start | bytes 786440 | tf_op jit(solution)/shard_map/ppermute | solution.py:26
  113.3 37.6 %collective-permute-start.24 = (bf16[1024,128]{1,0:T(8,128)(2,1)S(1)}, bf16[1024,128]{1,0:T(8,128)(2,1)S(1)}, u32[]{:S(2)}, u32[]{:S(2)}) collective-permute-start(bf16[1024,128]{1,0:T(8,128)(2,1)S(1)} %get-tuple-element.64), channel_id=1, source_target_pairs={{0,3},{1,2},{2,1},{3,0},{4,7},{5,6},{6,5},{7,4},{8,11},{9,10},{10,... | collective-permute-start | bytes 786440 | tf_op jit(solution)/shard_map/ppermute | solution.py:26
  113.9 24.7 %copy-start.2 = (bf16[2048,128]{1,0:T(8,128)(2,1)}, bf16[2048,128]{1,0:T(8,128)(2,1)S(1)}, u32[]{:S(2)}) copy-start(bf16[2048,128]{1,0:T(8,128)(2,1)S(1)} %collective-permute-done.20) | copy-start | bytes 1572868
  113.9 37.0 %collective-permute-start.21 = (bf16[1024,128]{1,0:T(8,128)(2,1)S(1)}, bf16[1024,128]{1,0:T(8,128)(2,1)S(1)}, u32[]{:S(2)}, u32[]{:S(2)}) collective-permute-start(bf16[1024,128]{1,0:T(8,128)(2,1)S(1)} %add_convert_fusion.2), channel_id=1, source_target_pairs={{0,1},{1,0},{2,3},{3,2},{4,5},{5,4},{6,7},{7,6},{8,9},{9,8},{10,11... | collective-permute-start | bytes 786440 | tf_op jit(solution)/shard_map/ppermute | solution.py:26
  138.4 11.3 %copy-start.13 = (f32[1024,128]{1,0:T(8,128)S(1)}, f32[1024,128]{1,0:T(8,128)}, u32[]{:S(2)}) copy-start(f32[1024,128]{1,0:T(8,128)} %get-tuple-element.43) | copy-start | bytes 1572868
  138.6 12.4 %collective-permute-start.11 = (bf16[1024,128]{1,0:T(8,128)(2,1)S(1)}, bf16[1024,128]{1,0:T(8,128)(2,1)S(1)}, u32[]{:S(2)}, u32[]{:S(2)}) collective-permute-start(bf16[1024,128]{1,0:T(8,128)(2,1)S(1)} %get-tuple-element.67), channel_id=1, source_target_pairs={{0,2},{1,3},{2,0},{3,1},{4,6},{5,7},{6,4},{7,5},{8,10},{9,11},{10,... | collective-permute-start | bytes 786440 | tf_op jit(solution)/shard_map/ppermute | solution.py:26
  149.3 8.5 %copy-start.3 = (bf16[2048,128]{1,0:T(8,128)(2,1)}, bf16[2048,128]{1,0:T(8,128)(2,1)S(1)}, u32[]{:S(2)}) copy-start(bf16[2048,128]{1,0:T(8,128)(2,1)S(1)} %collective-permute-done.8) | copy-start | bytes 1572868
  149.3 8.5 %collective-permute-start.12 = (bf16[1024,128]{1,0:T(8,128)(2,1)S(1)}, bf16[1024,128]{1,0:T(8,128)(2,1)S(1)}, u32[]{:S(2)}, u32[]{:S(2)}) collective-permute-start(bf16[1024,128]{1,0:T(8,128)(2,1)S(1)} %get-tuple-element.66), channel_id=1, source_target_pairs={{0,3},{1,2},{2,1},{3,0},{4,7},{5,6},{6,5},{7,4},{8,11},{9,10},{10,... | collective-permute-start | bytes 786440 | tf_op jit(solution)/shard_map/ppermute | solution.py:26
  149.8 8.0 %copy-start.21 = (bf16[1024,128]{1,0:T(8,128)(2,1)}, bf16[1024,128]{1,0:T(8,128)(2,1)S(1)}, u32[]{:S(2)}) copy-start(bf16[1024,128]{1,0:T(8,128)(2,1)S(1)} %collective-permute-done.23) | copy-start | bytes 786436
  149.8 8.0 %collective-permute-start.9 = (bf16[1024,128]{1,0:T(8,128)(2,1)S(1)}, bf16[1024,128]{1,0:T(8,128)(2,1)S(1)}, u32[]{:S(2)}, u32[]{:S(2)}) collective-permute-start(bf16[1024,128]{1,0:T(8,128)(2,1)S(1)} %add_convert_fusion.5), channel_id=1, source_target_pairs={{0,1},{1,0},{2,3},{3,2},{4,5},{5,4},{6,7},{7,6},{8,9},{9,8},{10,11... | collective-permute-start | bytes 786440 | tf_op jit(solution)/shard_map/ppermute | solution.py:26
  150.9 6.9 %copy-start.22 = (bf16[1024,128]{1,0:T(8,128)(2,1)}, bf16[1024,128]{1,0:T(8,128)(2,1)S(1)}, u32[]{:S(2)}) copy-start(bf16[1024,128]{1,0:T(8,128)(2,1)S(1)} %collective-permute-done.24) | copy-start | bytes 786436
  150.9 6.9 %copy-start.23 = (bf16[1024,128]{1,0:T(8,128)(2,1)}, bf16[1024,128]{1,0:T(8,128)(2,1)S(1)}, u32[]{:S(2)}) copy-start(bf16[1024,128]{1,0:T(8,128)(2,1)S(1)} %collective-permute-done.21) | copy-start | bytes 786436
  150.9 6.9 %copy-start.24 = (bf16[1024,128]{1,0:T(8,128)(2,1)}, bf16[1024,128]{1,0:T(8,128)(2,1)S(1)}, u32[]{:S(2)}) copy-start(bf16[1024,128]{1,0:T(8,128)(2,1)S(1)} %collective-permute-done.11) | copy-start | bytes 786436
  (4 other events, 3.1 us)

commit v4 on v3

--- a/solution.py
+++ b/solution.py
@@ -32,8 +32,11 @@
     length = outs[1].shape[0]
     me = lax.rem(lax.axis_index("ctx"), plane)
     for t, array in enumerate(refs[:arrays]):
-        rows, count, width = array.shape
-        wide[...] = array[...].astype(F32).reshape(rows * count, width)
+        rows, count, _ = array.shape
+        pitch = count + 1
+        values = array[...].astype(F32)
+        for r in range(rows):
+            wide[r * pitch : r * pitch + count, :] = values[r]
         for h in range(heads):
             for k in range(plane):
                 first = ((me ^ k) * heads + h) * group
@@ -41,7 +44,7 @@
                 for g in range(group):
                     at = (t * group + g) * rows + (h * length if k == 0 else 0)
                     out[at : at + rows, :] = wide[
-                        pl.ds(first + g, rows, stride=count), :
+                        pl.ds(first + g, rows, stride=pitch), :
                     ].astype(BF16)
     if group == 1:
         docs = seg[...].astype(F32)
@@ -65,7 +68,7 @@
         + [jax.ShapeDtypeStruct((length, width), BF16)] * pieces,
         in_specs=[vmem] * len(inputs),
         out_specs=[vmem] * (1 + pieces),
-        scratch_shapes=[pltpu.VMEM((rows * count, width), F32)],
+        scratch_shapes=[pltpu.VMEM((rows * (count + 1), width), F32)],
         name="pack",
     )(*inputs)
 
@@ -247,6 +250,7 @@
             pltpu.SMEM((2, blocks), F32),
             pltpu.SemaphoreType.DMA((15 * plane,)),
         ],
+        compiler_params=pltpu.CompilerParams(vmem_limit_bytes=32 << 20),
         name="attend",
     )(*own, *pairs, *queries)
     return results[:2], results[2:]
@@ -254,9 +258,11 @@
 
 def finish_kernel(plane, heads, *refs):
     pieces, returned = refs[: plane * heads], refs[plane * heads : plane * heads + heads]
-    outs = refs[-4:]
+    outs, wide = refs[-5:-1], refs[-1]
     me = lax.rem(lax.axis_index("ctx"), plane)
     rows = pieces[0].shape[1]
+    count = plane * heads
+    pitch = count + 1
     for h in range(heads):
         for k in range(plane):
             piece = pieces[h * plane + k]
@@ -265,7 +271,11 @@
                 value = piece[t].astype(F32)
                 if k == 0:
                     value = value + returned[h][t].astype(F32)
-                outs[t][pl.ds(head, rows, stride=plane * heads), :] = value
+                wide[t, pl.ds(head, rows, stride=pitch), :] = value
+    for t in range(4):
+        for r in range(rows):
+            at = slice(r * count, (r + 1) * count)
+            outs[t][at, :] = wide[t, r * pitch : r * pitch + count, :]
 
 
 def finish(pieces, returned, plane, heads):
@@ -280,6 +290,7 @@
         out_shape=[jax.ShapeDtypeStruct((rows * plane * heads, width), F32)] * 4,
         in_specs=[pl.BlockSpec((4, tile, width), lambda i: (0, i, 0))] * len(stacked),
         out_specs=[pl.BlockSpec((tile * plane * heads, width), lambda i: (i, 0))] * 4,
+        scratch_shapes=[pltpu.VMEM((4, tile * (plane * heads + 1), width), F32)],
         name="finish",
     )(*stacked)
 

time: 164 us -> 159 us (0.970)
  waiting for transfers between devices: 80.5 us -> 85.5 us
  Pallas kernels: 45.1 us -> 40.2 us
  other arithmetic: 3.34 us -> 1.36 us
  local copies, waits for them, and re-layouts: 3.33 us -> 1.6 us
    ppermute x7, waiting for transfers between devices: 33.4 us -> 38.3 us  [shifted(): return lax.ppermute(block, 'ctx', route)]
    pallas_call x2, Pallas kernels: 11.7 us -> 7.95 us  [pack(): pl.pallas_call(functools.partial(pack_kernel, plane, heads, group, len(ar...]
    unnamed x54 -> x30, local copies, waits for them, and re-layouts: 3.33 us -> 1.6 us
  transfers between devices with their start and end apart: 25 -> 25, of which waited for: 9 -> 10; matrix products, arithmetic and copies ran while one was open for 2% -> 1% of each run, Pallas kernels for 22% -> 20%
where the time goes in v4:
time: 159 us
  waiting for transfers between devices  85.5 us (54%)
  Pallas kernels  40.2 us (25%)
  starting transfers between devices  29.2 us (18%)
  local copies, waits for them, and re-layouts  1.6 us (1%)
    ppermute x18, waiting for transfers between devices, swapped(): return lax.ppermute(block, 'ctx', [(i, i ^ partner) for i in devices])  47.3 us
    ppermute x7, waiting for transfers between devices, shifted(): return lax.ppermute(block, 'ctx', route)  38.3 us
    pallas_call x2, Pallas kernels, attend(): pl.pallas_call(functools.partial(attend_kernel, plane, group, rows, width...  27.8 us
    ppermute x7, starting transfers between devices, shifted(): return lax.ppermute(block, 'ctx', route)  15.6 us
    ppermute x18, starting transfers between devices, swapped(): return lax.ppermute(block, 'ctx', [(i, i ^ partner) for i in devices])  13.5 us
    pallas_call x2, Pallas kernels, pack(): pl.pallas_call(functools.partial(pack_kernel, plane, heads, group, len(ar...  7.95 us
    pallas_call x1, Pallas kernels, finish(): pl.pallas_call(functools.partial(finish_kernel, plane, heads), grid=(step...  4.5 us
  transfers between devices with their start and end apart: 25, of which 10 were waited for; matrix products, arithmetic and copies ran while one was open for 1% of the time, Pallas kernels for 20%

profile of v4, /device:TPU:0, one launch (start us, length us, event | category | flops | bytes accessed | tf_op | source)
XLA Modules:
  0.0 158.8 jit_solution(7393273076254392204)
XLA Ops:
  0.6 3.5 %pack.2 = (bf16[2080,128]{1,0:T(8,128)(2,1)}, bf16[1040,128]{1,0:T(8,128)(2,1)}, bf16[1040,128]{1,0:T(8,128)(2,1)}, bf16[1040,128]{1,0:T(8,128)(2,1)}, bf16[1040...) custom-call(bf16[256,8,128]{2,1,0:T(8,128)(2,1)} %refs_0_.2, bf16[256,8,128]{2,1,0:T(8,128)(2,1)} %refs_1_.2, ...), custom_call_target="tpu_custom_call" | custom-call | tf_op jit(solution)/shard_map/pack/pallas_call | solution.py:65
  4.2 0.5 collective-permute-start.13
  4.6 2.6 %collective-permute-start.14 = (bf16[1040,128]{1,0:T(8,128)(2,1)}, bf16[1040,128]{1,0:T(8,128)(2,1)S(1)}, u32[]{:S(2)}, u32[]{:S(2)}) collective-permute-start(bf16[1040,128]{1,0:T(8,128)(2,1)} %get-tuple-element.49), channel_id=1, source_target_pairs={{0,2},{1,3},{2,0},{3,1},{4,6},{5,7},{6,4},{7,5},{8,10},{9,11},{10,... | collective-permute-start | bytes 798728 | tf_op jit(solution)/shard_map/ppermute | solution.py:26
  7.2 0.0 collective-permute-start.15
  7.3 0.1 collective-permute-start
  7.4 1.9 %collective-permute-start.1 = (bf16[1040,128]{1,0:T(8,128)(2,1)}, bf16[1040,128]{1,0:T(8,128)(2,1)S(1)}, u32[]{:S(2)}, u32[]{:S(2)}) collective-permute-start(bf16[1040,128]{1,0:T(8,128)(2,1)} %get-tuple-element.36), channel_id=1, source_target_pairs={{0,2},{1,3},{2,0},{3,1},{4,6},{5,7},{6,4},{7,5},{8,10},{9,11},{10,... | collective-permute-start | bytes 798728 | tf_op jit(solution)/shard_map/ppermute | solution.py:26
  9.4 5.3 %collective-permute-done.14.refs_2_ = bf16[1040,128]{1,0:T(8,128)(2,1)S(1)} collective-permute-done((bf16[1040,128]{1,0:T(8,128)(2,1)}, bf16[1040,128]{1,0:T(8,128)(2,1)S(1)}, u32[]{:S(2)}, u32[]{:S(2)}) %collective-permute-start.14) | collective-permute-done | bytes 266272 | tf_op jit(solution)/shard_map/ppermute | solution.py:26
  14.7 5.3 %collective-permute-done.15.refs_3_ = bf16[1040,128]{1,0:T(8,128)(2,1)S(1)} collective-permute-done((bf16[1040,128]{1,0:T(8,128)(2,1)}, bf16[1040,128]{1,0:T(8,128)(2,1)S(1)}, u32[]{:S(2)}, u32[]{:S(2)}) %collective-permute-start.15) | collective-permute-done | bytes 266272 | tf_op jit(solution)/shard_map/ppermute | solution.py:26
  20.0 0.9 pad_maximum_fusion.1
  21.0 3.5 %collective-permute-start.16 = (bf16[3120,128]{1,0:T(8,128)(2,1)}, bf16[3120,128]{1,0:T(8,128)(2,1)S(1)}, u32[]{:S(2)}, u32[]{:S(2)}) collective-permute-start(bf16[3120,128]{1,0:T(8,128)(2,1)} %pad_maximum_fusion.1), channel_id=1, source_target_pairs={{0,4},{1,5},{2,6},{3,7},{4,8},{5,9},{6,10},{7,11},{8,12},{9,13},{1... | collective-permute-start | bytes 2396168 | tf_op jit(solution)/shard_map/ppermute | solution.py:21
  24.5 3.5 %collective-permute-start.3 = (bf16[2080,128]{1,0:T(8,128)(2,1)S(1)}, bf16[2080,128]{1,0:T(8,128)(2,1)S(1)}, u32[]{:S(2)}, u32[]{:S(2)}) collective-permute-start(bf16[2080,128]{1,0:T(8,128)(2,1)S(1)} %copy-done.1), channel_id=1, source_target_pairs={{0,4},{1,5},{2,6},{3,7},{4,8},{5,9},{6,10},{7,11},{8,12},{9,13},{1... | collective-permute-start | bytes 1597448 | tf_op jit(solution)/shard_map/ppermute | solution.py:21
  28.0 4.4 %pack.3 = (bf16[3072,128]{1,0:T(8,128)(2,1)}, bf16[1536,128]{1,0:T(8,128)(2,1)}, bf16[1536,128]{1,0:T(8,128)(2,1)}, bf16[1536,128]{1,0:T(8,128)(2,1)}, bf16[1536...) custom-call(bf16[256,16,128]{2,1,0:T(8,128)(2,1)} %refs_0_.3, ...), custom_call_target="tpu_custom_call" | custom-call | tf_op jit(solution)/shard_map/pack/pallas_call | solution.py:65
  32.4 0.2 collective-permute-start.17
  32.6 0.0 collective-permute-done.1.refs_2_
  32.6 1.5 collective-permute-start.18
  34.1 0.2 collective-permute-start.19
  34.3 0.1 pad_maximum_fusion
  34.4 0.0 collective-permute-done.17.refs_7_
  34.4 3.5 %collective-permute-start.4 = (bf16[3120,128]{1,0:T(8,128)(2,1)S(1)}, bf16[3120,128]{1,0:T(8,128)(2,1)S(1)}, u32[]{:S(2)}, u32[]{:S(2)}) collective-permute-start(bf16[3120,128]{1,0:T(8,128)(2,1)S(1)} %pad_maximum_fusion), channel_id=1, source_target_pairs={{0,4},{1,5},{2,6},{3,7},{4,8},{5,9},{6,10},{7,11},{8,12},{9,13},{1... | collective-permute-start | bytes 2396168 | tf_op jit(solution)/shard_map/ppermute | solution.py:21
  37.9 6.9 %collective-permute-done.18.refs_8_ = bf16[1536,128]{1,0:T(8,128)(2,1)S(1)} collective-permute-done((bf16[1536,128]{1,0:T(8,128)(2,1)}, bf16[1536,128]{1,0:T(8,128)(2,1)S(1)}, u32[]{:S(2)}, u32[]{:S(2)}) %collective-permute-start.18) | collective-permute-done | bytes 393248 | tf_op jit(solution)/shard_map/ppermute | solution.py:26
  44.8 7.3 %collective-permute-done.19.refs_9_ = bf16[1536,128]{1,0:T(8,128)(2,1)S(1)} collective-permute-done((bf16[1536,128]{1,0:T(8,128)(2,1)}, bf16[1536,128]{1,0:T(8,128)(2,1)S(1)}, u32[]{:S(2)}, u32[]{:S(2)}) %collective-permute-start.19) | collective-permute-done | bytes 393248 | tf_op jit(solution)/shard_map/ppermute | solution.py:26
  52.1 2.2 %collective-permute-done.3.refs_4_ = bf16[2080,128]{1,0:T(8,128)(2,1)S(1)} collective-permute-done((bf16[2080,128]{1,0:T(8,128)(2,1)S(1)}, bf16[2080,128]{1,0:T(8,128)(2,1)S(1)}, u32[]{:S(2)}, u32[]{:S(2)}) %collective-permute-start.3) | collective-permute-done | bytes 532512 | tf_op jit(solution)/shard_map/ppermute | solution.py:21
  54.3 13.9 %attend.3 = (bf16[2048,128]{1,0:T(8,128)(2,1)S(1)}, bf16[2048,128]{1,0:T(8,128)(2,1)S(1)}, f32[1024,128]{1,0:T(8,128)S(1)}, f32[1024,128]{1,0:T(8,128)S(1)}, f32...) custom-call(bf16[2080,128]{1,0:T(8,128)(2,1)S(1)} %copy-done.1, bf16[1040,128]{1,0:T(8,128)(2,1)S(1)} %collective-permute-done.13.refs_1_, ...), custom_call_target="tpu_custom_call" | custom-call | tf_op jit(solution)/shard_map/attend/pallas_call | solution.py:229
  68.2 0.8 copy-done.2
  69.0 1.3 collective-permute-start.22
  70.3 1.4 collective-permute-start.6
  71.6 1.3 collective-permute-start.20
  72.9 9.4 %collective-permute-done.6.refs_8_ = bf16[1536,128]{1,0:T(8,128)(2,1)S(1)} collective-permute-done((bf16[1536,128]{1,0:T(8,128)(2,1)S(1)}, bf16[1536,128]{1,0:T(8,128)(2,1)S(1)}, u32[]{:S(2)}, u32[]{:S(2)}) %collective-permute-start.6) | collective-permute-done | bytes 393248 | tf_op jit(solution)/shard_map/ppermute | solution.py:26
  82.3 6.2 %collective-permute-done.7.refs_9_ = bf16[1536,128]{1,0:T(8,128)(2,1)S(1)} collective-permute-done((bf16[1536,128]{1,0:T(8,128)(2,1)S(1)}, bf16[1536,128]{1,0:T(8,128)(2,1)S(1)}, u32[]{:S(2)}, u32[]{:S(2)}) %collective-permute-start.7) | collective-permute-done | bytes 393248 | tf_op jit(solution)/shard_map/ppermute | solution.py:26
  88.5 13.9 %attend.2 = (bf16[2048,128]{1,0:T(8,128)(2,1)S(1)}, bf16[2048,128]{1,0:T(8,128)(2,1)S(1)}, f32[1024,128]{1,0:T(8,128)S(1)}, f32[1024,128]{1,0:T(8,128)S(1)}, f32...) custom-call(bf16[2080,128]{1,0:T(8,128)(2,1)S(1)} %copy-done.1, bf16[1040,128]{1,0:T(8,128)(2,1)S(1)} %collective-permute-done.refs_1_, ...), custom_call_target="tpu_custom_call" | custom-call | tf_op jit(solution)/shard_map/attend/pallas_call | solution.py:229
  102.4 1.3 collective-permute-start.10
  103.7 1.3 collective-permute-start.8
  105.0 0.1 add_convert_fusion
  105.1 1.5 collective-permute-start.23
  106.6 0.9 collective-permute-start.24
  107.5 0.1 add_convert_fusion.2
  107.6 0.1 collective-permute-start.21
  107.7 26.2 %collective-permute-done.10 = bf16[2048,128]{1,0:T(8,128)(2,1)S(1)} collective-permute-done((bf16[2048,128]{1,0:T(8,128)(2,1)S(1)}, bf16[2048,128]{1,0:T(8,128)(2,1)S(1)}, u32[]{:S(2)}, u32[]{:S(2)}) %collective-permute-start.10) | collective-permute-done | bytes 524320 | tf_op jit(solution)/shard_map/ppermute | solution.py:21
  133.9 0.1 add_convert_fusion.3
  134.1 1.2 collective-permute-start.11
  135.3 9.9 %collective-permute-done.8 = bf16[2048,128]{1,0:T(8,128)(2,1)S(1)} collective-permute-done((bf16[2048,128]{1,0:T(8,128)(2,1)S(1)}, bf16[2048,128]{1,0:T(8,128)(2,1)S(1)}, u32[]{:S(2)}, u32[]{:S(2)}) %collective-permute-start.8) | collective-permute-done | bytes 524320 | tf_op jit(solution)/shard_map/ppermute | solution.py:21
  145.2 1.0 collective-permute-start.12
  146.2 0.1 add_convert_fusion.5
  146.3 0.3 collective-permute-start.9
  146.6 6.8 %collective-permute-done.12 = bf16[1024,128]{1,0:T(8,128)(2,1)S(1)} collective-permute-done((bf16[1024,128]{1,0:T(8,128)(2,1)S(1)}, bf16[1024,128]{1,0:T(8,128)(2,1)S(1)}, u32[]{:S(2)}, u32[]{:S(2)}) %collective-permute-start.12) | collective-permute-done | bytes 262176 | tf_op jit(solution)/shard_map/ppermute | solution.py:26
  153.5 0.6 copy-done.10
  154.2 0.1 copy-done.11
  154.3 4.5 %finish.1 = (f32[2048,128]{1,0:T(8,128)}, f32[2048,128]{1,0:T(8,128)}, f32[2048,128]{1,0:T(8,128)}, f32[2048,128]{1,0:T(8,128)}) custom-call(f32[4,256,128]{2,1,0:T(8,128)} %bitcast.16, bf16[4,256,128]{2,1,0:T(8,128)(2,1)} %bitcast.24, bf16[4,256,128]{2,1,0:T(8,128)(2,1)} %bitcast.22, bf16[4,256,128]{2,1,0:T(8,128)(2,1)} %bitcast.23, ...), custom_call_target="tpu_custom_call" | custom-call | tf_op jit(solution)/shard_map/finish/pallas_call | solution.py:287
  (43 shorter events, 0.1 us)
Async XLA Ops:
  4.2 20.3 %copy-start.1 = (bf16[2080,128]{1,0:T(8,128)(2,1)S(1)}, bf16[2080,128]{1,0:T(8,128)(2,1)}, u32[]{:S(2)}) copy-start(bf16[2080,128]{1,0:T(8,128)(2,1)} %get-tuple-element.34.refs_0_) | copy-start | bytes 1597444
  4.2 5.2 %collective-permute-start.13 = (bf16[1040,128]{1,0:T(8,128)(2,1)}, bf16[1040,128]{1,0:T(8,128)(2,1)S(1)}, u32[]{:S(2)}, u32[]{:S(2)}) collective-permute-start(bf16[1040,128]{1,0:T(8,128)(2,1)} %get-tuple-element.48), channel_id=1, source_target_pairs={{0,1},{1,0},{2,3},{3,2},{4,5},{5,4},{6,7},{7,6},{8,9},{9,8},{10,11... | collective-permute-start | bytes 798728 | tf_op jit(solution)/shard_map/ppermute | solution.py:26
  4.6 10.0 %collective-permute-start.14 = (bf16[1040,128]{1,0:T(8,128)(2,1)}, bf16[1040,128]{1,0:T(8,128)(2,1)S(1)}, u32[]{:S(2)}, u32[]{:S(2)}) collective-permute-start(bf16[1040,128]{1,0:T(8,128)(2,1)} %get-tuple-element.49), channel_id=1, source_target_pairs={{0,2},{1,3},{2,0},{3,1},{4,6},{5,7},{6,4},{7,5},{8,10},{9,11},{10,... | collective-permute-start | bytes 798728 | tf_op jit(solution)/shard_map/ppermute | solution.py:26
  7.2 12.8 %collective-permute-start.15 = (bf16[1040,128]{1,0:T(8,128)(2,1)}, bf16[1040,128]{1,0:T(8,128)(2,1)S(1)}, u32[]{:S(2)}, u32[]{:S(2)}) collective-permute-start(bf16[1040,128]{1,0:T(8,128)(2,1)} %get-tuple-element.50), channel_id=1, source_target_pairs={{0,3},{1,2},{2,1},{3,0},{4,7},{5,6},{6,5},{7,4},{8,11},{9,10},{10,... | collective-permute-start | bytes 798728 | tf_op jit(solution)/shard_map/ppermute | solution.py:26
  7.3 25.1 %collective-permute-start = (bf16[1040,128]{1,0:T(8,128)(2,1)}, bf16[1040,128]{1,0:T(8,128)(2,1)S(1)}, u32[]{:S(2)}, u32[]{:S(2)}) collective-permute-start(bf16[1040,128]{1,0:T(8,128)(2,1)} %get-tuple-element.35), channel_id=1, source_target_pairs={{0,1},{1,0},{2,3},{3,2},{4,5},{5,4},{6,7},{7,6},{8,9},{9,8},{10,11... | collective-permute-start | bytes 798728 | tf_op jit(solution)/shard_map/ppermute | solution.py:26
  7.4 25.2 %collective-permute-start.1 = (bf16[1040,128]{1,0:T(8,128)(2,1)}, bf16[1040,128]{1,0:T(8,128)(2,1)S(1)}, u32[]{:S(2)}, u32[]{:S(2)}) collective-permute-start(bf16[1040,128]{1,0:T(8,128)(2,1)} %get-tuple-element.36), channel_id=1, source_target_pairs={{0,2},{1,3},{2,0},{3,1},{4,6},{5,7},{6,4},{7,5},{8,10},{9,11},{10,... | collective-permute-start | bytes 798728 | tf_op jit(solution)/shard_map/ppermute | solution.py:26
  9.4 24.8 %collective-permute-start.2 = (bf16[1040,128]{1,0:T(8,128)(2,1)}, bf16[1040,128]{1,0:T(8,128)(2,1)S(1)}, u32[]{:S(2)}, u32[]{:S(2)}) collective-permute-start(bf16[1040,128]{1,0:T(8,128)(2,1)} %get-tuple-element.37), channel_id=1, source_target_pairs={{0,3},{1,2},{2,1},{3,0},{4,7},{5,6},{6,5},{7,4},{8,11},{9,10},{10,... | collective-permute-start | bytes 798728 | tf_op jit(solution)/shard_map/ppermute | solution.py:26
  21.0 33.3 %collective-permute-start.16 = (bf16[3120,128]{1,0:T(8,128)(2,1)}, bf16[3120,128]{1,0:T(8,128)(2,1)S(1)}, u32[]{:S(2)}, u32[]{:S(2)}) collective-permute-start(bf16[3120,128]{1,0:T(8,128)(2,1)} %pad_maximum_fusion.1), channel_id=1, source_target_pairs={{0,4},{1,5},{2,6},{3,7},{4,8},{5,9},{6,10},{7,11},{8,12},{9,13},{1... | collective-permute-start | bytes 2396168 | tf_op jit(solution)/shard_map/ppermute | solution.py:21
  24.5 29.7 %collective-permute-start.3 = (bf16[2080,128]{1,0:T(8,128)(2,1)S(1)}, bf16[2080,128]{1,0:T(8,128)(2,1)S(1)}, u32[]{:S(2)}, u32[]{:S(2)}) collective-permute-start(bf16[2080,128]{1,0:T(8,128)(2,1)S(1)} %copy-done.1), channel_id=1, source_target_pairs={{0,4},{1,5},{2,6},{3,7},{4,8},{5,9},{6,10},{7,11},{8,12},{9,13},{1... | collective-permute-start | bytes 1597448 | tf_op jit(solution)/shard_map/ppermute | solution.py:21
  32.4 12.4 %copy-start.14 = (bf16[1536,128]{1,0:T(8,128)(2,1)S(1)}, bf16[1536,128]{1,0:T(8,128)(2,1)}, u32[]{:S(2)}) copy-start(bf16[1536,128]{1,0:T(8,128)(2,1)} %get-tuple-element.39) | copy-start | bytes 1179652
  32.4 21.8 %copy-start = (bf16[3072,128]{1,0:T(8,128)(2,1)S(1)}, bf16[3072,128]{1,0:T(8,128)(2,1)}, u32[]{:S(2)}) copy-start(bf16[3072,128]{1,0:T(8,128)(2,1)} %get-tuple-element.38.refs_6_) | copy-start | bytes 2359300
  32.4 2.0 %collective-permute-start.17 = (bf16[1536,128]{1,0:T(8,128)(2,1)}, bf16[1536,128]{1,0:T(8,128)(2,1)S(1)}, u32[]{:S(2)}, u32[]{:S(2)}) collective-permute-start(bf16[1536,128]{1,0:T(8,128)(2,1)} %get-tuple-element.51), channel_id=1, source_target_pairs={{0,1},{1,0},{2,3},{3,2},{4,5},{5,4},{6,7},{7,6},{8,9},{9,8},{10,11... | collective-permute-start | bytes 1179656 | tf_op jit(solution)/shard_map/ppermute | solution.py:26
  32.6 12.2 %collective-permute-start.18 = (bf16[1536,128]{1,0:T(8,128)(2,1)}, bf16[1536,128]{1,0:T(8,128)(2,1)S(1)}, u32[]{:S(2)}, u32[]{:S(2)}) collective-permute-start(bf16[1536,128]{1,0:T(8,128)(2,1)} %get-tuple-element.52), channel_id=1, source_target_pairs={{0,2},{1,3},{2,0},{3,1},{4,6},{5,7},{6,4},{7,5},{8,10},{9,11},{10,... | collective-permute-start | bytes 1179656 | tf_op jit(solution)/shard_map/ppermute | solution.py:26
  34.1 18.0 %collective-permute-start.19 = (bf16[1536,128]{1,0:T(8,128)(2,1)}, bf16[1536,128]{1,0:T(8,128)(2,1)S(1)}, u32[]{:S(2)}, u32[]{:S(2)}) collective-permute-start(bf16[1536,128]{1,0:T(8,128)(2,1)} %get-tuple-element.53), channel_id=1, source_target_pairs={{0,3},{1,2},{2,1},{3,0},{4,7},{5,6},{6,5},{7,4},{8,11},{9,10},{10,... | collective-permute-start | bytes 1179656 | tf_op jit(solution)/shard_map/ppermute | solution.py:26
  34.4 54.1 %collective-permute-start.4 = (bf16[3120,128]{1,0:T(8,128)(2,1)S(1)}, bf16[3120,128]{1,0:T(8,128)(2,1)S(1)}, u32[]{:S(2)}, u32[]{:S(2)}) collective-permute-start(bf16[3120,128]{1,0:T(8,128)(2,1)S(1)} %pad_maximum_fusion), channel_id=1, source_target_pairs={{0,4},{1,5},{2,6},{3,7},{4,8},{5,9},{6,10},{7,11},{8,12},{9,13},{1... | collective-permute-start | bytes 2396168 | tf_op jit(solution)/shard_map/ppermute | solution.py:21
  44.8 26.8 %collective-permute-start.5 = (bf16[1536,128]{1,0:T(8,128)(2,1)S(1)}, bf16[1536,128]{1,0:T(8,128)(2,1)S(1)}, u32[]{:S(2)}, u32[]{:S(2)}) collective-permute-start(bf16[1536,128]{1,0:T(8,128)(2,1)S(1)} %copy-done.14), channel_id=1, source_target_pairs={{0,1},{1,0},{2,3},{3,2},{4,5},{5,4},{6,7},{7,6},{8,9},{9,8},{10,11... | collective-permute-start | bytes 1179656 | tf_op jit(solution)/shard_map/ppermute | solution.py:26
  54.2 16.0 %copy-start.13 = (bf16[1536,128]{1,0:T(8,128)(2,1)S(1)}, bf16[1536,128]{1,0:T(8,128)(2,1)}, u32[]{:S(2)}) copy-start(bf16[1536,128]{1,0:T(8,128)(2,1)} %get-tuple-element.40) | copy-start | bytes 1179652
  54.2 17.4 %copy-start.12 = (bf16[1536,128]{1,0:T(8,128)(2,1)S(1)}, bf16[1536,128]{1,0:T(8,128)(2,1)}, u32[]{:S(2)}) copy-start(bf16[1536,128]{1,0:T(8,128)(2,1)} %get-tuple-element.41) | copy-start | bytes 1179652
  68.1 0.8 copy-start.2
  69.0 36.1 %collective-permute-start.22 = (bf16[2048,128]{1,0:T(8,128)(2,1)S(1)}, bf16[2048,128]{1,0:T(8,128)(2,1)S(1)}, u32[]{:S(2)}, u32[]{:S(2)}) collective-permute-start(bf16[2048,128]{1,0:T(8,128)(2,1)S(1)} %get-tuple-element.58), channel_id=1, source_target_pairs={{4,0},{5,1},{6,2},{7,3},{8,4},{9,5},{10,6},{11,7},{12,8},{13,9},{1... | collective-permute-start | bytes 1572872 | tf_op jit(solution)/shard_map/ppermute | solution.py:21
  70.3 12.1 %collective-permute-start.6 = (bf16[1536,128]{1,0:T(8,128)(2,1)S(1)}, bf16[1536,128]{1,0:T(8,128)(2,1)S(1)}, u32[]{:S(2)}, u32[]{:S(2)}) collective-permute-start(bf16[1536,128]{1,0:T(8,128)(2,1)S(1)} %copy-done.13), channel_id=1, source_target_pairs={{0,2},{1,3},{2,0},{3,1},{4,6},{5,7},{6,4},{7,5},{8,10},{9,11},{10,... | collective-permute-start | bytes 1179656 | tf_op jit(solution)/shard_map/ppermute | solution.py:26
  71.6 16.9 %collective-permute-start.7 = (bf16[1536,128]{1,0:T(8,128)(2,1)S(1)}, bf16[1536,128]{1,0:T(8,128)(2,1)S(1)}, u32[]{:S(2)}, u32[]{:S(2)}) collective-permute-start(bf16[1536,128]{1,0:T(8,128)(2,1)S(1)} %copy-done.12), channel_id=1, source_target_pairs={{0,3},{1,2},{2,1},{3,0},{4,7},{5,6},{6,5},{7,4},{8,11},{9,10},{10,... | collective-permute-start | bytes 1179656 | tf_op jit(solution)/shard_map/ppermute | solution.py:26
  71.6 35.9 %collective-permute-start.20 = (bf16[2048,128]{1,0:T(8,128)(2,1)S(1)}, bf16[2048,128]{1,0:T(8,128)(2,1)S(1)}, u32[]{:S(2)}, u32[]{:S(2)}) collective-permute-start(bf16[2048,128]{1,0:T(8,128)(2,1)S(1)} %get-tuple-element.56), channel_id=1, source_target_pairs={{4,0},{5,1},{6,2},{7,3},{8,4},{9,5},{10,6},{11,7},{12,8},{13,9},{1... | collective-permute-start | bytes 1572872 | tf_op jit(solution)/shard_map/ppermute | solution.py:21
  102.4 2.7 %copy-start.3 = (f32[1024,128]{1,0:T(8,128)}, f32[1024,128]{1,0:T(8,128)S(1)}, u32[]{:S(2)}) copy-start(f32[1024,128]{1,0:T(8,128)S(1)} %get-tuple-element.42) | copy-start | bytes 1572868
  102.4 31.5 %collective-permute-start.10 = (bf16[2048,128]{1,0:T(8,128)(2,1)S(1)}, bf16[2048,128]{1,0:T(8,128)(2,1)S(1)}, u32[]{:S(2)}, u32[]{:S(2)}) collective-permute-start(bf16[2048,128]{1,0:T(8,128)(2,1)S(1)} %get-tuple-element.46), channel_id=1, source_target_pairs={{4,0},{5,1},{6,2},{7,3},{8,4},{9,5},{10,6},{11,7},{12,8},{13,9},{1... | collective-permute-start | bytes 1572872 | tf_op jit(solution)/shard_map/ppermute | solution.py:21
  103.7 41.4 %collective-permute-start.8 = (bf16[2048,128]{1,0:T(8,128)(2,1)S(1)}, bf16[2048,128]{1,0:T(8,128)(2,1)S(1)}, u32[]{:S(2)}, u32[]{:S(2)}) collective-permute-start(bf16[2048,128]{1,0:T(8,128)(2,1)S(1)} %get-tuple-element.44), channel_id=1, source_target_pairs={{4,0},{5,1},{6,2},{7,3},{8,4},{9,5},{10,6},{11,7},{12,8},{13,9},{1... | collective-permute-start | bytes 1572872 | tf_op jit(solution)/shard_map/ppermute | solution.py:21
  105.1 41.1 %collective-permute-start.23 = (bf16[1024,128]{1,0:T(8,128)(2,1)S(1)}, bf16[1024,128]{1,0:T(8,128)(2,1)S(1)}, u32[]{:S(2)}, u32[]{:S(2)}) collective-permute-start(bf16[1024,128]{1,0:T(8,128)(2,1)S(1)} %get-tuple-element.65), channel_id=1, source_target_pairs={{0,2},{1,3},{2,0},{3,1},{4,6},{5,7},{6,4},{7,5},{8,10},{9,11},{10,... | collective-permute-start | bytes 786440 | tf_op jit(solution)/shard_map/ppermute | solution.py:26
  106.6 39.9 %collective-permute-start.24 = (bf16[1024,128]{1,0:T(8,128)(2,1)S(1)}, bf16[1024,128]{1,0:T(8,128)(2,1)S(1)}, u32[]{:S(2)}, u32[]{:S(2)}) collective-permute-start(bf16[1024,128]{1,0:T(8,128)(2,1)S(1)} %get-tuple-element.64), channel_id=1, source_target_pairs={{0,3},{1,2},{2,1},{3,0},{4,7},{5,6},{6,5},{7,4},{8,11},{9,10},{10,... | collective-permute-start | bytes 786440 | tf_op jit(solution)/shard_map/ppermute | solution.py:26
  107.5 26.6 %copy-start.4 = (bf16[2048,128]{1,0:T(8,128)(2,1)}, bf16[2048,128]{1,0:T(8,128)(2,1)S(1)}, u32[]{:S(2)}) copy-start(bf16[2048,128]{1,0:T(8,128)(2,1)S(1)} %collective-permute-done.20) | copy-start | bytes 1572868
  107.6 39.0 %collective-permute-start.21 = (bf16[1024,128]{1,0:T(8,128)(2,1)S(1)}, bf16[1024,128]{1,0:T(8,128)(2,1)S(1)}, u32[]{:S(2)}, u32[]{:S(2)}) collective-permute-start(bf16[1024,128]{1,0:T(8,128)(2,1)S(1)} %add_convert_fusion.2), channel_id=1, source_target_pairs={{0,1},{1,0},{2,3},{3,2},{4,5},{5,4},{6,7},{7,6},{8,9},{9,8},{10,11... | collective-permute-start | bytes 786440 | tf_op jit(solution)/shard_map/ppermute | solution.py:26
  134.1 12.5 %collective-permute-start.11 = (bf16[1024,128]{1,0:T(8,128)(2,1)S(1)}, bf16[1024,128]{1,0:T(8,128)(2,1)S(1)}, u32[]{:S(2)}, u32[]{:S(2)}) collective-permute-start(bf16[1024,128]{1,0:T(8,128)(2,1)S(1)} %get-tuple-element.67), channel_id=1, source_target_pairs={{0,2},{1,3},{2,0},{3,1},{4,6},{5,7},{6,4},{7,5},{8,10},{9,11},{10,... | collective-permute-start | bytes 786440 | tf_op jit(solution)/shard_map/ppermute | solution.py:26
  145.2 8.3 %copy-start.5 = (bf16[2048,128]{1,0:T(8,128)(2,1)}, bf16[2048,128]{1,0:T(8,128)(2,1)S(1)}, u32[]{:S(2)}) copy-start(bf16[2048,128]{1,0:T(8,128)(2,1)S(1)} %collective-permute-done.8) | copy-start | bytes 1572868
  145.2 8.3 %collective-permute-start.12 = (bf16[1024,128]{1,0:T(8,128)(2,1)S(1)}, bf16[1024,128]{1,0:T(8,128)(2,1)S(1)}, u32[]{:S(2)}, u32[]{:S(2)}) collective-permute-start(bf16[1024,128]{1,0:T(8,128)(2,1)S(1)} %get-tuple-element.66), channel_id=1, source_target_pairs={{0,3},{1,2},{2,1},{3,0},{4,7},{5,6},{6,5},{7,4},{8,11},{9,10},{10,... | collective-permute-start | bytes 786440 | tf_op jit(solution)/shard_map/ppermute | solution.py:26
  146.2 7.2 %copy-start.6 = (bf16[1024,128]{1,0:T(8,128)(2,1)}, bf16[1024,128]{1,0:T(8,128)(2,1)S(1)}, u32[]{:S(2)}) copy-start(bf16[1024,128]{1,0:T(8,128)(2,1)S(1)} %collective-permute-done.23) | copy-start | bytes 786436
  146.3 7.2 %collective-permute-start.9 = (bf16[1024,128]{1,0:T(8,128)(2,1)S(1)}, bf16[1024,128]{1,0:T(8,128)(2,1)S(1)}, u32[]{:S(2)}, u32[]{:S(2)}) collective-permute-start(bf16[1024,128]{1,0:T(8,128)(2,1)S(1)} %add_convert_fusion.5), channel_id=1, source_target_pairs={{0,1},{1,0},{2,3},{3,2},{4,5},{5,4},{6,7},{7,6},{8,9},{9,8},{10,11... | collective-permute-start | bytes 786440 | tf_op jit(solution)/shard_map/ppermute | solution.py:26
  146.6 6.9 %copy-start.7 = (bf16[1024,128]{1,0:T(8,128)(2,1)}, bf16[1024,128]{1,0:T(8,128)(2,1)S(1)}, u32[]{:S(2)}) copy-start(bf16[1024,128]{1,0:T(8,128)(2,1)S(1)} %collective-permute-done.24) | copy-start | bytes 786436
  146.6 6.9 %copy-start.8 = (bf16[1024,128]{1,0:T(8,128)(2,1)}, bf16[1024,128]{1,0:T(8,128)(2,1)S(1)}, u32[]{:S(2)}) copy-start(bf16[1024,128]{1,0:T(8,128)(2,1)S(1)} %collective-permute-done.21) | copy-start | bytes 786436
  146.6 6.9 %copy-start.9 = (bf16[1024,128]{1,0:T(8,128)(2,1)}, bf16[1024,128]{1,0:T(8,128)(2,1)S(1)}, u32[]{:S(2)}) copy-start(bf16[1024,128]{1,0:T(8,128)(2,1)S(1)} %collective-permute-done.11) | copy-start | bytes 786436
  153.5 0.7 copy-start.10
  153.5 0.8 copy-start.11

commit v5 on v4

--- a/solution.py
+++ b/solution.py
@@ -73,12 +73,18 @@
     )(*inputs)
 
 
-def attend_kernel(plane, group, rows, width, head, *refs):
+def attend_kernel(plane, group, rows, width, head, picks, begin, end, *refs):
     half = plane // 2
     length = 4 * rows + TAIL
-    own, pairs, queries = refs[:plane], refs[plane : plane + 2], refs[plane + 2 : 2 * plane + 2]
-    out_prev, out_own = refs[2 * plane + 2 : 2 * plane + 4], refs[2 * plane + 4 : 3 * plane + 4]
-    ka, kd, vv, segs, qq, do, qt, qa, dt, s, sd, u, ud, acc, tri, lims, sem = refs[3 * plane + 4 :]
+    own, pairs, refs = refs[:plane], refs[plane : plane + 2], refs[plane + 2 :]
+    queries, refs = refs[: len(picks)], refs[len(picks) :]
+    if not begin:
+        start_sums, refs = refs[0], refs[1:]
+    if end:
+        out_prev, out_own, refs = refs[:2], refs[2 : plane + 2], refs[plane + 2 :]
+    else:
+        end_sums, refs = refs[0], refs[1:]
+    ka, kd, vv, segs, qq, do, qt, qa, dt, s, sd, u, ud, acc, tri, lims, sem = refs
     device = lax.axis_index("ctx")
     me = lax.rem(device, plane)
     span = group * rows
@@ -105,19 +111,19 @@
             fetch(part[2], kd.at[block, :, low])
             fetch(part[3], vv.at[block, 1])
             fetch(piece.at[pl.ds(start + 4 * rows, TAIL), :], segs.at[block])
-        block = me ^ k
+    for i, k in enumerate(picks):
         start = head * 3 * span if k == 0 else 0
-        part = [queries[k].at[pl.ds(start + t * span, span), :] for t in range(3)]
-        fetch(part[0], qq.at[block, :, low])
-        fetch(part[1], qq.at[block, :, high])
-        fetch(part[2], do.at[block])
+        part = [queries[i].at[pl.ds(start + t * span, span), :] for t in range(3)]
+        fetch(part[0], qq.at[i, :, low])
+        fetch(part[1], qq.at[i, :, high])
+        fetch(part[2], do.at[i])
     key_at = lax.broadcasted_iota(jnp.int32, (rows, rows), 0)
     row_at = lax.broadcasted_iota(jnp.int32, (rows, rows), 1)
     for g in range(group):
         lanes = slice(g * rows, (g + 1) * rows)
         tri[0, :, lanes] = jnp.where(key_at > row_at, 0.0, HIDDEN)
         tri[1, :, lanes] = jnp.where(key_at <= row_at, 0.0, HIDDEN)
-    acc[...] = jnp.zeros_like(acc)
+    acc[...] = jnp.zeros_like(acc) if begin else start_sums[...]
     for copy in copies:
         copy.wait()
 
@@ -139,17 +145,18 @@
     def folded(values):
         return values.reshape(rows // 8, 8, span)
 
-    def one_block(a, carry):
+    def one_block(i, carry):
+        a = me ^ (picks[0] + i)
         first = lims[0, plane + a]
         skip = sum((lims[1, a + b] < first).astype(jnp.int32) for b in range(plane))
-        both = qq[a].astype(F32).T.astype(BF16)
+        both = qq[i].astype(F32).T.astype(BF16)
         qt[...] = both
         qa[:width, :] = both[:width, :]
         docs = document_row(plane + a)
         cover = jnp.where(names == docs, 0.0, HIDDEN).astype(BF16)
         for g in range(group):
             qa[width:, g * rows : (g + 1) * rows] = cover
-        dt[...] = do[a].astype(F32).T.astype(BF16)
+        dt[...] = do[i].astype(F32).T.astype(BF16)
 
         def score(b, bias, top):
             value = jnp.dot(ka[a + b], qa[...], preferred_element_type=F32)
@@ -197,12 +204,12 @@
             grad_dot = mix * (dot * up + (ud[b] - center_dot))
             mix_b, mix_dot_b = mix.astype(BF16), mix_dot.astype(BF16)
             grad_b, grad_dot_b = grad.astype(BF16), grad_dot.astype(BF16)
-            cot = do[a]
-            pair = jnp.dot(grad_b, qq[a], preferred_element_type=F32)
+            cot = do[i]
+            pair = jnp.dot(grad_b, qq[i], preferred_element_type=F32)
             acc[a + b, 0] += pair[:, :width]
             acc[a + b, 1] += jnp.dot(mix_b, cot, preferred_element_type=F32)
             acc[a + b, 2] += pair[:, width:] + jnp.dot(
-                grad_dot_b, qq[a, :, :width], preferred_element_type=F32
+                grad_dot_b, qq[i, :, :width], preferred_element_type=F32
             )
             acc[a + b, 3] += jnp.dot(mix_dot_b, cot, preferred_element_type=F32)
             return carry
@@ -210,7 +217,10 @@
         lax.fori_loop(skip, plane + 1, adjoints, 0)
         return carry
 
-    lax.fori_loop(0, plane, one_block, 0)
+    lax.fori_loop(0, len(picks), one_block, 0)
+    if not end:
+        end_sums[...] = acc[...]
+        return
     for k in range(plane):
         for t in range(4):
             scale = factor if t % 2 == 0 else 1.0
@@ -220,25 +230,37 @@
             out_own[k][at, :] = scale * acc[plane + (me ^ k), t]
 
 
-def attend(own, pairs, queries, plane, group, head):
+def attend(own, pairs, queries, plane, group, head, picks, sums=None, end=True):
     length, width = own[1].shape
     rows = (length - TAIL) // 4
     span = group * rows
     vmem = pl.BlockSpec(memory_space=pltpu.VMEM)
     blocks = 2 * plane
+    begin = sums is None
+    if end:
+        out_shape = [jax.ShapeDtypeStruct((2 * plane * rows, width), BF16)] * 2
+        out_shape += [jax.ShapeDtypeStruct((4 * rows, width), F32)] * plane
+    else:
+        out_shape = [pltpu.VMEM((blocks, 4, rows, width), F32)]
+    inputs = [*own, *pairs, *queries]
+    in_specs = [pl.BlockSpec(memory_space=pl.ANY)] * len(inputs)
+    if not begin:
+        inputs.append(pltpu.with_memory_space_constraint(sums, pltpu.VMEM))
+        in_specs.append(vmem)
     results = pl.pallas_call(
-        functools.partial(attend_kernel, plane, group, rows, width, head),
-        out_shape=[jax.ShapeDtypeStruct((2 * plane * rows, width), BF16)] * 2
-        + [jax.ShapeDtypeStruct((4 * rows, width), F32)] * plane,
-        in_specs=[pl.BlockSpec(memory_space=pl.ANY)] * (2 * plane + 2),
-        out_specs=[vmem] * (plane + 2),
+        functools.partial(
+            attend_kernel, plane, group, rows, width, head, tuple(picks), begin, end
+        ),
+        out_shape=out_shape,
+        in_specs=in_specs,
+        out_specs=[vmem] * len(out_shape),
         scratch_shapes=[
             pltpu.VMEM((blocks, rows, 2 * width), BF16),
             pltpu.VMEM((blocks, rows, 2 * width), BF16),
             pltpu.VMEM((blocks, 2, rows, width), BF16),
             pltpu.VMEM((blocks, TAIL, width), BF16),
-            pltpu.VMEM((plane, span, 2 * width), BF16),
-            pltpu.VMEM((plane, span, width), BF16),
+            pltpu.VMEM((len(picks), span, 2 * width), BF16),
+            pltpu.VMEM((len(picks), span, width), BF16),
             pltpu.VMEM((2 * width, span), BF16),
             pltpu.VMEM((2 * width, span), BF16),
             pltpu.VMEM((width, span), BF16),
@@ -248,32 +270,31 @@
             pltpu.VMEM((blocks, 4, rows, width), F32),
             pltpu.VMEM((2, rows, span), F32),
             pltpu.SMEM((2, blocks), F32),
-            pltpu.SemaphoreType.DMA((15 * plane,)),
+            pltpu.SemaphoreType.DMA((12 * plane + 3 * len(picks),)),
         ],
         compiler_params=pltpu.CompilerParams(vmem_limit_bytes=32 << 20),
         name="attend",
-    )(*own, *pairs, *queries)
-    return results[:2], results[2:]
-
-
-def finish_kernel(plane, heads, *refs):
+    )(*inputs)
+    return (results[:2], results[2:]) if end else results[0]
+
+
+def finish_kernel(plane, heads, tile, *refs):
     pieces, returned = refs[: plane * heads], refs[plane * heads : plane * heads + heads]
     outs, wide = refs[-5:-1], refs[-1]
     me = lax.rem(lax.axis_index("ctx"), plane)
-    rows = pieces[0].shape[1]
     count = plane * heads
     pitch = count + 1
+    here = pl.ds(pl.multiple_of(pl.program_id(0) * tile, tile), tile)
     for h in range(heads):
         for k in range(plane):
-            piece = pieces[h * plane + k]
             head = (me ^ k) * heads + h
             for t in range(4):
-                value = piece[t].astype(F32)
+                value = pieces[h * plane + k][t, here, :].astype(F32)
                 if k == 0:
-                    value = value + returned[h][t].astype(F32)
-                wide[t, pl.ds(head, rows, stride=pitch), :] = value
+                    value = value + returned[h][t, here, :].astype(F32)
+                wide[t, pl.ds(head, tile, stride=pitch), :] = value
     for t in range(4):
-        for r in range(rows):
+        for r in range(tile):
             at = slice(r * count, (r + 1) * count)
             outs[t][at, :] = wide[t, r * pitch : r * pitch + count, :]
 
@@ -284,13 +305,15 @@
     steps = 4
     tile = rows // steps
     stacked = [x.reshape(-1, rows, width) for x in list(pieces) + list(returned)]
+    stacked = [pltpu.with_memory_space_constraint(x, pltpu.VMEM) for x in stacked]
     return pl.pallas_call(
-        functools.partial(finish_kernel, plane, heads),
+        functools.partial(finish_kernel, plane, heads, tile),
         grid=(steps,),
         out_shape=[jax.ShapeDtypeStruct((rows * plane * heads, width), F32)] * 4,
-        in_specs=[pl.BlockSpec((4, tile, width), lambda i: (0, i, 0))] * len(stacked),
+        in_specs=[pl.BlockSpec(memory_space=pltpu.VMEM)] * len(stacked),
         out_specs=[pl.BlockSpec((tile * plane * heads, width), lambda i: (i, 0))] * 4,
         scratch_shapes=[pltpu.VMEM((4, tile * (plane * heads + 1), width), F32)],
+        compiler_params=pltpu.CompilerParams(vmem_limit_bytes=24 << 20),
         name="finish",
     )(*stacked)
 
@@ -320,7 +343,12 @@
         own = spread(kv, h)
         pairs = [first, shifted(jnp.concatenate(own[1:], axis=0), plane)]
         queries = spread(qs, h)
-        sums_prev, sums_own = attend(own, pairs, queries, plane, group, h)
+        near, far, every = range(half), range(half, plane), range(plane)
+        if h == 0:
+            sums = attend(own, pairs, queries[:half], plane, group, h, near, end=False)
+            sums_prev, sums_own = attend(own, pairs, queries[half:], plane, group, h, far, sums)
+        else:
+            sums_prev, sums_own = attend(own, pairs, queries, plane, group, h, every)
         back = [None, None]
         for i in (1, 0):
             back[i] = shifted(sums_prev[i], -plane)

time: 159 us -> 153 us (0.962)
  the two profiles are of different devices: /device:TPU:0 before, /device:TPU:21 now
where the time goes in v5:
time: 153 us; the launch traced here: 150 us
  waiting for transfers between devices  65.5 us (43%)
  Pallas kernels  42.2 us (28%)
  starting transfers between devices  39.7 us (26%)
    ppermute x18, waiting for transfers between devices, swapped(): return lax.ppermute(block, 'ctx', [(i, i ^ partner) for i in devices])  43.2 us
    pallas_call x3, Pallas kernels, attend(): pl.pallas_call(functools.partial(attend_kernel, plane, group, rows, width...  31.9 us
    ppermute x7, starting transfers between devices, shifted(): return lax.ppermute(block, 'ctx', route)  24.9 us
    ppermute x7, waiting for transfers between devices, shifted(): return lax.ppermute(block, 'ctx', route)  22.3 us
    ppermute x18, starting transfers between devices, swapped(): return lax.ppermute(block, 'ctx', [(i, i ^ partner) for i in devices])  14.9 us
    pallas_call x2, Pallas kernels, pack(): pl.pallas_call(functools.partial(pack_kernel, plane, heads, group, len(ar...  7.91 us
  transfers between devices with their start and end apart: 25, of which 11 were waited for; matrix products, arithmetic and copies ran while one was open for 1% of the time, Pallas kernels for 24%

profile of v5, /device:TPU:21, one launch (start us, length us, event | category | flops | bytes accessed | tf_op | source)
XLA Modules:
  0.0 149.7 jit_solution(7026502302407922208)
XLA Ops:
  0.6 3.5 %pack.2 = (bf16[2080,128]{1,0:T(8,128)(2,1)}, bf16[1040,128]{1,0:T(8,128)(2,1)}, bf16[1040,128]{1,0:T(8,128)(2,1)}, bf16[1040,128]{1,0:T(8,128)(2,1)}, bf16[1040...) custom-call(bf16[256,8,128]{2,1,0:T(8,128)(2,1)} %refs_0_.2, bf16[256,8,128]{2,1,0:T(8,128)(2,1)} %refs_1_.2, ...), custom_call_target="tpu_custom_call" | custom-call | tf_op jit(solution)/shard_map/pack/pallas_call | solution.py:65
  4.2 0.7 collective-permute-start.13
  4.8 0.2 collective-permute-start.14
  5.1 1.5 collective-permute-start.15
  6.5 0.2 collective-permute-start
  6.7 0.2 collective-permute-start.1
  6.9 1.8 %collective-permute-start.2 = (bf16[1040,128]{1,0:T(8,128)(2,1)}, bf16[1040,128]{1,0:T(8,128)(2,1)S(1)}, u32[]{:S(2)}, u32[]{:S(2)}) collective-permute-start(bf16[1040,128]{1,0:T(8,128)(2,1)} %get-tuple-element.37), channel_id=1, source_target_pairs={{0,3},{1,2},{2,1},{3,0},{4,7},{5,6},{6,5},{7,4},{8,11},{9,10},{10,... | collective-permute-start | bytes 798728 | tf_op jit(solution)/shard_map/ppermute | solution.py:26
  8.7 4.2 %collective-permute-done.14.refs_2_ = bf16[1040,128]{1,0:T(8,128)(2,1)S(1)} collective-permute-done((bf16[1040,128]{1,0:T(8,128)(2,1)}, bf16[1040,128]{1,0:T(8,128)(2,1)S(1)}, u32[]{:S(2)}, u32[]{:S(2)}) %collective-permute-start.14) | collective-permute-done | bytes 266272 | tf_op jit(solution)/shard_map/ppermute | solution.py:26
  12.9 6.5 %collective-permute-done.15.refs_3_ = bf16[1040,128]{1,0:T(8,128)(2,1)S(1)} collective-permute-done((bf16[1040,128]{1,0:T(8,128)(2,1)}, bf16[1040,128]{1,0:T(8,128)(2,1)S(1)}, u32[]{:S(2)}, u32[]{:S(2)}) %collective-permute-start.15) | collective-permute-done | bytes 266272 | tf_op jit(solution)/shard_map/ppermute | solution.py:26
  19.4 0.9 pad_maximum_fusion.1
  20.3 3.2 %collective-permute-start.16 = (bf16[3120,128]{1,0:T(8,128)(2,1)}, bf16[3120,128]{1,0:T(8,128)(2,1)S(1)}, u32[]{:S(2)}, u32[]{:S(2)}) collective-permute-start(bf16[3120,128]{1,0:T(8,128)(2,1)} %pad_maximum_fusion.1), channel_id=1, source_target_pairs={{0,4},{1,5},{2,6},{3,7},{4,8},{5,9},{6,10},{7,11},{8,12},{9,13},{1... | collective-permute-start | bytes 2396168 | tf_op jit(solution)/shard_map/ppermute | solution.py:21
  23.5 1.9 %collective-permute-start.3 = (bf16[2080,128]{1,0:T(8,128)(2,1)S(1)}, bf16[2080,128]{1,0:T(8,128)(2,1)S(1)}, u32[]{:S(2)}, u32[]{:S(2)}) collective-permute-start(bf16[2080,128]{1,0:T(8,128)(2,1)S(1)} %copy-done), channel_id=1, source_target_pairs={{0,4},{1,5},{2,6},{3,7},{4,8},{5,9},{6,10},{7,11},{8,12},{9,13},{1... | collective-permute-start | bytes 1597448 | tf_op jit(solution)/shard_map/ppermute | solution.py:21
  25.5 4.4 %pack.3 = (bf16[3072,128]{1,0:T(8,128)(2,1)}, bf16[1536,128]{1,0:T(8,128)(2,1)}, bf16[1536,128]{1,0:T(8,128)(2,1)}, bf16[1536,128]{1,0:T(8,128)(2,1)}, bf16[1536...) custom-call(bf16[256,16,128]{2,1,0:T(8,128)(2,1)} %refs_0_.3, ...), custom_call_target="tpu_custom_call" | custom-call | tf_op jit(solution)/shard_map/pack/pallas_call | solution.py:65
  29.9 0.1 collective-permute-start.17
  30.0 0.3 collective-permute-start.18
  30.3 0.3 collective-permute-done.2.refs_3_
  30.6 1.5 %collective-permute-start.19 = (bf16[1536,128]{1,0:T(8,128)(2,1)}, bf16[1536,128]{1,0:T(8,128)(2,1)S(1)}, u32[]{:S(2)}, u32[]{:S(2)}) collective-permute-start(bf16[1536,128]{1,0:T(8,128)(2,1)} %get-tuple-element.53), channel_id=1, source_target_pairs={{0,3},{1,2},{2,1},{3,0},{4,7},{5,6},{6,5},{7,4},{8,11},{9,10},{10,... | collective-permute-start | bytes 1179656 | tf_op jit(solution)/shard_map/ppermute | solution.py:26
  32.1 0.1 pad_maximum_fusion
  32.1 1.9 %collective-permute-start.4 = (bf16[3120,128]{1,0:T(8,128)(2,1)S(1)}, bf16[3120,128]{1,0:T(8,128)(2,1)S(1)}, u32[]{:S(2)}, u32[]{:S(2)}) collective-permute-start(bf16[3120,128]{1,0:T(8,128)(2,1)S(1)} %pad_maximum_fusion), channel_id=1, source_target_pairs={{0,4},{1,5},{2,6},{3,7},{4,8},{5,9},{6,10},{7,11},{8,12},{9,13},{1... | collective-permute-start | bytes 2396168 | tf_op jit(solution)/shard_map/ppermute | solution.py:21
  34.1 6.4 %collective-permute-done.18.refs_8_ = bf16[1536,128]{1,0:T(8,128)(2,1)S(1)} collective-permute-done((bf16[1536,128]{1,0:T(8,128)(2,1)}, bf16[1536,128]{1,0:T(8,128)(2,1)S(1)}, u32[]{:S(2)}, u32[]{:S(2)}) %collective-permute-start.18) | collective-permute-done | bytes 393248 | tf_op jit(solution)/shard_map/ppermute | solution.py:26
  40.5 2.2 %collective-permute-start.7 = (bf16[1536,128]{1,0:T(8,128)(2,1)S(1)}, bf16[1536,128]{1,0:T(8,128)(2,1)S(1)}, u32[]{:S(2)}, u32[]{:S(2)}) collective-permute-start(bf16[1536,128]{1,0:T(8,128)(2,1)S(1)} %copy-done.4), channel_id=1, source_target_pairs={{0,1},{1,0},{2,3},{3,2},{4,5},{5,4},{6,7},{7,6},{8,9},{9,8},{10,11... | collective-permute-start | bytes 1179656 | tf_op jit(solution)/shard_map/ppermute | solution.py:26
  42.6 7.1 %collective-permute-done.19.refs_9_ = bf16[1536,128]{1,0:T(8,128)(2,1)S(1)} collective-permute-done((bf16[1536,128]{1,0:T(8,128)(2,1)}, bf16[1536,128]{1,0:T(8,128)(2,1)S(1)}, u32[]{:S(2)}, u32[]{:S(2)}) %collective-permute-start.19) | collective-permute-done | bytes 393248 | tf_op jit(solution)/shard_map/ppermute | solution.py:26
  49.8 3.8 %collective-permute-done.3.refs_4_ = bf16[2080,128]{1,0:T(8,128)(2,1)S(1)} collective-permute-done((bf16[2080,128]{1,0:T(8,128)(2,1)S(1)}, bf16[2080,128]{1,0:T(8,128)(2,1)S(1)}, u32[]{:S(2)}, u32[]{:S(2)}) %collective-permute-start.3) | collective-permute-done | bytes 532512 | tf_op jit(solution)/shard_map/ppermute | solution.py:21
  53.6 14.4 %attend.5 = (bf16[2048,128]{1,0:T(8,128)(2,1)S(1)}, bf16[2048,128]{1,0:T(8,128)(2,1)S(1)}, f32[1024,128]{1,0:T(8,128)S(1)}, f32[1024,128]{1,0:T(8,128)S(1)}, f32...) custom-call(bf16[2080,128]{1,0:T(8,128)(2,1)S(1)} %copy-done, bf16[1040,128]{1,0:T(8,128)(2,1)S(1)} %collective-permute-done.13.refs_1_, ...), custom_call_target="tpu_custom_call" | custom-call | tf_op jit(solution)/shard_map/attend/pallas_call | solution.py:250
  68.0 7.5 %collective-permute-start.20 = (bf16[2048,128]{1,0:T(8,128)(2,1)S(1)}, bf16[2048,128]{1,0:T(8,128)(2,1)S(1)}, u32[]{:S(2)}, u32[]{:S(2)}) collective-permute-start(bf16[2048,128]{1,0:T(8,128)(2,1)S(1)} %get-tuple-element.56), channel_id=1, source_target_pairs={{4,0},{5,1},{6,2},{7,3},{8,4},{9,5},{10,6},{11,7},{12,8},{13,9},{1... | collective-permute-start | bytes 1572872 | tf_op jit(solution)/shard_map/ppermute | solution.py:21
  75.5 0.1 collective-permute-start.5
  75.6 2.5 %collective-permute-start.6 = (bf16[1536,128]{1,0:T(8,128)(2,1)S(1)}, bf16[1536,128]{1,0:T(8,128)(2,1)S(1)}, u32[]{:S(2)}, u32[]{:S(2)}) collective-permute-start(bf16[1536,128]{1,0:T(8,128)(2,1)S(1)} %copy-done.2), channel_id=1, source_target_pairs={{0,3},{1,2},{2,1},{3,0},{4,7},{5,6},{6,5},{7,4},{8,11},{9,10},{10,... | collective-permute-start | bytes 1179656 | tf_op jit(solution)/shard_map/ppermute | solution.py:26
  78.0 2.1 %collective-permute-start.22 = (bf16[2048,128]{1,0:T(8,128)(2,1)S(1)}, bf16[2048,128]{1,0:T(8,128)(2,1)S(1)}, u32[]{:S(2)}, u32[]{:S(2)}) collective-permute-start(bf16[2048,128]{1,0:T(8,128)(2,1)S(1)} %get-tuple-element.58), channel_id=1, source_target_pairs={{4,0},{5,1},{6,2},{7,3},{8,4},{9,5},{10,6},{11,7},{12,8},{13,9},{1... | collective-permute-start | bytes 1572872 | tf_op jit(solution)/shard_map/ppermute | solution.py:21
  80.2 8.2 %attend.3.refs_8_ = f32[8,4,256,128]{3,2,1,0:T(8,128)S(1)} custom-call(bf16[2080,128]{1,0:T(8,128)(2,1)S(1)} %copy-done, bf16[1040,128]{1,0:T(8,128)(2,1)S(1)} %collective-permute-done.refs_1_, bf16[1040,128]{1,0:T(8,128)(2,1)S(1)} %collective-permute-done.1.refs_2_, bf16[1040,128]{1,0:T(8,128)(2,1)S(1)} %collective-permute-done.2.refs_3_, ...), custom_call_target="tpu_custom_call" | custom-call | tf_op jit(solution)/shard_map/attend/pallas_call | solution.py:250
  88.4 6.7 %collective-permute-done.6.refs_7_ = bf16[1536,128]{1,0:T(8,128)(2,1)S(1)} collective-permute-done((bf16[1536,128]{1,0:T(8,128)(2,1)S(1)}, bf16[1536,128]{1,0:T(8,128)(2,1)S(1)}, u32[]{:S(2)}, u32[]{:S(2)}) %collective-permute-start.6) | collective-permute-done | bytes 393248 | tf_op jit(solution)/shard_map/ppermute | solution.py:26
  95.1 9.3 %attend.4 = (bf16[2048,128]{1,0:T(8,128)(2,1)S(1)}, bf16[2048,128]{1,0:T(8,128)(2,1)S(1)}, f32[1024,128]{1,0:T(8,128)S(1)}, f32[1024,128]{1,0:T(8,128)S(1)}, f32...) custom-call(bf16[2080,128]{1,0:T(8,128)(2,1)S(1)} %copy-done, bf16[1040,128]{1,0:T(8,128)(2,1)S(1)} %collective-permute-done.refs_1_, ...), custom_call_target="tpu_custom_call" | custom-call | tf_op jit(solution)/shard_map/attend/pallas_call | solution.py:250
  104.3 6.3 %collective-permute-start.8 = (bf16[2048,128]{1,0:T(8,128)(2,1)S(1)}, bf16[2048,128]{1,0:T(8,128)(2,1)S(1)}, u32[]{:S(2)}, u32[]{:S(2)}) collective-permute-start(bf16[2048,128]{1,0:T(8,128)(2,1)S(1)} %get-tuple-element.44), channel_id=1, source_target_pairs={{4,0},{5,1},{6,2},{7,3},{8,4},{9,5},{10,6},{11,7},{12,8},{13,9},{1... | collective-permute-start | bytes 1572872 | tf_op jit(solution)/shard_map/ppermute | solution.py:21
  110.7 1.9 %collective-permute-start.10 = (bf16[2048,128]{1,0:T(8,128)(2,1)S(1)}, bf16[2048,128]{1,0:T(8,128)(2,1)S(1)}, u32[]{:S(2)}, u32[]{:S(2)}) collective-permute-start(bf16[2048,128]{1,0:T(8,128)(2,1)S(1)} %get-tuple-element.46), channel_id=1, source_target_pairs={{4,0},{5,1},{6,2},{7,3},{8,4},{9,5},{10,6},{11,7},{12,8},{13,9},{1... | collective-permute-start | bytes 1572872 | tf_op jit(solution)/shard_map/ppermute | solution.py:21
  112.6 0.1 add_convert_fusion.2
  112.7 0.1 collective-permute-start.21
  112.7 0.1 add_convert_fusion
  112.9 0.1 collective-permute-start.24
  113.0 1.8 %collective-permute-start.23 = (bf16[1024,128]{1,0:T(8,128)(2,1)S(1)}, bf16[1024,128]{1,0:T(8,128)(2,1)S(1)}, u32[]{:S(2)}, u32[]{:S(2)}) collective-permute-start(bf16[1024,128]{1,0:T(8,128)(2,1)S(1)} %get-tuple-element.65), channel_id=1, source_target_pairs={{0,2},{1,3},{2,0},{3,1},{4,6},{5,7},{6,4},{7,5},{8,10},{9,11},{10,... | collective-permute-start | bytes 786440 | tf_op jit(solution)/shard_map/ppermute | solution.py:26
  114.8 7.6 %collective-permute-done.8 = bf16[2048,128]{1,0:T(8,128)(2,1)S(1)} collective-permute-done((bf16[2048,128]{1,0:T(8,128)(2,1)S(1)}, bf16[2048,128]{1,0:T(8,128)(2,1)S(1)}, u32[]{:S(2)}, u32[]{:S(2)}) %collective-permute-start.8) | collective-permute-done | bytes 524320 | tf_op jit(solution)/shard_map/ppermute | solution.py:21
  122.4 0.1 add_convert_fusion.5
  122.4 0.2 collective-permute-start.9
  122.6 10.9 %collective-permute-done.10 = bf16[2048,128]{1,0:T(8,128)(2,1)S(1)} collective-permute-done((bf16[2048,128]{1,0:T(8,128)(2,1)S(1)}, bf16[2048,128]{1,0:T(8,128)(2,1)S(1)}, u32[]{:S(2)}, u32[]{:S(2)}) %collective-permute-start.10) | collective-permute-done | bytes 524320 | tf_op jit(solution)/shard_map/ppermute | solution.py:21
  133.6 0.1 add_convert_fusion.3
  133.7 0.1 collective-permute-start.12
  133.8 1.5 %collective-permute-start.11 = (bf16[1024,128]{1,0:T(8,128)(2,1)S(1)}, bf16[1024,128]{1,0:T(8,128)(2,1)S(1)}, u32[]{:S(2)}, u32[]{:S(2)}) collective-permute-start(bf16[1024,128]{1,0:T(8,128)(2,1)S(1)} %get-tuple-element.67), channel_id=1, source_target_pairs={{0,2},{1,3},{2,0},{3,1},{4,6},{5,7},{6,4},{7,5},{8,10},{9,11},{10,... | collective-permute-start | bytes 786440 | tf_op jit(solution)/shard_map/ppermute | solution.py:26
  135.3 7.1 %collective-permute-done.12 = bf16[1024,128]{1,0:T(8,128)(2,1)S(1)} collective-permute-done((bf16[1024,128]{1,0:T(8,128)(2,1)S(1)}, bf16[1024,128]{1,0:T(8,128)(2,1)S(1)}, u32[]{:S(2)}, u32[]{:S(2)}) %collective-permute-start.12) | collective-permute-done | bytes 262176 | tf_op jit(solution)/shard_map/ppermute | solution.py:26
  142.4 4.9 %collective-permute-done.11 = bf16[1024,128]{1,0:T(8,128)(2,1)S(1)} collective-permute-done((bf16[1024,128]{1,0:T(8,128)(2,1)S(1)}, bf16[1024,128]{1,0:T(8,128)(2,1)S(1)}, u32[]{:S(2)}, u32[]{:S(2)}) %collective-permute-start.11) | collective-permute-done | bytes 262176 | tf_op jit(solution)/shard_map/ppermute | solution.py:26
  147.2 2.5 %finish.1 = (f32[2048,128]{1,0:T(8,128)}, f32[2048,128]{1,0:T(8,128)}, f32[2048,128]{1,0:T(8,128)}, f32[2048,128]{1,0:T(8,128)}) custom-call(f32[4,256,128]{2,1,0:T(8,128)S(1)} %bitcast.18, bf16[4,256,128]{2,1,0:T(8,128)(2,1)S(1)} %bitcast.22, bf16[4,256,128]{2,1,0:T(8,128)(2,1)S(1)} %bitcast.24, bf16[4,256,128]{2,1,0:T(8,128)(2,1)S(1)} %bitcast.23, ...), custom_call_target="tpu_custom_call" | custom-call | tf_op jit(solution)/shard_map/finish/pallas_call | solution.py:309
  (24 shorter events, 0.1 us)
Async XLA Ops:
  4.2 19.4 %copy-start = (bf16[2080,128]{1,0:T(8,128)(2,1)S(1)}, bf16[2080,128]{1,0:T(8,128)(2,1)}, u32[]{:S(2)}) copy-start(bf16[2080,128]{1,0:T(8,128)(2,1)} %get-tuple-element.34.refs_0_) | copy-start | bytes 1597444
  4.2 2.8 %collective-permute-start.13 = (bf16[1040,128]{1,0:T(8,128)(2,1)}, bf16[1040,128]{1,0:T(8,128)(2,1)S(1)}, u32[]{:S(2)}, u32[]{:S(2)}) collective-permute-start(bf16[1040,128]{1,0:T(8,128)(2,1)} %get-tuple-element.48), channel_id=1, source_target_pairs={{0,1},{1,0},{2,3},{3,2},{4,5},{5,4},{6,7},{7,6},{8,9},{9,8},{10,11... | collective-permute-start | bytes 798728 | tf_op jit(solution)/shard_map/ppermute | solution.py:26
  4.8 8.1 %collective-permute-start.14 = (bf16[1040,128]{1,0:T(8,128)(2,1)}, bf16[1040,128]{1,0:T(8,128)(2,1)S(1)}, u32[]{:S(2)}, u32[]{:S(2)}) collective-permute-start(bf16[1040,128]{1,0:T(8,128)(2,1)} %get-tuple-element.49), channel_id=1, source_target_pairs={{0,2},{1,3},{2,0},{3,1},{4,6},{5,7},{6,4},{7,5},{8,10},{9,11},{10,... | collective-permute-start | bytes 798728 | tf_op jit(solution)/shard_map/ppermute | solution.py:26
  5.1 14.3 %collective-permute-start.15 = (bf16[1040,128]{1,0:T(8,128)(2,1)}, bf16[1040,128]{1,0:T(8,128)(2,1)S(1)}, u32[]{:S(2)}, u32[]{:S(2)}) collective-permute-start(bf16[1040,128]{1,0:T(8,128)(2,1)} %get-tuple-element.50), channel_id=1, source_target_pairs={{0,3},{1,2},{2,1},{3,0},{4,7},{5,6},{6,5},{7,4},{8,11},{9,10},{10,... | collective-permute-start | bytes 798728 | tf_op jit(solution)/shard_map/ppermute | solution.py:26
  6.5 23.3 %collective-permute-start = (bf16[1040,128]{1,0:T(8,128)(2,1)}, bf16[1040,128]{1,0:T(8,128)(2,1)S(1)}, u32[]{:S(2)}, u32[]{:S(2)}) collective-permute-start(bf16[1040,128]{1,0:T(8,128)(2,1)} %get-tuple-element.35), channel_id=1, source_target_pairs={{0,1},{1,0},{2,3},{3,2},{4,5},{5,4},{6,7},{7,6},{8,9},{9,8},{10,11... | collective-permute-start | bytes 798728 | tf_op jit(solution)/shard_map/ppermute | solution.py:26
  6.7 23.3 %collective-permute-start.1 = (bf16[1040,128]{1,0:T(8,128)(2,1)}, bf16[1040,128]{1,0:T(8,128)(2,1)S(1)}, u32[]{:S(2)}, u32[]{:S(2)}) collective-permute-start(bf16[1040,128]{1,0:T(8,128)(2,1)} %get-tuple-element.36), channel_id=1, source_target_pairs={{0,2},{1,3},{2,0},{3,1},{4,6},{5,7},{6,4},{7,5},{8,10},{9,11},{10,... | collective-permute-start | bytes 798728 | tf_op jit(solution)/shard_map/ppermute | solution.py:26
  6.9 23.6 %collective-permute-start.2 = (bf16[1040,128]{1,0:T(8,128)(2,1)}, bf16[1040,128]{1,0:T(8,128)(2,1)S(1)}, u32[]{:S(2)}, u32[]{:S(2)}) collective-permute-start(bf16[1040,128]{1,0:T(8,128)(2,1)} %get-tuple-element.37), channel_id=1, source_target_pairs={{0,3},{1,2},{2,1},{3,0},{4,7},{5,6},{6,5},{7,4},{8,11},{9,10},{10,... | collective-permute-start | bytes 798728 | tf_op jit(solution)/shard_map/ppermute | solution.py:26
  20.3 33.2 %collective-permute-start.16 = (bf16[3120,128]{1,0:T(8,128)(2,1)}, bf16[3120,128]{1,0:T(8,128)(2,1)S(1)}, u32[]{:S(2)}, u32[]{:S(2)}) collective-permute-start(bf16[3120,128]{1,0:T(8,128)(2,1)} %pad_maximum_fusion.1), channel_id=1, source_target_pairs={{0,4},{1,5},{2,6},{3,7},{4,8},{5,9},{6,10},{7,11},{8,12},{9,13},{1... | collective-permute-start | bytes 2396168 | tf_op jit(solution)/shard_map/ppermute | solution.py:21
  23.5 30.0 %collective-permute-start.3 = (bf16[2080,128]{1,0:T(8,128)(2,1)S(1)}, bf16[2080,128]{1,0:T(8,128)(2,1)S(1)}, u32[]{:S(2)}, u32[]{:S(2)}) collective-permute-start(bf16[2080,128]{1,0:T(8,128)(2,1)S(1)} %copy-done), channel_id=1, source_target_pairs={{0,4},{1,5},{2,6},{3,7},{4,8},{5,9},{6,10},{7,11},{8,12},{9,13},{1... | collective-permute-start | bytes 1597448 | tf_op jit(solution)/shard_map/ppermute | solution.py:21
  29.9 10.6 %copy-start.4 = (bf16[1536,128]{1,0:T(8,128)(2,1)S(1)}, bf16[1536,128]{1,0:T(8,128)(2,1)}, u32[]{:S(2)}) copy-start(bf16[1536,128]{1,0:T(8,128)(2,1)} %get-tuple-element.41) | copy-start | bytes 1179652
  29.9 23.7 %copy-start.1 = (bf16[3072,128]{1,0:T(8,128)(2,1)S(1)}, bf16[3072,128]{1,0:T(8,128)(2,1)}, u32[]{:S(2)}) copy-start(bf16[3072,128]{1,0:T(8,128)(2,1)} %get-tuple-element.40.refs_6_) | copy-start | bytes 2359300
  29.9 2.3 %collective-permute-start.17 = (bf16[1536,128]{1,0:T(8,128)(2,1)}, bf16[1536,128]{1,0:T(8,128)(2,1)S(1)}, u32[]{:S(2)}, u32[]{:S(2)}) collective-permute-start(bf16[1536,128]{1,0:T(8,128)(2,1)} %get-tuple-element.51), channel_id=1, source_target_pairs={{0,1},{1,0},{2,3},{3,2},{4,5},{5,4},{6,7},{7,6},{8,9},{9,8},{10,11... | collective-permute-start | bytes 1179656 | tf_op jit(solution)/shard_map/ppermute | solution.py:26
  30.0 10.5 %collective-permute-start.18 = (bf16[1536,128]{1,0:T(8,128)(2,1)}, bf16[1536,128]{1,0:T(8,128)(2,1)S(1)}, u32[]{:S(2)}, u32[]{:S(2)}) collective-permute-start(bf16[1536,128]{1,0:T(8,128)(2,1)} %get-tuple-element.52), channel_id=1, source_target_pairs={{0,2},{1,3},{2,0},{3,1},{4,6},{5,7},{6,4},{7,5},{8,10},{9,11},{10,... | collective-permute-start | bytes 1179656 | tf_op jit(solution)/shard_map/ppermute | solution.py:26
  30.6 19.2 %collective-permute-start.19 = (bf16[1536,128]{1,0:T(8,128)(2,1)}, bf16[1536,128]{1,0:T(8,128)(2,1)S(1)}, u32[]{:S(2)}, u32[]{:S(2)}) collective-permute-start(bf16[1536,128]{1,0:T(8,128)(2,1)} %get-tuple-element.53), channel_id=1, source_target_pairs={{0,3},{1,2},{2,1},{3,0},{4,7},{5,6},{6,5},{7,4},{8,11},{9,10},{10,... | collective-permute-start | bytes 1179656 | tf_op jit(solution)/shard_map/ppermute | solution.py:26
  32.1 48.0 %collective-permute-start.4 = (bf16[3120,128]{1,0:T(8,128)(2,1)S(1)}, bf16[3120,128]{1,0:T(8,128)(2,1)S(1)}, u32[]{:S(2)}, u32[]{:S(2)}) collective-permute-start(bf16[3120,128]{1,0:T(8,128)(2,1)S(1)} %pad_maximum_fusion), channel_id=1, source_target_pairs={{0,4},{1,5},{2,6},{3,7},{4,8},{5,9},{6,10},{7,11},{8,12},{9,13},{1... | collective-permute-start | bytes 2396168 | tf_op jit(solution)/shard_map/ppermute | solution.py:21
  40.5 37.6 %collective-permute-start.7 = (bf16[1536,128]{1,0:T(8,128)(2,1)S(1)}, bf16[1536,128]{1,0:T(8,128)(2,1)S(1)}, u32[]{:S(2)}, u32[]{:S(2)}) collective-permute-start(bf16[1536,128]{1,0:T(8,128)(2,1)S(1)} %copy-done.4), channel_id=1, source_target_pairs={{0,1},{1,0},{2,3},{3,2},{4,5},{5,4},{6,7},{7,6},{8,9},{9,8},{10,11... | collective-permute-start | bytes 1179656 | tf_op jit(solution)/shard_map/ppermute | solution.py:26
  53.6 21.9 %copy-start.3 = (bf16[1536,128]{1,0:T(8,128)(2,1)S(1)}, bf16[1536,128]{1,0:T(8,128)(2,1)}, u32[]{:S(2)}) copy-start(bf16[1536,128]{1,0:T(8,128)(2,1)} %get-tuple-element.38) | copy-start | bytes 1179652
  53.6 22.0 %copy-start.2 = (bf16[1536,128]{1,0:T(8,128)(2,1)S(1)}, bf16[1536,128]{1,0:T(8,128)(2,1)}, u32[]{:S(2)}) copy-start(bf16[1536,128]{1,0:T(8,128)(2,1)} %get-tuple-element.39) | copy-start | bytes 1179652
  68.0 44.6 %collective-permute-start.20 = (bf16[2048,128]{1,0:T(8,128)(2,1)S(1)}, bf16[2048,128]{1,0:T(8,128)(2,1)S(1)}, u32[]{:S(2)}, u32[]{:S(2)}) collective-permute-start(bf16[2048,128]{1,0:T(8,128)(2,1)S(1)} %get-tuple-element.56), channel_id=1, source_target_pairs={{4,0},{5,1},{6,2},{7,3},{8,4},{9,5},{10,6},{11,7},{12,8},{13,9},{1... | collective-permute-start | bytes 1572872 | tf_op jit(solution)/shard_map/ppermute | solution.py:21
  75.5 12.9 %collective-permute-start.5 = (bf16[1536,128]{1,0:T(8,128)(2,1)S(1)}, bf16[1536,128]{1,0:T(8,128)(2,1)S(1)}, u32[]{:S(2)}, u32[]{:S(2)}) collective-permute-start(bf16[1536,128]{1,0:T(8,128)(2,1)S(1)} %copy-done.3), channel_id=1, source_target_pairs={{0,2},{1,3},{2,0},{3,1},{4,6},{5,7},{6,4},{7,5},{8,10},{9,11},{10,... | collective-permute-start | bytes 1179656 | tf_op jit(solution)/shard_map/ppermute | solution.py:26
  75.6 19.5 %collective-permute-start.6 = (bf16[1536,128]{1,0:T(8,128)(2,1)S(1)}, bf16[1536,128]{1,0:T(8,128)(2,1)S(1)}, u32[]{:S(2)}, u32[]{:S(2)}) collective-permute-start(bf16[1536,128]{1,0:T(8,128)(2,1)S(1)} %copy-done.2), channel_id=1, source_target_pairs={{0,3},{1,2},{2,1},{3,0},{4,7},{5,6},{6,5},{7,4},{8,11},{9,10},{10,... | collective-permute-start | bytes 1179656 | tf_op jit(solution)/shard_map/ppermute | solution.py:26
  78.0 34.7 %collective-permute-start.22 = (bf16[2048,128]{1,0:T(8,128)(2,1)S(1)}, bf16[2048,128]{1,0:T(8,128)(2,1)S(1)}, u32[]{:S(2)}, u32[]{:S(2)}) collective-permute-start(bf16[2048,128]{1,0:T(8,128)(2,1)S(1)} %get-tuple-element.58), channel_id=1, source_target_pairs={{4,0},{5,1},{6,2},{7,3},{8,4},{9,5},{10,6},{11,7},{12,8},{13,9},{1... | collective-permute-start | bytes 1572872 | tf_op jit(solution)/shard_map/ppermute | solution.py:21
  104.3 18.0 %collective-permute-start.8 = (bf16[2048,128]{1,0:T(8,128)(2,1)S(1)}, bf16[2048,128]{1,0:T(8,128)(2,1)S(1)}, u32[]{:S(2)}, u32[]{:S(2)}) collective-permute-start(bf16[2048,128]{1,0:T(8,128)(2,1)S(1)} %get-tuple-element.44), channel_id=1, source_target_pairs={{4,0},{5,1},{6,2},{7,3},{8,4},{9,5},{10,6},{11,7},{12,8},{13,9},{1... | collective-permute-start | bytes 1572872 | tf_op jit(solution)/shard_map/ppermute | solution.py:21
  110.7 22.9 %collective-permute-start.10 = (bf16[2048,128]{1,0:T(8,128)(2,1)S(1)}, bf16[2048,128]{1,0:T(8,128)(2,1)S(1)}, u32[]{:S(2)}, u32[]{:S(2)}) collective-permute-start(bf16[2048,128]{1,0:T(8,128)(2,1)S(1)} %get-tuple-element.46), channel_id=1, source_target_pairs={{4,0},{5,1},{6,2},{7,3},{8,4},{9,5},{10,6},{11,7},{12,8},{13,9},{1... | collective-permute-start | bytes 1572872 | tf_op jit(solution)/shard_map/ppermute | solution.py:21
  112.7 21.1 %collective-permute-start.21 = (bf16[1024,128]{1,0:T(8,128)(2,1)S(1)}, bf16[1024,128]{1,0:T(8,128)(2,1)S(1)}, u32[]{:S(2)}, u32[]{:S(2)}) collective-permute-start(bf16[1024,128]{1,0:T(8,128)(2,1)S(1)} %add_convert_fusion.2), channel_id=1, source_target_pairs={{0,1},{1,0},{2,3},{3,2},{4,5},{5,4},{6,7},{7,6},{8,9},{9,8},{10,11... | collective-permute-start | bytes 786440 | tf_op jit(solution)/shard_map/ppermute | solution.py:26
  112.9 22.4 %collective-permute-start.24 = (bf16[1024,128]{1,0:T(8,128)(2,1)S(1)}, bf16[1024,128]{1,0:T(8,128)(2,1)S(1)}, u32[]{:S(2)}, u32[]{:S(2)}) collective-permute-start(bf16[1024,128]{1,0:T(8,128)(2,1)S(1)} %get-tuple-element.64), channel_id=1, source_target_pairs={{0,3},{1,2},{2,1},{3,0},{4,7},{5,6},{6,5},{7,4},{8,11},{9,10},{10,... | collective-permute-start | bytes 786440 | tf_op jit(solution)/shard_map/ppermute | solution.py:26
  113.0 22.3 %collective-permute-start.23 = (bf16[1024,128]{1,0:T(8,128)(2,1)S(1)}, bf16[1024,128]{1,0:T(8,128)(2,1)S(1)}, u32[]{:S(2)}, u32[]{:S(2)}) collective-permute-start(bf16[1024,128]{1,0:T(8,128)(2,1)S(1)} %get-tuple-element.65), channel_id=1, source_target_pairs={{0,2},{1,3},{2,0},{3,1},{4,6},{5,7},{6,4},{7,5},{8,10},{9,11},{10,... | collective-permute-start | bytes 786440 | tf_op jit(solution)/shard_map/ppermute | solution.py:26
  122.4 12.8 %collective-permute-start.9 = (bf16[1024,128]{1,0:T(8,128)(2,1)S(1)}, bf16[1024,128]{1,0:T(8,128)(2,1)S(1)}, u32[]{:S(2)}, u32[]{:S(2)}) collective-permute-start(bf16[1024,128]{1,0:T(8,128)(2,1)S(1)} %add_convert_fusion.5), channel_id=1, source_target_pairs={{0,1},{1,0},{2,3},{3,2},{4,5},{5,4},{6,7},{7,6},{8,9},{9,8},{10,11... | collective-permute-start | bytes 786440 | tf_op jit(solution)/shard_map/ppermute | solution.py:26
  133.7 8.7 %collective-permute-start.12 = (bf16[1024,128]{1,0:T(8,128)(2,1)S(1)}, bf16[1024,128]{1,0:T(8,128)(2,1)S(1)}, u32[]{:S(2)}, u32[]{:S(2)}) collective-permute-start(bf16[1024,128]{1,0:T(8,128)(2,1)S(1)} %get-tuple-element.66), channel_id=1, source_target_pairs={{0,3},{1,2},{2,1},{3,0},{4,7},{5,6},{6,5},{7,4},{8,11},{9,10},{10,... | collective-permute-start | bytes 786440 | tf_op jit(solution)/shard_map/ppermute | solution.py:26
  133.8 13.5 %collective-permute-start.11 = (bf16[1024,128]{1,0:T(8,128)(2,1)S(1)}, bf16[1024,128]{1,0:T(8,128)(2,1)S(1)}, u32[]{:S(2)}, u32[]{:S(2)}) collective-permute-start(bf16[1024,128]{1,0:T(8,128)(2,1)S(1)} %get-tuple-element.67), channel_id=1, source_target_pairs={{0,2},{1,3},{2,0},{3,1},{4,6},{5,7},{6,4},{7,5},{8,10},{9,11},{10,... | collective-permute-start | bytes 786440 | tf_op jit(solution)/shard_map/ppermute | solution.py:26

commit v6 on v5

--- a/solution.py
+++ b/solution.py
@@ -28,8 +28,8 @@
 
 def pack_kernel(plane, heads, group, arrays, *refs):
     seg = refs[arrays] if group == 1 else None
-    outs, wide = refs[-2 - (plane - 1) * heads : -1], refs[-1]
-    length = outs[1].shape[0]
+    outs, wide = refs[-1 - plane * heads : -1], refs[-1]
+    length = outs[0].shape[0]
     me = lax.rem(lax.axis_index("ctx"), plane)
     for t, array in enumerate(refs[:arrays]):
         rows, count, _ = array.shape
@@ -40,19 +40,16 @@
         for h in range(heads):
             for k in range(plane):
                 first = ((me ^ k) * heads + h) * group
-                out = outs[0] if k == 0 else outs[h * (plane - 1) + k]
                 for g in range(group):
-                    at = (t * group + g) * rows + (h * length if k == 0 else 0)
-                    out[at : at + rows, :] = wide[
+                    at = (t * group + g) * rows
+                    outs[h * plane + k][at : at + rows, :] = wide[
                         pl.ds(first + g, rows, stride=pitch), :
                     ].astype(BF16)
     if group == 1:
         docs = seg[...].astype(F32)
         filler = jnp.zeros((TAIL - docs.shape[0], docs.shape[1]), F32)
         tail = jnp.concatenate([docs, filler], axis=0).astype(BF16)
-        for h in range(heads):
-            outs[0][(h + 1) * length - TAIL : (h + 1) * length, :] = tail
-        for out in outs[1:]:
+        for out in outs:
             out[length - TAIL :, :] = tail
 
 
@@ -61,13 +58,11 @@
     length = len(arrays) * group * rows + (0 if seg is None else TAIL)
     vmem = pl.BlockSpec(memory_space=pltpu.VMEM)
     inputs = list(arrays) + ([] if seg is None else [seg])
-    pieces = (plane - 1) * heads
     return pl.pallas_call(
         functools.partial(pack_kernel, plane, heads, group, len(arrays)),
-        out_shape=[jax.ShapeDtypeStruct((heads * length, width), BF16)]
-        + [jax.ShapeDtypeStruct((length, width), BF16)] * pieces,
+        out_shape=[jax.ShapeDtypeStruct((length, width), BF16)] * (plane * heads),
         in_specs=[vmem] * len(inputs),
-        out_specs=[vmem] * (1 + pieces),
+        out_specs=[vmem] * (plane * heads),
         scratch_shapes=[pltpu.VMEM((rows * (count + 1), width), F32)],
         name="pack",
     )(*inputs)
@@ -76,7 +71,9 @@
 def attend_kernel(plane, group, rows, width, head, picks, begin, end, *refs):
     half = plane // 2
     length = 4 * rows + TAIL
-    own, pairs, refs = refs[:plane], refs[plane : plane + 2], refs[plane + 2 :]
+    own, refs = refs[:plane], refs[plane:]
+    came = 2 if head == 0 else 1
+    pairs, refs = refs[:came], refs[came:]
     queries, refs = refs[: len(picks)], refs[len(picks) :]
     if not begin:
         start_sums, refs = refs[0], refs[1:]
@@ -85,6 +82,8 @@
     else:
         end_sums, refs = refs[0], refs[1:]
     ka, kd, vv, segs, qq, do, qt, qa, dt, s, sd, u, ud, acc, tri, lims, sem = refs
+    if not end:
+        acc = end_sums
     device = lax.axis_index("ctx")
     me = lax.rem(device, plane)
     span = group * rows
@@ -100,20 +99,19 @@
 
     low, high = pl.ds(0, width), pl.ds(width, width)
     for k in range(plane):
-        mine = (own[k], head * length if k == 0 else 0, plane)
-        past = (pairs[min(k, 1)], (head if k == 0 else k - 1) * length, 0)
+        mine = (own[k], 0, plane)
+        past = (pairs[min(k, came - 1)], max(k - came + 1, 0) * length, 0)
         for piece, start, base in (mine, past):
             block = base + (me ^ k)
             part = [piece.at[pl.ds(start + t * rows, rows), :] for t in range(4)]
             fetch(part[0], ka.at[block, :, low])
             fetch(part[0], kd.at[block, :, high])
-            fetch(part[1], vv.at[block, 0])
+            fetch(part[1], vv.at[block, pl.ds(0, rows)])
             fetch(part[2], kd.at[block, :, low])
-            fetch(part[3], vv.at[block, 1])
+            fetch(part[3], vv.at[block, pl.ds(rows, rows)])
             fetch(piece.at[pl.ds(start + 4 * rows, TAIL), :], segs.at[block])
     for i, k in enumerate(picks):
-        start = head * 3 * span if k == 0 else 0
-        part = [queries[i].at[pl.ds(start + t * span, span), :] for t in range(3)]
+        part = [queries[i].at[pl.ds(t * span, span), :] for t in range(3)]
         fetch(part[0], qq.at[i, :, low])
         fetch(part[1], qq.at[i, :, high])
         fetch(part[2], do.at[i])
@@ -149,14 +147,14 @@
         a = me ^ (picks[0] + i)
         first = lims[0, plane + a]
         skip = sum((lims[1, a + b] < first).astype(jnp.int32) for b in range(plane))
-        both = qq[i].astype(F32).T.astype(BF16)
+        both = qq[i].T
         qt[...] = both
         qa[:width, :] = both[:width, :]
         docs = document_row(plane + a)
         cover = jnp.where(names == docs, 0.0, HIDDEN).astype(BF16)
         for g in range(group):
             qa[width:, g * rows : (g + 1) * rows] = cover
-        dt[...] = do[i].astype(F32).T.astype(BF16)
+        dt[...] = do[i].T
 
         def score(b, bias, top):
             value = jnp.dot(ka[a + b], qa[...], preferred_element_type=F32)
@@ -177,9 +175,9 @@
             s[b] = weight
             dot = factor * jnp.dot(kd[a + b], qt[...], preferred_element_type=F32)
             sd[b] = dot
-            up = jnp.dot(vv[a + b, 0], dt[...], preferred_element_type=F32)
+            stacked = jnp.dot(vv[a + b], dt[...], preferred_element_type=F32)
+            up, updot = stacked[:rows], stacked[rows:]
             u[b] = up
-            updot = jnp.dot(vv[a + b, 1], dt[...], preferred_element_type=F32)
             ud[b] = updot
             total = total + jnp.sum(folded(weight), axis=0)
             dots = dots + jnp.sum(folded(weight * dot), axis=0)
@@ -219,7 +217,6 @@
 
     lax.fori_loop(0, len(picks), one_block, 0)
     if not end:
-        end_sums[...] = acc[...]
         return
     for k in range(plane):
         for t in range(4):
@@ -257,7 +254,7 @@
         scratch_shapes=[
             pltpu.VMEM((blocks, rows, 2 * width), BF16),
             pltpu.VMEM((blocks, rows, 2 * width), BF16),
-            pltpu.VMEM((blocks, 2, rows, width), BF16),
+            pltpu.VMEM((blocks, 2 * rows, width), BF16),
             pltpu.VMEM((blocks, TAIL, width), BF16),
             pltpu.VMEM((len(picks), span, 2 * width), BF16),
             pltpu.VMEM((len(picks), span, width), BF16),
@@ -267,7 +264,7 @@
         ]
         + [pltpu.VMEM((plane + 1, rows, span), F32)] * 4
         + [
-            pltpu.VMEM((blocks, 4, rows, width), F32),
+            pltpu.VMEM((blocks if end else 1, 4, rows, width), F32),
             pltpu.VMEM((2, rows, span), F32),
             pltpu.SMEM((2, blocks), F32),
             pltpu.SemaphoreType.DMA((12 * plane + 3 * len(picks),)),
@@ -329,19 +326,22 @@
     far_first = list(range(half, plane)) + list(range(1, half))
 
     def spread(blocks, h):
-        results = [blocks[0]] + [None] * (plane - 1)
+        results = [blocks[h * plane]] + [None] * (plane - 1)
         for k in far_first:
-            results[k] = swapped(blocks[h * (plane - 1) + k], k)
+            results[k] = swapped(blocks[h * plane + k], k)
         return results
 
     seg = segment_ids.reshape(rows // width, width)
     kv = pack((keys, values, key_direction, value_direction), plane, heads, 1, seg)
     qs = pack((query, query_tangent, out_cotangent), plane, heads, group)
-    first = shifted(kv[0], plane)
+    first = [shifted(kv[0], plane)]
     pieces, returned = [], []
     for h in range(heads):
         own = spread(kv, h)
-        pairs = [first, shifted(jnp.concatenate(own[1:], axis=0), plane)]
+        rest = own[1:] if h == 0 else own
+        pairs = (first if h == 0 else []) + [
+            shifted(jnp.concatenate(rest, axis=0), plane)
+        ]
         queries = spread(qs, h)
         near, far, every = range(half), range(half, plane), range(plane)
         if h == 0:

time: 153 us -> 158 us (1.033)
  the two profiles are of different devices: /device:TPU:21 before, /device:TPU:0 now
where the time goes in v6:
time: 158 us; the launch traced here: 157 us
  waiting for transfers between devices  82.6 us (52%)
  Pallas kernels  38.7 us (24%)
  starting transfers between devices  31.9 us (20%)
  other arithmetic  2.31 us (1%)
    ppermute x18, waiting for transfers between devices, swapped(): return lax.ppermute(block, 'ctx', [(i, i ^ partner) for i in devices])  50.6 us
    ppermute x7, waiting for transfers between devices, shifted(): return lax.ppermute(block, 'ctx', route)  32 us
    pallas_call x3, Pallas kernels, attend(): pl.pallas_call(functools.partial(attend_kernel, plane, group, rows, width...  28.3 us
    ppermute x7, starting transfers between devices, shifted(): return lax.ppermute(block, 'ctx', route)  17.4 us
    ppermute x18, starting transfers between devices, swapped(): return lax.ppermute(block, 'ctx', [(i, i ^ partner) for i in devices])  14.5 us
    pallas_call x2, Pallas kernels, pack(): pl.pallas_call(functools.partial(pack_kernel, plane, heads, group, len(ar...  7.91 us
  transfers between devices with their start and end apart: 25, of which 12 were waited for; matrix products, arithmetic and copies ran while one was open for 1% of the time, Pallas kernels for 21%

profile of v6, /device:TPU:0, one launch (start us, length us, event | category | flops | bytes accessed | tf_op | source)
XLA Modules:
  0.0 157.3 jit_solution(14762269019240327398)
XLA Ops:
  0.6 3.5 %pack.2 = (bf16[1040,128]{1,0:T(8,128)(2,1)}, bf16[1040,128]{1,0:T(8,128)(2,1)}, bf16[1040,128]{1,0:T(8,128)(2,1)}, bf16[1040,128]{1,0:T(8,128)(2,1)}, bf16[1040...) custom-call(bf16[256,8,128]{2,1,0:T(8,128)(2,1)} %refs_0_.2, ...), custom_call_target="tpu_custom_call" | custom-call | tf_op jit(solution)/shard_map/pack/pallas_call | solution.py:61
  4.2 0.5 collective-permute-start
  4.6 2.6 %collective-permute-start.1 = (bf16[1040,128]{1,0:T(8,128)(2,1)}, bf16[1040,128]{1,0:T(8,128)(2,1)S(1)}, u32[]{:S(2)}, u32[]{:S(2)}) collective-permute-start(bf16[1040,128]{1,0:T(8,128)(2,1)} %get-tuple-element.38), channel_id=1, source_target_pairs={{0,2},{1,3},{2,0},{3,1},{4,6},{5,7},{6,4},{7,5},{8,10},{9,11},{10,... | collective-permute-start | bytes 798728 | tf_op jit(solution)/shard_map/ppermute | solution.py:26
  7.2 0.0 collective-permute-start.2
  7.3 0.1 collective-permute-start.13
  7.4 1.9 %collective-permute-start.14 = (bf16[1040,128]{1,0:T(8,128)(2,1)}, bf16[1040,128]{1,0:T(8,128)(2,1)S(1)}, u32[]{:S(2)}, u32[]{:S(2)}) collective-permute-start(bf16[1040,128]{1,0:T(8,128)(2,1)} %get-tuple-element.52), channel_id=1, source_target_pairs={{0,2},{1,3},{2,0},{3,1},{4,6},{5,7},{6,4},{7,5},{8,10},{9,11},{10,... | collective-permute-start | bytes 798728 | tf_op jit(solution)/shard_map/ppermute | solution.py:26
  9.4 5.3 %collective-permute-done.1.refs_2_ = bf16[1040,128]{1,0:T(8,128)(2,1)S(1)} collective-permute-done((bf16[1040,128]{1,0:T(8,128)(2,1)}, bf16[1040,128]{1,0:T(8,128)(2,1)S(1)}, u32[]{:S(2)}, u32[]{:S(2)}) %collective-permute-start.1) | collective-permute-done | bytes 266272 | tf_op jit(solution)/shard_map/ppermute | solution.py:26
  14.7 4.0 %collective-permute-start.3 = (bf16[1040,128]{1,0:T(8,128)(2,1)}, bf16[1040,128]{1,0:T(8,128)(2,1)S(1)}, u32[]{:S(2)}, u32[]{:S(2)}) collective-permute-start(bf16[1040,128]{1,0:T(8,128)(2,1)} %get-tuple-element.36.refs_0_), channel_id=1, source_target_pairs={{0,4},{1,5},{2,6},{3,7},{4,8},{5,9},{6,10},{7,11},{8,12},{9,13},{1... | collective-permute-start | bytes 798728 | tf_op jit(solution)/shard_map/ppermute | solution.py:21
  18.7 1.4 collective-permute-done.2.refs_3_
  20.0 0.9 pad_maximum_fusion.1
  21.0 3.5 %collective-permute-start.4 = (bf16[3120,128]{1,0:T(8,128)(2,1)}, bf16[3120,128]{1,0:T(8,128)(2,1)S(1)}, u32[]{:S(2)}, u32[]{:S(2)}) collective-permute-start(bf16[3120,128]{1,0:T(8,128)(2,1)} %pad_maximum_fusion.1), channel_id=1, source_target_pairs={{0,4},{1,5},{2,6},{3,7},{4,8},{5,9},{6,10},{7,11},{8,12},{9,13},{1... | collective-permute-start | bytes 2396168 | tf_op jit(solution)/shard_map/ppermute | solution.py:21
  24.5 1.6 %collective-permute-done.14.refs_2_ = bf16[1040,128]{1,0:T(8,128)(2,1)S(1)} collective-permute-done((bf16[1040,128]{1,0:T(8,128)(2,1)}, bf16[1040,128]{1,0:T(8,128)(2,1)S(1)}, u32[]{:S(2)}, u32[]{:S(2)}) %collective-permute-start.14) | collective-permute-done | bytes 266272 | tf_op jit(solution)/shard_map/ppermute | solution.py:26
  26.1 5.2 %collective-permute-done.15.refs_3_ = bf16[1040,128]{1,0:T(8,128)(2,1)S(1)} collective-permute-done((bf16[1040,128]{1,0:T(8,128)(2,1)}, bf16[1040,128]{1,0:T(8,128)(2,1)S(1)}, u32[]{:S(2)}, u32[]{:S(2)}) %collective-permute-start.15) | collective-permute-done | bytes 266272 | tf_op jit(solution)/shard_map/ppermute | solution.py:26
  31.3 1.1 pad_maximum_fusion
  32.3 4.5 %collective-permute-start.16 = (bf16[4160,128]{1,0:T(8,128)(2,1)}, bf16[4160,128]{1,0:T(8,128)(2,1)}, u32[]{:S(2)}, u32[]{:S(2)}) collective-permute-start(bf16[4160,128]{1,0:T(8,128)(2,1)} %pad_maximum_fusion), channel_id=1, source_target_pairs={{0,4},{1,5},{2,6},{3,7},{4,8},{5,9},{6,10},{7,11},{8,12},{9,13},{1... | collective-permute-start | bytes 3194888 | tf_op jit(solution)/shard_map/ppermute | solution.py:21
  36.9 4.4 %pack.3 = (bf16[1536,128]{1,0:T(8,128)(2,1)}, bf16[1536,128]{1,0:T(8,128)(2,1)}, bf16[1536,128]{1,0:T(8,128)(2,1)}, bf16[1536,128]{1,0:T(8,128)(2,1)}, bf16[1536...) custom-call(bf16[256,16,128]{2,1,0:T(8,128)(2,1)} %refs_0_.3, ...), custom_call_target="tpu_custom_call" | custom-call | tf_op jit(solution)/shard_map/pack/pallas_call | solution.py:61
  41.3 0.4 collective-permute-start.7
  41.6 1.5 collective-permute-start.5
  43.2 0.6 collective-permute-start.17
  43.8 1.0 copy-done.3
  44.8 6.8 %attend.3.refs_8_ = f32[8,4,256,128]{3,2,1,0:T(8,128)S(1)} custom-call(bf16[1040,128]{1,0:T(8,128)(2,1)S(1)} %copy-done, bf16[1040,128]{1,0:T(8,128)(2,1)S(1)} %collective-permute-done.refs_1_, bf16[1040,128]{1,0:T(8,128)(2,1)S(1)} %collective-permute-done.1.refs_2_, bf16[1040,128]{1,0:T(8,128)(2,1)S(1)} %collective-permute-done.2.refs_3_, ...), custom_call_target="tpu_custom_call" | custom-call | tf_op jit(solution)/shard_map/attend/pallas_call | solution.py:247
  51.6 2.2 %collective-permute-done.5.refs_6_ = bf16[1536,128]{1,0:T(8,128)(2,1)S(1)} collective-permute-done((bf16[1536,128]{1,0:T(8,128)(2,1)}, bf16[1536,128]{1,0:T(8,128)(2,1)S(1)}, u32[]{:S(2)}, u32[]{:S(2)}) %collective-permute-start.5) | collective-permute-done | bytes 393248 | tf_op jit(solution)/shard_map/ppermute | solution.py:26
  53.8 6.8 %collective-permute-done.6.refs_7_ = bf16[1536,128]{1,0:T(8,128)(2,1)S(1)} collective-permute-done((bf16[1536,128]{1,0:T(8,128)(2,1)}, bf16[1536,128]{1,0:T(8,128)(2,1)S(1)}, u32[]{:S(2)}, u32[]{:S(2)}) %collective-permute-start.6) | collective-permute-done | bytes 393248 | tf_op jit(solution)/shard_map/ppermute | solution.py:26
  60.6 9.2 %attend.4 = (bf16[2048,128]{1,0:T(8,128)(2,1)S(1)}, bf16[2048,128]{1,0:T(8,128)(2,1)S(1)}, f32[1024,128]{1,0:T(8,128)S(1)}, f32[1024,128]{1,0:T(8,128)S(1)}, f32...) custom-call(bf16[1040,128]{1,0:T(8,128)(2,1)S(1)} %copy-done, bf16[1040,128]{1,0:T(8,128)(2,1)S(1)} %collective-permute-done.refs_1_, ...), custom_call_target="tpu_custom_call" | custom-call | tf_op jit(solution)/shard_map/attend/pallas_call | solution.py:247
  69.8 1.3 collective-permute-start.8
  71.2 0.1 collective-permute-start.18
  71.2 1.9 %collective-permute-start.19 = (bf16[1536,128]{1,0:T(8,128)(2,1)S(1)}, bf16[1536,128]{1,0:T(8,128)(2,1)S(1)}, u32[]{:S(2)}, u32[]{:S(2)}) collective-permute-start(bf16[1536,128]{1,0:T(8,128)(2,1)S(1)} %copy-done.4), channel_id=1, source_target_pairs={{0,3},{1,2},{2,1},{3,0},{4,7},{5,6},{6,5},{7,4},{8,11},{9,10},{10,... | collective-permute-start | bytes 1179656 | tf_op jit(solution)/shard_map/ppermute | solution.py:26
  73.2 1.5 collective-permute-start.10
  74.7 8.5 %collective-permute-done.18.refs_7_ = bf16[1536,128]{1,0:T(8,128)(2,1)S(1)} collective-permute-done((bf16[1536,128]{1,0:T(8,128)(2,1)S(1)}, bf16[1536,128]{1,0:T(8,128)(2,1)S(1)}, u32[]{:S(2)}, u32[]{:S(2)}) %collective-permute-start.18) | collective-permute-done | bytes 393248 | tf_op jit(solution)/shard_map/ppermute | solution.py:26
  83.2 7.7 %collective-permute-done.19.refs_8_ = bf16[1536,128]{1,0:T(8,128)(2,1)S(1)} collective-permute-done((bf16[1536,128]{1,0:T(8,128)(2,1)S(1)}, bf16[1536,128]{1,0:T(8,128)(2,1)S(1)}, u32[]{:S(2)}, u32[]{:S(2)}) %collective-permute-start.19) | collective-permute-done | bytes 393248 | tf_op jit(solution)/shard_map/ppermute | solution.py:26
  90.9 12.3 %attend.5 = (bf16[2048,128]{1,0:T(8,128)(2,1)S(1)}, bf16[2048,128]{1,0:T(8,128)(2,1)S(1)}, f32[1024,128]{1,0:T(8,128)S(1)}, f32[1024,128]{1,0:T(8,128)S(1)}, f32...) custom-call(bf16[1040,128]{1,0:T(8,128)(2,1)S(1)} %copy-done.1, bf16[1040,128]{1,0:T(8,128)(2,1)S(1)} %collective-permute-done.13.refs_1_, ...), custom_call_target="tpu_custom_call" | custom-call | tf_op jit(solution)/shard_map/attend/pallas_call | solution.py:247
  103.3 1.3 collective-permute-start.20
  104.6 1.3 collective-permute-start.22
  105.9 0.1 add_convert_fusion.5
  106.0 0.6 collective-permute-start.9
  106.5 0.1 add_convert_fusion.3
  106.6 0.3 collective-permute-start.12
  106.9 1.5 collective-permute-start.11
  108.3 21.9 %collective-permute-done.20 = bf16[2048,128]{1,0:T(8,128)(2,1)S(1)} collective-permute-done((bf16[2048,128]{1,0:T(8,128)(2,1)S(1)}, bf16[2048,128]{1,0:T(8,128)(2,1)S(1)}, u32[]{:S(2)}, u32[]{:S(2)}) %collective-permute-start.20) | collective-permute-done | bytes 524320 | tf_op jit(solution)/shard_map/ppermute | solution.py:21
  130.2 0.1 add_convert_fusion.2
  130.3 0.1 collective-permute-start.21
  130.3 10.1 %collective-permute-done.22 = bf16[2048,128]{1,0:T(8,128)(2,1)S(1)} collective-permute-done((bf16[2048,128]{1,0:T(8,128)(2,1)S(1)}, bf16[2048,128]{1,0:T(8,128)(2,1)S(1)}, u32[]{:S(2)}, u32[]{:S(2)}) %collective-permute-start.22) | collective-permute-done | bytes 524320 | tf_op jit(solution)/shard_map/ppermute | solution.py:21
  140.5 0.1 add_convert_fusion
  140.6 1.4 collective-permute-start.24
  142.0 1.0 collective-permute-start.23
  143.0 5.3 %collective-permute-done.24 = bf16[1024,128]{1,0:T(8,128)(2,1)S(1)} collective-permute-done((bf16[1024,128]{1,0:T(8,128)(2,1)S(1)}, bf16[1024,128]{1,0:T(8,128)(2,1)S(1)}, u32[]{:S(2)}, u32[]{:S(2)}) %collective-permute-start.24) | collective-permute-done | bytes 262176 | tf_op jit(solution)/shard_map/ppermute | solution.py:26
  148.4 6.5 %collective-permute-done.23 = bf16[1024,128]{1,0:T(8,128)(2,1)S(1)} collective-permute-done((bf16[1024,128]{1,0:T(8,128)(2,1)S(1)}, bf16[1024,128]{1,0:T(8,128)(2,1)S(1)}, u32[]{:S(2)}, u32[]{:S(2)}) %collective-permute-start.23) | collective-permute-done | bytes 262176 | tf_op jit(solution)/shard_map/ppermute | solution.py:26
  154.9 2.5 %finish.1 = (f32[2048,128]{1,0:T(8,128)}, f32[2048,128]{1,0:T(8,128)}, f32[2048,128]{1,0:T(8,128)}, f32[2048,128]{1,0:T(8,128)}) custom-call(f32[4,256,128]{2,1,0:T(8,128)S(1)} %bitcast.17, bf16[4,256,128]{2,1,0:T(8,128)(2,1)S(1)} %bitcast.19, bf16[4,256,128]{2,1,0:T(8,128)(2,1)S(1)} %bitcast.21, bf16[4,256,128]{2,1,0:T(8,128)(2,1)S(1)} %bitcast.20, ...), custom_call_target="tpu_custom_call" | custom-call | tf_op jit(solution)/shard_map/finish/pallas_call | solution.py:306
  (26 shorter events, 0.1 us)
Async XLA Ops:
  4.1 27.1 %copy-start.1 = (bf16[1040,128]{1,0:T(8,128)(2,1)S(1)}, bf16[1040,128]{1,0:T(8,128)(2,1)}, u32[]{:S(2)}) copy-start(bf16[1040,128]{1,0:T(8,128)(2,1)} %get-tuple-element.50.refs_0_) | copy-start | bytes 798724
  4.2 5.2 %collective-permute-start = (bf16[1040,128]{1,0:T(8,128)(2,1)}, bf16[1040,128]{1,0:T(8,128)(2,1)S(1)}, u32[]{:S(2)}, u32[]{:S(2)}) collective-permute-start(bf16[1040,128]{1,0:T(8,128)(2,1)} %get-tuple-element.37), channel_id=1, source_target_pairs={{0,1},{1,0},{2,3},{3,2},{4,5},{5,4},{6,7},{7,6},{8,9},{9,8},{10,11... | collective-permute-start | bytes 798728 | tf_op jit(solution)/shard_map/ppermute | solution.py:26
  4.6 10.0 %collective-permute-start.1 = (bf16[1040,128]{1,0:T(8,128)(2,1)}, bf16[1040,128]{1,0:T(8,128)(2,1)S(1)}, u32[]{:S(2)}, u32[]{:S(2)}) collective-permute-start(bf16[1040,128]{1,0:T(8,128)(2,1)} %get-tuple-element.38), channel_id=1, source_target_pairs={{0,2},{1,3},{2,0},{3,1},{4,6},{5,7},{6,4},{7,5},{8,10},{9,11},{10,... | collective-permute-start | bytes 798728 | tf_op jit(solution)/shard_map/ppermute | solution.py:26
  7.2 12.8 %collective-permute-start.2 = (bf16[1040,128]{1,0:T(8,128)(2,1)}, bf16[1040,128]{1,0:T(8,128)(2,1)S(1)}, u32[]{:S(2)}, u32[]{:S(2)}) collective-permute-start(bf16[1040,128]{1,0:T(8,128)(2,1)} %get-tuple-element.39), channel_id=1, source_target_pairs={{0,3},{1,2},{2,1},{3,0},{4,7},{5,6},{6,5},{7,4},{8,11},{9,10},{10,... | collective-permute-start | bytes 798728 | tf_op jit(solution)/shard_map/ppermute | solution.py:26
  7.3 17.2 %collective-permute-start.13 = (bf16[1040,128]{1,0:T(8,128)(2,1)}, bf16[1040,128]{1,0:T(8,128)(2,1)S(1)}, u32[]{:S(2)}, u32[]{:S(2)}) collective-permute-start(bf16[1040,128]{1,0:T(8,128)(2,1)} %get-tuple-element.51), channel_id=1, source_target_pairs={{0,1},{1,0},{2,3},{3,2},{4,5},{5,4},{6,7},{7,6},{8,9},{9,8},{10,11... | collective-permute-start | bytes 798728 | tf_op jit(solution)/shard_map/ppermute | solution.py:26
  7.4 18.7 %collective-permute-start.14 = (bf16[1040,128]{1,0:T(8,128)(2,1)}, bf16[1040,128]{1,0:T(8,128)(2,1)S(1)}, u32[]{:S(2)}, u32[]{:S(2)}) collective-permute-start(bf16[1040,128]{1,0:T(8,128)(2,1)} %get-tuple-element.52), channel_id=1, source_target_pairs={{0,2},{1,3},{2,0},{3,1},{4,6},{5,7},{6,4},{7,5},{8,10},{9,11},{10,... | collective-permute-start | bytes 798728 | tf_op jit(solution)/shard_map/ppermute | solution.py:26
  9.4 21.9 %collective-permute-start.15 = (bf16[1040,128]{1,0:T(8,128)(2,1)}, bf16[1040,128]{1,0:T(8,128)(2,1)S(1)}, u32[]{:S(2)}, u32[]{:S(2)}) collective-permute-start(bf16[1040,128]{1,0:T(8,128)(2,1)} %get-tuple-element.53), channel_id=1, source_target_pairs={{0,3},{1,2},{2,1},{3,0},{4,7},{5,6},{6,5},{7,4},{8,11},{9,10},{10,... | collective-permute-start | bytes 798728 | tf_op jit(solution)/shard_map/ppermute | solution.py:26
  14.7 28.5 %collective-permute-start.3 = (bf16[1040,128]{1,0:T(8,128)(2,1)}, bf16[1040,128]{1,0:T(8,128)(2,1)S(1)}, u32[]{:S(2)}, u32[]{:S(2)}) collective-permute-start(bf16[1040,128]{1,0:T(8,128)(2,1)} %get-tuple-element.36.refs_0_), channel_id=1, source_target_pairs={{0,4},{1,5},{2,6},{3,7},{4,8},{5,9},{6,10},{7,11},{8,12},{9,13},{1... | collective-permute-start | bytes 798728 | tf_op jit(solution)/shard_map/ppermute | solution.py:21
  21.0 22.8 %collective-permute-start.4 = (bf16[3120,128]{1,0:T(8,128)(2,1)}, bf16[3120,128]{1,0:T(8,128)(2,1)S(1)}, u32[]{:S(2)}, u32[]{:S(2)}) collective-permute-start(bf16[3120,128]{1,0:T(8,128)(2,1)} %pad_maximum_fusion.1), channel_id=1, source_target_pairs={{0,4},{1,5},{2,6},{3,7},{4,8},{5,9},{6,10},{7,11},{8,12},{9,13},{1... | collective-permute-start | bytes 2396168 | tf_op jit(solution)/shard_map/ppermute | solution.py:21
  32.3 11.4 %copy-start = (bf16[1040,128]{1,0:T(8,128)(2,1)S(1)}, bf16[1040,128]{1,0:T(8,128)(2,1)}, u32[]{:S(2)}) copy-start(bf16[1040,128]{1,0:T(8,128)(2,1)} %get-tuple-element.36.refs_0_) | copy-start | bytes 798724
  32.3 58.6 %collective-permute-start.16 = (bf16[4160,128]{1,0:T(8,128)(2,1)}, bf16[4160,128]{1,0:T(8,128)(2,1)}, u32[]{:S(2)}, u32[]{:S(2)}) collective-permute-start(bf16[4160,128]{1,0:T(8,128)(2,1)} %pad_maximum_fusion), channel_id=1, source_target_pairs={{0,4},{1,5},{2,6},{3,7},{4,8},{5,9},{6,10},{7,11},{8,12},{9,13},{1... | collective-permute-start | bytes 3194888 | tf_op jit(solution)/shard_map/ppermute | solution.py:21
  41.3 1.9 %collective-permute-start.7 = (bf16[1536,128]{1,0:T(8,128)(2,1)}, bf16[1536,128]{1,0:T(8,128)(2,1)S(1)}, u32[]{:S(2)}, u32[]{:S(2)}) collective-permute-start(bf16[1536,128]{1,0:T(8,128)(2,1)} %get-tuple-element.43), channel_id=1, source_target_pairs={{0,1},{1,0},{2,3},{3,2},{4,5},{5,4},{6,7},{7,6},{8,9},{9,8},{10,11... | collective-permute-start | bytes 1179656 | tf_op jit(solution)/shard_map/ppermute | solution.py:26
  41.6 12.2 %collective-permute-start.5 = (bf16[1536,128]{1,0:T(8,128)(2,1)}, bf16[1536,128]{1,0:T(8,128)(2,1)S(1)}, u32[]{:S(2)}, u32[]{:S(2)}) collective-permute-start(bf16[1536,128]{1,0:T(8,128)(2,1)} %get-tuple-element.40), channel_id=1, source_target_pairs={{0,2},{1,3},{2,0},{3,1},{4,6},{5,7},{6,4},{7,5},{8,10},{9,11},{10,... | collective-permute-start | bytes 1179656 | tf_op jit(solution)/shard_map/ppermute | solution.py:26
  43.1 17.5 %collective-permute-start.6 = (bf16[1536,128]{1,0:T(8,128)(2,1)}, bf16[1536,128]{1,0:T(8,128)(2,1)S(1)}, u32[]{:S(2)}, u32[]{:S(2)}) collective-permute-start(bf16[1536,128]{1,0:T(8,128)(2,1)} %get-tuple-element.41), channel_id=1, source_target_pairs={{0,3},{1,2},{2,1},{3,0},{4,7},{5,6},{6,5},{7,4},{8,11},{9,10},{10,... | collective-permute-start | bytes 1179656 | tf_op jit(solution)/shard_map/ppermute | solution.py:26
  43.2 30.0 %collective-permute-start.17 = (bf16[1536,128]{1,0:T(8,128)(2,1)}, bf16[1536,128]{1,0:T(8,128)(2,1)S(1)}, u32[]{:S(2)}, u32[]{:S(2)}) collective-permute-start(bf16[1536,128]{1,0:T(8,128)(2,1)} %get-tuple-element.55), channel_id=1, source_target_pairs={{0,1},{1,0},{2,3},{3,2},{4,5},{5,4},{6,7},{7,6},{8,9},{9,8},{10,11... | collective-permute-start | bytes 1179656 | tf_op jit(solution)/shard_map/ppermute | solution.py:26
  43.8 1.0 copy-start.3
  51.6 19.6 %copy-start.5 = (bf16[1536,128]{1,0:T(8,128)(2,1)S(1)}, bf16[1536,128]{1,0:T(8,128)(2,1)}, u32[]{:S(2)}) copy-start(bf16[1536,128]{1,0:T(8,128)(2,1)} %get-tuple-element.56) | copy-start | bytes 1179652
  51.6 19.7 %copy-start.4 = (bf16[1536,128]{1,0:T(8,128)(2,1)S(1)}, bf16[1536,128]{1,0:T(8,128)(2,1)}, u32[]{:S(2)}) copy-start(bf16[1536,128]{1,0:T(8,128)(2,1)} %get-tuple-element.57) | copy-start | bytes 1179652
  51.6 39.4 %copy-start.2 = (bf16[1536,128]{1,0:T(8,128)(2,1)S(1)}, bf16[1536,128]{1,0:T(8,128)(2,1)}, u32[]{:S(2)}) copy-start(bf16[1536,128]{1,0:T(8,128)(2,1)} %get-tuple-element.54.refs_5_) | copy-start | bytes 1179652
  69.8 36.0 %collective-permute-start.8 = (bf16[2048,128]{1,0:T(8,128)(2,1)S(1)}, bf16[2048,128]{1,0:T(8,128)(2,1)S(1)}, u32[]{:S(2)}, u32[]{:S(2)}) collective-permute-start(bf16[2048,128]{1,0:T(8,128)(2,1)S(1)} %get-tuple-element.46), channel_id=1, source_target_pairs={{4,0},{5,1},{6,2},{7,3},{8,4},{9,5},{10,6},{11,7},{12,8},{13,9},{1... | collective-permute-start | bytes 1572872 | tf_op jit(solution)/shard_map/ppermute | solution.py:21
  71.2 12.1 %collective-permute-start.18 = (bf16[1536,128]{1,0:T(8,128)(2,1)S(1)}, bf16[1536,128]{1,0:T(8,128)(2,1)S(1)}, u32[]{:S(2)}, u32[]{:S(2)}) collective-permute-start(bf16[1536,128]{1,0:T(8,128)(2,1)S(1)} %copy-done.5), channel_id=1, source_target_pairs={{0,2},{1,3},{2,0},{3,1},{4,6},{5,7},{6,4},{7,5},{8,10},{9,11},{10,... | collective-permute-start | bytes 1179656 | tf_op jit(solution)/shard_map/ppermute | solution.py:26
  71.2 19.7 %collective-permute-start.19 = (bf16[1536,128]{1,0:T(8,128)(2,1)S(1)}, bf16[1536,128]{1,0:T(8,128)(2,1)S(1)}, u32[]{:S(2)}, u32[]{:S(2)}) collective-permute-start(bf16[1536,128]{1,0:T(8,128)(2,1)S(1)} %copy-done.4), channel_id=1, source_target_pairs={{0,3},{1,2},{2,1},{3,0},{4,7},{5,6},{6,5},{7,4},{8,11},{9,10},{10,... | collective-permute-start | bytes 1179656 | tf_op jit(solution)/shard_map/ppermute | solution.py:26
  73.2 33.3 %collective-permute-start.10 = (bf16[2048,128]{1,0:T(8,128)(2,1)S(1)}, bf16[2048,128]{1,0:T(8,128)(2,1)S(1)}, u32[]{:S(2)}, u32[]{:S(2)}) collective-permute-start(bf16[2048,128]{1,0:T(8,128)(2,1)S(1)} %get-tuple-element.48), channel_id=1, source_target_pairs={{4,0},{5,1},{6,2},{7,3},{8,4},{9,5},{10,6},{11,7},{12,8},{13,9},{1... | collective-permute-start | bytes 1572872 | tf_op jit(solution)/shard_map/ppermute | solution.py:21
  103.3 26.9 %collective-permute-start.20 = (bf16[2048,128]{1,0:T(8,128)(2,1)S(1)}, bf16[2048,128]{1,0:T(8,128)(2,1)S(1)}, u32[]{:S(2)}, u32[]{:S(2)}) collective-permute-start(bf16[2048,128]{1,0:T(8,128)(2,1)S(1)} %get-tuple-element.60), channel_id=1, source_target_pairs={{4,0},{5,1},{6,2},{7,3},{8,4},{9,5},{10,6},{11,7},{12,8},{13,9},{1... | collective-permute-start | bytes 1572872 | tf_op jit(solution)/shard_map/ppermute | solution.py:21
  104.6 35.9 %collective-permute-start.22 = (bf16[2048,128]{1,0:T(8,128)(2,1)S(1)}, bf16[2048,128]{1,0:T(8,128)(2,1)S(1)}, u32[]{:S(2)}, u32[]{:S(2)}) collective-permute-start(bf16[2048,128]{1,0:T(8,128)(2,1)S(1)} %get-tuple-element.62), channel_id=1, source_target_pairs={{4,0},{5,1},{6,2},{7,3},{8,4},{9,5},{10,6},{11,7},{12,8},{13,9},{1... | collective-permute-start | bytes 1572872 | tf_op jit(solution)/shard_map/ppermute | solution.py:21
  106.0 36.0 %collective-permute-start.9 = (bf16[1024,128]{1,0:T(8,128)(2,1)S(1)}, bf16[1024,128]{1,0:T(8,128)(2,1)S(1)}, u32[]{:S(2)}, u32[]{:S(2)}) collective-permute-start(bf16[1024,128]{1,0:T(8,128)(2,1)S(1)} %add_convert_fusion.5), channel_id=1, source_target_pairs={{0,1},{1,0},{2,3},{3,2},{4,5},{5,4},{6,7},{7,6},{8,9},{9,8},{10,11... | collective-permute-start | bytes 786440 | tf_op jit(solution)/shard_map/ppermute | solution.py:26
  106.6 36.4 %collective-permute-start.12 = (bf16[1024,128]{1,0:T(8,128)(2,1)S(1)}, bf16[1024,128]{1,0:T(8,128)(2,1)S(1)}, u32[]{:S(2)}, u32[]{:S(2)}) collective-permute-start(bf16[1024,128]{1,0:T(8,128)(2,1)S(1)} %get-tuple-element.70), channel_id=1, source_target_pairs={{0,3},{1,2},{2,1},{3,0},{4,7},{5,6},{6,5},{7,4},{8,11},{9,10},{10,... | collective-permute-start | bytes 786440 | tf_op jit(solution)/shard_map/ppermute | solution.py:26
  106.9 36.2 %collective-permute-start.11 = (bf16[1024,128]{1,0:T(8,128)(2,1)S(1)}, bf16[1024,128]{1,0:T(8,128)(2,1)S(1)}, u32[]{:S(2)}, u32[]{:S(2)}) collective-permute-start(bf16[1024,128]{1,0:T(8,128)(2,1)S(1)} %get-tuple-element.71), channel_id=1, source_target_pairs={{0,2},{1,3},{2,0},{3,1},{4,6},{5,7},{6,4},{7,5},{8,10},{9,11},{10,... | collective-permute-start | bytes 786440 | tf_op jit(solution)/shard_map/ppermute | solution.py:26
  130.3 12.8 %collective-permute-start.21 = (bf16[1024,128]{1,0:T(8,128)(2,1)S(1)}, bf16[1024,128]{1,0:T(8,128)(2,1)S(1)}, u32[]{:S(2)}, u32[]{:S(2)}) collective-permute-start(bf16[1024,128]{1,0:T(8,128)(2,1)S(1)} %add_convert_fusion.2), channel_id=1, source_target_pairs={{0,1},{1,0},{2,3},{3,2},{4,5},{5,4},{6,7},{7,6},{8,9},{9,8},{10,11... | collective-permute-start | bytes 786440 | tf_op jit(solution)/shard_map/ppermute | solution.py:26
  140.6 7.8 %collective-permute-start.24 = (bf16[1024,128]{1,0:T(8,128)(2,1)S(1)}, bf16[1024,128]{1,0:T(8,128)(2,1)S(1)}, u32[]{:S(2)}, u32[]{:S(2)}) collective-permute-start(bf16[1024,128]{1,0:T(8,128)(2,1)S(1)} %get-tuple-element.68), channel_id=1, source_target_pairs={{0,3},{1,2},{2,1},{3,0},{4,7},{5,6},{6,5},{7,4},{8,11},{9,10},{10,... | collective-permute-start | bytes 786440 | tf_op jit(solution)/shard_map/ppermute | solution.py:26
  142.0 12.9 %collective-permute-start.23 = (bf16[1024,128]{1,0:T(8,128)(2,1)S(1)}, bf16[1024,128]{1,0:T(8,128)(2,1)S(1)}, u32[]{:S(2)}, u32[]{:S(2)}) collective-permute-start(bf16[1024,128]{1,0:T(8,128)(2,1)S(1)} %get-tuple-element.69), channel_id=1, source_target_pairs={{0,2},{1,3},{2,0},{3,1},{4,6},{5,7},{6,4},{7,5},{8,10},{9,11},{10,... | collective-permute-start | bytes 786440 | tf_op jit(solution)/shard_map/ppermute | solution.py:26
